TPU v7x, 128 devices: a whole 4x4x4 slice. The times are simulated.
128 devices in a mesh: var: 16 (over x, z), samp: 8 (over y, core).
Axes of the slice: x: 4, y: 4, z: 4, core: 2. Of those that a mesh axis runs over, the one named last changes fastest.
Arguments:
- data: bfloat16 [2048, 32768], P('samp', 'var'), may hold values from -6 to 6
- omega: float32 [256, 8, 128, 128], P('var'), may hold values from -1.2 to 3, as said below
- pattern: int32 [256, 8], P('var'), may hold values from 0 to 255, as said below
- counts: int32 [256], P('var'), may hold values from 2 to 8, as said below
Outputs:
- omega_next: float32 [256, 8, 128, 128], P('var', None, 'samp')
Inputs may be any that keep to these rules, and one draw needn't show every extreme that they name: pattern[r, 0] = r; the live slots of a row name distinct blocks, each owned by the same index of var as r, by a neighbouring one, or a hub block (a block whose row has all 8 slots live); dead slots also name such blocks. `counts`: exactly 2 block rows of each index of var, the hub blocks, have all 8 slots live; the others from 2 to 4. `omega`: diagonal entries of slot 0 lie in 1 to 3; tiles of dead slots hold values that are not part of Omega.
All inputs are finite; a program needn't handle non-finite values.
Results may differ from a plain program's by a relative error of at most 0.00045.
Values may be sent and summed in bfloat16 or wider, within the bound.
No kernel may reach another device: no remote copies, remote signals or barrier semaphores. Data moves between devices by JAX's collectives and lax.ppermute only.
A program may use at most 192 MiB of HBM per device.

v0:
```python
import jax
import jax.numpy as jnp
from jax import lax
from jax.experimental import pallas as pl
from jax.experimental.pallas import tpu as pltpu
from jax.sharding import PartitionSpec as P


HUB_DEV = 2
ITERS = 2
STEP_SIZE = 0.25
PENALTY = 1.0
HALF = 4
GROUP = 4
SIDE = 4
CORES = 2
LEVELS = 32000.0
TINY = 1e-30
BF = jnp.bfloat16
F32 = jnp.float32
WIRE = jnp.int16
ANY = pl.BlockSpec(memory_space=pl.ANY)
SMEM = pl.BlockSpec(memory_space=pltpu.SMEM)
VMEM = pl.BlockSpec(memory_space=pltpu.VMEM)


def grant(mib):
    return pltpu.CompilerParams(vmem_limit_bytes=mib << 20)


def cost(flops, moved):
    return pl.CostEstimate(flops=flops, bytes_accessed=moved, transcendentals=0)


def var_shift(dx, dz):
    return [
        (x * SIDE + z, ((x + dx) % SIDE) * SIDE + (z + dz) % SIDE)
        for x in range(SIDE)
        for z in range(SIDE)
    ]


def samp_shift(dy, dc):
    return [
        (y * CORES + c, ((y + dy) % SIDE) * CORES + (c + dc) % CORES)
        for y in range(SIDE)
        for c in range(CORES)
    ]


def row_order(counts, order, slots):
    def step(r, carry):
        hubs, others = carry
        hub = jnp.where(counts[r] == slots, 1, 0)
        order[jnp.where(hub == 1, hubs, HUB_DEV + others)] = r
        return hubs + hub, others + 1 - hub

    lax.fori_loop(0, order.shape[0], step, (jnp.int32(0), jnp.int32(0)))


def slot_base(p, slots):
    return p * slots if p < HUB_DEV else HUB_DEV * slots + (p - HUB_DEV) * HALF


def aligned(index, size):
    return pl.ds(pl.multiple_of(index * size, size), size)


def turned(data, row, bs):
    shape = (bs, bs)
    eye = lax.broadcasted_iota(jnp.int32, shape, 0) == lax.broadcasted_iota(jnp.int32, shape, 1)
    block = data[:, aligned(row, bs)]
    return lax.dot_general(
        eye.astype(F32).astype(BF), block, (((1,), (1,)), ((), ())), preferred_element_type=F32
    ).astype(BF)


def pack_hub_kernel(slots, bs, counts, data, out, order):
    row_order(counts, order, slots)
    first = lax.axis_index("var") * order.shape[0]
    for p in range(HUB_DEV):
        out[p * bs : (p + 1) * bs, :] = turned(data, order[p], bs)
    tail = out.shape[0] - HUB_DEV * bs
    lead = lax.broadcasted_iota(jnp.int32, (tail, out.shape[1]), 0) == 0
    ids = jnp.where(lead, first + order[0], first + order[1])
    out[HUB_DEV * bs :, :] = ids.astype(F32).astype(BF)


def pack_plain_kernel(slots, bs, counts, data, _, out, order):
    row_order(counts, order, slots)
    for p in range(out.shape[0]):
        out[p] = turned(data, order[HUB_DEV + p], bs)


def pack_hub(data, counts, slots, bs):
    return pl.pallas_call(
        lambda *refs: pack_hub_kernel(slots, bs, *refs),
        out_shape=jax.ShapeDtypeStruct((HUB_DEV * bs + 16, data.shape[0]), BF),
        in_specs=[SMEM, VMEM],
        out_specs=VMEM,
        scratch_shapes=[pltpu.SMEM(counts.shape, jnp.int32)],
        compiler_params=grant(8),
        cost_estimate=cost(1 << 20, 1 << 20),
        name="pack_hub",
    )(counts, data)


def pack_plain(data, counts, slots, bs, after):
    return pl.pallas_call(
        lambda *refs: pack_plain_kernel(slots, bs, *refs),
        out_shape=jax.ShapeDtypeStruct((counts.shape[0] - HUB_DEV, bs, data.shape[0]), BF),
        in_specs=[SMEM, VMEM, ANY],
        out_specs=VMEM,
        scratch_shapes=[pltpu.SMEM(counts.shape, jnp.int32)],
        compiler_params=grant(8),
        cost_estimate=cost(1 << 20, 1 << 20),
        name="pack_plain",
    )(counts, data, after)


class Gather:
    def __init__(self, near, hubs, table, sem, bs):
        below, below_edge, own, above, above_edge = near
        plain = own.shape[0]
        size = plain * bs
        z = lax.axis_index("var") % SIDE

        def copy(ref, at):
            return pltpu.make_async_copy(ref.reshape(size, ref.shape[2]), table.at[pl.ds(at, size), :], sem)

        self.choices = [
            (z == 0, copy(below, 0), copy(below_edge, 0)),
            (z == SIDE - 1, copy(above, 2 * size), copy(above_edge, 2 * size)),
        ]
        self.copies = [copy(own, size)]
        at = 3 * size
        for ref in hubs:
            for i in range(ref.shape[0]):
                self.copies.append(
                    pltpu.make_async_copy(
                        ref.at[i, pl.ds(0, HUB_DEV * bs), :],
                        table.at[pl.ds(at, HUB_DEV * bs), :],
                        sem,
                    )
                )
                at += HUB_DEV * bs

    def start(self):
        for copy in self.copies:
            copy.start()
        for edge, usual, other in self.choices:
            pl.when(edge)(other.start)
            pl.when(jnp.logical_not(edge))(usual.start)

    def wait(self):
        for copy in self.copies:
            copy.wait()
        for _, usual, _ in self.choices:
            usual.wait()


def fill_lookup(pattern, ids, order, inverse, lookup):
    rows, slots = pattern.shape
    plain = rows - HUB_DEV
    base = lax.axis_index("var") * rows

    def clear(i, _):
        inverse[base + i] = -1
        return 0

    lax.fori_loop(0, 3 * rows, clear, 0)

    def mark(q, _):
        inverse[ids[q] + rows] = 3 * plain + q
        return 0

    lax.fori_loop(0, ids.shape[0], mark, 0)
    for side in range(3):

        def place(i, found):
            at = base + side * rows + i
            seen = inverse[at]
            inverse[at] = jnp.where(seen < 0, side * plain + found, seen)
            return found + jnp.where(seen < 0, 1, 0)

        lax.fori_loop(0, rows, place, jnp.int32(0))
    total = 3 * plain + ids.shape[0]
    for p in range(rows):
        for k in range(slots if p < HUB_DEV else HALF):
            c = inverse[pattern[order[p], k] + rows]
            lookup[slot_base(p, slots) + k] = jnp.clip(c, 0, total - 1)


def image_group(tile_of, blocks_of, live, bs):
    high, low, blocks = [], [], []
    for k in range(GROUP):
        tile = tile_of(k)
        if live is not None:
            tile = jnp.where(k < live, tile, 0.0)
        top = tile.astype(BF)
        high.append(top)
        low.append((tile - top.astype(F32)).astype(BF))
        blocks.append(blocks_of(k))
    left = jnp.concatenate([jnp.concatenate(high, axis=1), jnp.concatenate(low, axis=1)], axis=0)
    both = jnp.dot(left, jnp.concatenate(blocks, axis=0), preferred_element_type=F32)
    return both[:bs] + both[bs:]


def hub_images(tile_of, lookup, table, out, slots, bs):
    for p in range(HUB_DEV):
        total = None
        for start in range(p * slots, (p + 1) * slots, GROUP):
            part = image_group(
                lambda k: tile_of(start + k),
                lambda k: table[aligned(lookup[start + k], bs), :],
                None,
                bs,
            )
            total = part if total is None else total + part
        out[p * bs : (p + 1) * bs, :] = total.astype(BF)


def plain_images(counts, order, ready, tile_of, lookup, table, out, slots, bs):
    def one(p, _):
        ready(p)
        start = HUB_DEV * slots + p * HALF
        image = image_group(
            lambda k: tile_of(p * HALF + k),
            lambda k: table[aligned(lookup[start + k], bs), :],
            counts[order[HUB_DEV + p]],
            bs,
        )
        out[p] = image.astype(BF)
        return 0

    lax.fori_loop(0, out.shape[0], one, 0, unroll=2)


def first_hub_kernel(*refs):
    counts, pattern, ids, omega = refs[:4]
    near, hubs = refs[4:9], refs[9:13]
    out, lookup, table, rows_out = refs[13:17]
    order, inverse, tiles, table_sem, tile_sem = refs[17:]
    rows, slots = pattern.shape
    bs, share = tiles.shape[1], rows_out.shape[1]
    row_order(counts, order, slots)
    gather = Gather(near, hubs, table, table_sem, bs)
    gather.start()
    part = aligned(lax.axis_index("samp"), share)
    moves = []
    for p in range(rows):
        n = slots if p < HUB_DEV else HALF
        at = pl.ds(slot_base(p, slots), n)
        moves.append(
            pltpu.make_async_copy(omega.at[order[p], pl.ds(0, n), part], rows_out.at[at], tile_sem)
        )
        if p < HUB_DEV:
            moves.append(pltpu.make_async_copy(omega.at[order[p]], tiles.at[at], tile_sem))
    for move in moves:
        move.start()
    fill_lookup(pattern, ids, order, inverse, lookup)
    for move in moves:
        move.wait()
    gather.wait()
    hub_images(lambda s: tiles[s], lookup, table, out, slots, bs)


def first_hub(counts, pattern, ids, omega, near, hubs, part_count):
    rows, slots, bs, _ = omega.shape
    total = HUB_DEV * slots + (rows - HUB_DEV) * HALF
    local = hubs[0].shape[2]
    table = (3 * (rows - HUB_DEV) + SIDE * SIDE * HUB_DEV) * bs
    return pl.pallas_call(
        first_hub_kernel,
        out_shape=(
            jax.ShapeDtypeStruct((HUB_DEV * bs, local), BF),
            jax.ShapeDtypeStruct((total,), jnp.int32),
            jax.ShapeDtypeStruct((table, local), BF),
            jax.ShapeDtypeStruct((total, bs // part_count, bs), F32),
        ),
        in_specs=[SMEM, SMEM, SMEM] + [ANY] * 10,
        out_specs=(VMEM, SMEM, VMEM, VMEM),
        scratch_shapes=[
            pltpu.SMEM((rows,), jnp.int32),
            pltpu.SMEM((rows * (SIDE * SIDE + 2),), jnp.int32),
            pltpu.VMEM((HUB_DEV * slots, bs, bs), F32),
            pltpu.SemaphoreType.DMA,
            pltpu.SemaphoreType.DMA,
        ],
        compiler_params=grant(16),
        cost_estimate=cost(1 << 28, 12 << 20),
        name="hub_first",
    )(counts, pattern, ids, omega, *near, *hubs)


def first_plain_kernel(slots, *refs):
    counts, lookup, omega, table, _, out = refs[:6]
    order, tiles, sems = refs[6:]
    bs = tiles.shape[1]
    row_order(counts, order, slots)

    def move(p):
        return pltpu.make_async_copy(
            omega.at[order[HUB_DEV + p], pl.ds(0, HALF)], tiles.at[pl.ds(p * HALF, HALF)], sems.at[p]
        )

    for p in range(out.shape[0]):
        move(p).start()
    plain_images(
        counts, order, lambda p: move(p).wait(), lambda s: tiles[s], lookup, table, out, slots, bs
    )


def first_plain(counts, lookup, omega, table, after):
    rows, slots, bs, _ = omega.shape
    plain = rows - HUB_DEV
    return pl.pallas_call(
        lambda *refs: first_plain_kernel(slots, *refs),
        out_shape=jax.ShapeDtypeStruct((plain, bs, table.shape[1]), BF),
        in_specs=[SMEM, SMEM, ANY, VMEM, ANY],
        out_specs=VMEM,
        scratch_shapes=[
            pltpu.SMEM((rows,), jnp.int32),
            pltpu.VMEM((plain * HALF, bs, bs), F32),
            pltpu.SemaphoreType.DMA((plain,)),
        ],
        compiler_params=grant(16),
        cost_estimate=cost(1 << 29, 10 << 20),
        name="plain_first",
    )(counts, lookup, omega, table, after)


def wire_scales(tail, scales):
    exponent = tail.astype(jnp.int32).astype(F32).reshape(scales.shape)
    scales[...] = jnp.exp2(exponent) * (1.0 / LEVELS)


def to_wire(read, out, scales, total):
    scales[...] = jnp.ones_like(scales)

    def peak(s, _):
        scales[pl.ds(s, 1), :] = jnp.max(jnp.abs(read(s)), axis=0, keepdims=True)
        return 0

    lax.fori_loop(0, total, peak, 0, unroll=8)
    exponent = jnp.ceil(jnp.log2(jnp.maximum(scales[...], TINY)))
    tail = exponent.reshape(-1, *out.shape[1:])
    out[total:] = tail.astype(jnp.int32).astype(WIRE)
    scales[...] = jnp.exp2(-exponent) * LEVELS

    def put(s, _):
        out[s] = jnp.round(read(s) * scales[pl.ds(s, 1), :]).astype(jnp.int32).astype(WIRE)
        return 0

    lax.fori_loop(0, total, put, 0, unroll=8)


def wire_shape(total, share, bs):
    return (total + -(-total // share), share, bs)


def later_kernel(slots, hub, *refs):
    counts, lookup, mine, partner, table, _, out = refs[:7]
    order, levels, tails, scales, sem = refs[7:]
    total, bs = lookup.shape[0], levels.shape[1]
    share = mine.shape[2]
    first = 0 if hub else HUB_DEV * slots
    row_order(counts, order, slots)
    part = lax.axis_index("samp")
    moves = []
    for j in range(SIDE):
        for ref, core in ((mine, part % CORES), (partner, (part + 1) % CORES)):
            at = ((part // CORES + j) % SIDE) * CORES + core
            moves.append(
                pltpu.make_async_copy(
                    ref.at[j, pl.ds(first, levels.shape[0])],
                    levels.at[:, aligned(at, share), :],
                    sem,
                )
            )
            moves.append(
                pltpu.make_async_copy(
                    ref.at[j, pl.ds(total, mine.shape[1] - total)], tails.at[at], sem
                )
            )
    for move in moves:
        move.start()
    for move in moves:
        move.wait()
    for g in range(SIDE * CORES):
        wire_scales(tails[g], scales.at[g])

    def tile_of(s):
        rows = [
            levels[s, g * share : (g + 1) * share, :].astype(jnp.int32).astype(F32)
            * scales[g, pl.ds(first + s, 1), :]
            for g in range(SIDE * CORES)
        ]
        return jnp.concatenate(rows, axis=0)

    if hub:
        hub_images(tile_of, lookup, table, out, slots, bs)
    else:
        plain_images(
            counts, order, lambda p: None, tile_of, lookup, table, out, slots, bs
        )


def later_image(counts, lookup, mine, partner, table, slots, after):
    total = lookup.shape[0]
    plain = counts.shape[0] - HUB_DEV
    _, long, share, bs = mine.shape
    local = table.shape[1]
    groups = SIDE * CORES
    hub = after is None
    count = HUB_DEV * slots if hub else plain * HALF
    return pl.pallas_call(
        lambda *refs: later_kernel(slots, hub, *refs),
        out_shape=jax.ShapeDtypeStruct(
            (HUB_DEV * bs, local) if hub else (plain, bs, local), BF
        ),
        in_specs=[SMEM, SMEM, ANY, ANY, VMEM, ANY],
        out_specs=VMEM,
        scratch_shapes=[
            pltpu.SMEM(counts.shape, jnp.int32),
            pltpu.VMEM((count, bs, bs), WIRE),
            pltpu.VMEM((groups, long - total, share, bs), WIRE),
            pltpu.VMEM((groups, (long - total) * share, bs), F32),
            pltpu.SemaphoreType.DMA,
        ],
        compiler_params=grant(16),
        cost_estimate=cost(1 << 28 if hub else 1 << 29, (2 if hub else 8) << 20),
        name="hub_later" if hub else "plain_later",
    )(counts, lookup, mine, partner, table, counts if hub else after)


def gradient_kernel(scale, slots, *refs):
    lookup, x_table = refs[:2]
    near, hubs = refs[2:7], refs[7:11]
    keep, send, m_table, sem = refs[11:]
    plain, bs, _ = near[0].shape
    gather = Gather(near, hubs, m_table, sem, bs)
    gather.start()
    gather.wait()
    part = lax.axis_index("samp")
    y, core = part // CORES, part % CORES
    share = keep.shape[2]

    def group(start, own):
        mine = aligned(own, bs)
        left = jnp.concatenate([m_table[mine, :], x_table[mine, :]], axis=1)
        right = []
        for k in range(GROUP):
            at = aligned(lookup[start + k], bs)
            right.append(jnp.concatenate([x_table[at, :], m_table[at, :]], axis=1))
        both = lax.dot_general(
            left,
            jnp.concatenate(right, axis=0),
            (((1,), (1,)), ((), ())),
            preferred_element_type=F32,
        )
        both = both * scale
        for k in range(GROUP):
            tile = both[:, k * bs : (k + 1) * bs].reshape(SIDE, CORES, share, bs)
            even, odd = tile[:, 0], tile[:, 1]
            stay = jnp.where(core == 0, even, odd)
            leave = jnp.where(core == 0, odd, even)
            for g in range(SIDE):
                to = (g + SIDE - y) % SIDE
                keep[to, start + k] = stay[g]
                send[to, start + k] = leave[g]

    for p in range(HUB_DEV):
        for start in range(p * slots, (p + 1) * slots, GROUP):
            group(start, 3 * plain + p)

    def step(p, _):
        group(HUB_DEV * slots + p * HALF, plain + p)
        return 0

    lax.fori_loop(0, plain, step, 0, unroll=2)


def gradient(lookup, table, near, hubs, scale, slots, part_count):
    total = lookup.shape[0]
    bs = near[0].shape[1]
    shape = jax.ShapeDtypeStruct((SIDE, total, bs // part_count, bs), F32)
    return pl.pallas_call(
        lambda *refs: gradient_kernel(scale, slots, *refs),
        out_shape=(shape, shape),
        in_specs=[SMEM, VMEM] + [ANY] * 9,
        out_specs=(VMEM, VMEM),
        scratch_shapes=[pltpu.VMEM(table.shape, BF), pltpu.SemaphoreType.DMA],
        compiler_params=grant(24),
        cost_estimate=cost(1 << 30, 16 << 20),
        name="gradient",
    )(lookup, table, *near, *hubs)


def add_kernel(keep, other, own, *refs):
    sends, total_sum, scales = refs[:-2], refs[-2], refs[-1]
    total = own.shape[0]
    own[...] = keep[0] + other[0]
    for j, ref in enumerate(sends):
        total_sum[...] = keep[j + 1] + other[j + 1]
        to_wire(lambda s: total_sum[s], ref, scales, total)


def add_cores(keep, other):
    side, total, share, bs = keep.shape
    wire = jax.ShapeDtypeStruct(wire_shape(total, share, bs), WIRE)
    return pl.pallas_call(
        add_kernel,
        out_shape=(jax.ShapeDtypeStruct((total, share, bs), F32),) + (wire,) * (side - 1),
        in_specs=[VMEM, VMEM],
        out_specs=(VMEM,) * side,
        scratch_shapes=[
            pltpu.VMEM((total, share, bs), F32),
            pltpu.VMEM(((wire.shape[0] - total) * share, bs), F32),
        ],
        compiler_params=grant(16),
        name="add_cores",
    )(keep, other)


def new_tile(tile, slope, leading, live, part, share):
    stepped = tile - STEP_SIZE * slope
    edge = STEP_SIZE * PENALTY
    shrunk = stepped - jnp.minimum(jnp.maximum(stepped, -edge), edge)
    if leading:
        shape = stepped.shape
        row = part * share + lax.broadcasted_iota(jnp.int32, shape, 0)
        col = lax.broadcasted_iota(jnp.int32, shape, 1)
        barrier = 0.5 * (stepped + jnp.sqrt(stepped * stepped + 4.0 * STEP_SIZE))
        shrunk = jnp.where(row == col, barrier, shrunk)
    return jnp.where(live, shrunk, 0.0)


def prox_kernel(last, slots, counts, tiles, own, *refs):
    sends = refs[: SIDE - 1]
    outs = refs[SIDE - 1 : -2]
    order, scales = refs[-2:]
    rows = order.shape[0]
    row_order(counts, order, slots)
    part = lax.axis_index("samp")
    total, share, bs = own.shape
    for j, ref in enumerate(sends):
        wire_scales(ref[total:], scales.at[j])

    def slot(row, s, k, n):
        slope = own[s]
        for j, ref in enumerate(sends):
            slope = slope + ref[s].astype(jnp.int32).astype(F32) * scales[j, pl.ds(s, 1), :]
        value = new_tile(tiles[s], slope, k == 0, k < n, part, share)
        if last:
            outs[0][row, k] = value
        else:
            outs[0][s] = value

    for p in range(HUB_DEV):
        for k in range(slots):
            slot(order[p], p * slots + k, k, slots)

    def plain(p, _):
        row = order[HUB_DEV + p]
        n = counts[row]
        for k in range(HALF):
            slot(row, HUB_DEV * slots + p * HALF + k, k, n)
        if last:
            for k in range(HALF, slots):
                outs[0][row, k] = jnp.zeros((share, bs), F32)
        return 0

    lax.fori_loop(0, rows - HUB_DEV, plain, 0, unroll=2)
    if not last:
        to_wire(lambda s: outs[0][s], outs[1], scales.at[0], total)


def prox(counts, tiles, terms, slots, last):
    rows = counts.shape[0]
    total, share, bs = tiles.shape
    wire = wire_shape(total, share, bs)
    if last:
        outs = (jax.ShapeDtypeStruct((rows, slots, share, bs), F32),)
    else:
        outs = (jax.ShapeDtypeStruct((total, share, bs), F32), jax.ShapeDtypeStruct(wire, WIRE))
    return pl.pallas_call(
        lambda *refs: prox_kernel(last, slots, *refs),
        out_shape=outs,
        in_specs=[SMEM] + [VMEM] * 5,
        out_specs=(VMEM,) * len(outs),
        scratch_shapes=[
            pltpu.SMEM((rows,), jnp.int32),
            pltpu.VMEM((SIDE - 1, (wire[0] - total) * share, bs), F32),
        ],
        compiler_params=grant(16),
        name="prox_last" if last else "prox",
    )(counts, tiles, *terms)


def share_near(value):
    size = lax.axis_size("var")
    up = [(i, i + 1) for i in range(size - 1)]
    moves = []
    for pairs in (up, [(j, i) for i, j in up]):
        inner = [(i, j) for i, j in pairs if i // SIDE == j // SIDE]
        edge = [(i, j) for i, j in pairs if i // SIDE != j // SIDE]
        crossing = lax.ppermute(value, "var", edge)
        moves.append((crossing, lax.ppermute(value, "var", inner)))
    (below_edge, below), (above_edge, above) = moves
    return below, below_edge, value, above, above_edge


def share_hubs(value):
    by_z = [value] + [lax.ppermute(value, "var", var_shift(0, d)) for d in (1, -1, 2)]
    column = jnp.stack(by_z)
    return [column] + [lax.ppermute(column, "var", var_shift(d, 0)) for d in (1, -1, 2)]


def per_device(data, omega, pattern, counts):
    parts = lax.axis_size("samp")
    _, slots, bs, _ = omega.shape
    scale = 0.5 / (data.shape[0] * parts)
    x_hub = pack_hub(data, counts, slots, bs)
    x_hubs = share_hubs(x_hub)
    x_own = pack_plain(data, counts, slots, bs, x_hub)
    x_near = share_near(x_own)
    ids = jnp.stack([g[:, HUB_DEV * bs : HUB_DEV * bs + HUB_DEV, 0] for g in x_hubs])
    ids = ids.reshape(-1).astype(jnp.int32)
    for iteration in range(ITERS):
        if iteration == 0:
            m_hub, lookup, table, tiles = first_hub(
                counts, pattern, ids, omega, x_near, x_hubs, parts
            )
        else:
            mine = jnp.stack(
                [
                    sent,
                    lax.ppermute(sent, "samp", samp_shift(-1, 0)),
                    lax.ppermute(sent, "samp", samp_shift(2, 0)),
                    lax.ppermute(sent, "samp", samp_shift(1, 0)),
                ]
            )
            partner = lax.ppermute(mine, "samp", samp_shift(0, 1))
            m_hub = later_image(counts, lookup, mine, partner, table, slots, None)
        m_hubs = share_hubs(m_hub)
        if iteration == 0:
            m_own = first_plain(counts, lookup, omega, table, m_hub)
        else:
            m_own = later_image(counts, lookup, mine, partner, table, slots, m_hub)
        m_near = share_near(m_own)
        keep, leave = gradient(lookup, table, m_near, m_hubs, scale, slots, parts)
        other = lax.ppermute(leave, "samp", samp_shift(0, 1))
        own, up, across, down = add_cores(keep, other)
        terms = (
            own,
            lax.ppermute(up, "samp", samp_shift(1, 0)),
            lax.ppermute(across, "samp", samp_shift(2, 0)),
            lax.ppermute(down, "samp", samp_shift(-1, 0)),
        )
        if iteration < ITERS - 1:
            tiles, sent = prox(counts, tiles, terms, slots, False)
        else:
            (tiles,) = prox(counts, tiles, terms, slots, True)
    return tiles


def solution(mesh):
    placed = (P("samp", "var"), P("var", None, None, None), P("var", None), P("var"))
    return jax.shard_map(
        per_device,
        mesh=mesh,
        in_specs=placed,
        out_specs=P("var", None, "samp", None),
        check_vma=False,
    )
```

profile of v0, /device:TPU:98, one launch (start us, length us, event | category | flops | bytes accessed | tf_op | source)
XLA Modules:
  0.0 277.2 jit_solution(8565922877998105920)
XLA Ops:
  0.0 1.2 copy-done.2
  3.5 3.2 %collective-permute-start = (bf16[272,256]{1,0:T(8,128)(2,1)S(1)}, bf16[272,256]{1,0:T(8,128)(2,1)S(1)}, u32[]{:S(2)}, u32[]{:S(2)}) collective-permute-start(bf16[272,256]{1,0:T(8,128)(2,1)S(1)} %pack_hub.1.refs_2_), channel_id=1, source_target_pairs={{0,8},{8,16},{16,24},{24,0},{32,40},{40,48},{48,56},{56,32},{64,72... | collective-permute-start | bytes 417800 | tf_op jit(solution)/shard_map/ppermute | solution.py:615
  6.7 4.3 %collective-permute-done.2 = bf16[272,256]{1,0:T(8,128)(2,1)S(1)} collective-permute-done((bf16[272,256]{1,0:T(8,128)(2,1)S(1)}, bf16[272,256]{1,0:T(8,128)(2,1)S(1)}, u32[]{:S(2)}, u32[]{:S(2)}) %collective-permute-start.2) | collective-permute-done | bytes 139296 | tf_op jit(solution)/shard_map/ppermute | solution.py:615
  10.9 1.8 collective-permute-done.1
  12.9 2.2 collective-permute-start.5
  15.1 1.4 collective-permute-start.4
  16.5 1.2 pack_plain.1.refs_6_
  17.7 1.3 collective-permute-start.9
  19.0 1.8 collective-permute-start.8
  20.8 7.1 %collective-permute-start.7 = (bf16[14,128,256]{2,1,0:T(8,128)(2,1)S(1)}, bf16[14,128,256]{2,1,0:T(8,128)(2,1)}, u32[]{:S(2)}, u32[]{:S(2)}) collective-permute-start(bf16[14,128,256]{2,1,0:T(8,128)(2,1)S(1)} %pack_plain.1.refs_6_), channel_id=1, source_target_pairs={{24,32},{56,64},{88,96},{25,33},{57,65},{89,97},{26,34},{58,66},{9... | collective-permute-start | bytes 2752520 | tf_op jit(solution)/shard_map/ppermute | solution.py:608
  27.9 2.2 collective-permute-done.5.refs_12_
  30.1 1.3 collective-permute-start.6
  31.4 9.6 %collective-permute-done.4.refs_11_ = bf16[4,272,256]{2,1,0:T(8,128)(2,1)} collective-permute-done((bf16[4,272,256]{2,1,0:T(8,128)(2,1)S(1)}, bf16[4,272,256]{2,1,0:T(8,128)(2,1)}, u32[]{:S(2)}, u32[]{:S(2)}) %collective-permute-start.4) | collective-permute-done | bytes 557088 | tf_op jit(solution)/shard_map/ppermute | solution.py:617
  43.5 17.2 %collective-permute-done.3.refs_10_ = bf16[4,272,256]{2,1,0:T(8,128)(2,1)} collective-permute-done((bf16[4,272,256]{2,1,0:T(8,128)(2,1)S(1)}, bf16[4,272,256]{2,1,0:T(8,128)(2,1)}, u32[]{:S(2)}, u32[]{:S(2)}) %collective-permute-start.3) | collective-permute-done | bytes 557088 | tf_op jit(solution)/shard_map/ppermute | solution.py:617
  61.8 3.4 %copy-done = f32[16,8,128,128]{3,2,1,0:T(8,128)S(1)} copy-done((f32[16,8,128,128]{3,2,1,0:T(8,128)S(1)}, f32[16,8,128,128]{3,2,1,0:T(8,128)}, u32[]{:S(2)}) %copy-start) | copy-done | bytes 8388632
  65.2 4.8 %hub_first.1 = (bf16[256,256]{1,0:T(8,128)(2,1)S(1)}, s32[72]{0:T(128)S(1)}, bf16[9472,256]{1,0:T(8,128)(2,1)S(1)}, f32[72,16,128]{2,1,0:T(8,128)S(1)}) custom-call(s32[16]{0:T(128)S(1)} %copy-done.5, s32[16,8]{1,0:T(8,128)S(1)} %copy.26.refs_1_, s32[32]{0:T(128)S(1)} %reshape.3.refs_2_, f32[16,8,128,128]{3,2,1,0:T(8,128)S(1)} %copy-done, ...), custom_call_target="tpu_custom_call" | custom-call | flops 268435456 | bytes 12582912 | tf_op jit(solution)/shard_map/hub_first/pallas_call | solution.py:273
  70.2 3.2 %collective-permute-start.14 = (bf16[256,256]{1,0:T(8,128)(2,1)S(1)}, bf16[256,256]{1,0:T(8,128)(2,1)S(1)}, u32[]{:S(2)}, u32[]{:S(2)}) collective-permute-start(bf16[256,256]{1,0:T(8,128)(2,1)S(1)} %get-tuple-element.26.refs_4_), channel_id=1, source_target_pairs={{0,8},{8,16},{16,24},{24,0},{32,40},{40,48},{48,56},{56,32},{64,72... | collective-permute-start | bytes 393224 | tf_op jit(solution)/shard_map/ppermute | solution.py:615
  73.4 4.2 %collective-permute-done.16 = bf16[256,256]{1,0:T(8,128)(2,1)S(1)} collective-permute-done((bf16[256,256]{1,0:T(8,128)(2,1)S(1)}, bf16[256,256]{1,0:T(8,128)(2,1)S(1)}, u32[]{:S(2)}, u32[]{:S(2)}) %collective-permute-start.16) | collective-permute-done | bytes 131104 | tf_op jit(solution)/shard_map/ppermute | solution.py:615
  77.6 1.1 collective-permute-done.15
  78.9 4.0 %collective-permute-start.18 = (bf16[4,256,256]{2,1,0:T(8,128)(2,1)S(1)}, bf16[4,256,256]{2,1,0:T(8,128)(2,1)S(1)}, u32[]{:S(2)}, u32[]{:S(2)}) collective-permute-start(bf16[4,256,256]{2,1,0:T(8,128)(2,1)S(1)} %pad_maximum_fusion.1.refs_7_), channel_id=1, source_target_pairs={{0,96},{8,104},{16,112},{24,120},{32,0},{40,8},{48,16},{56,24},{64... | collective-permute-start | bytes 1572872 | tf_op jit(solution)/shard_map/ppermute | solution.py:617
  82.9 5.2 %plain_first.1.refs_4_ = bf16[14,128,256]{2,1,0:T(8,128)(2,1)S(1)} custom-call(s32[16]{0:T(128)S(1)} %copy-done.5, s32[72]{0:T(128)S(1)} %get-tuple-element.24.refs_1_.refs_0_, f32[16,8,128,128]{3,2,1,0:T(8,128)S(1)} %copy-done.1, bf16[9472,256]{1,0:T(8,128)(2,1)S(1)} %get-tuple-element.25.refs_3_.refs_1_.refs_4_, bf16[256,256]{1,0:T(8,128)(2,1)S(1)} %get-tuple-element.26.refs_4_), custom_call_target="tpu_custom_call" | custom-call | flops 536870912 | bytes 10485760 | tf_op jit(solution)/shard_map/plain_first/pallas_call | solution.py:317
  88.1 1.3 collective-permute-start.13
  89.4 1.3 collective-permute-start.12
  90.8 6.7 %collective-permute-start.11 = (bf16[14,128,256]{2,1,0:T(8,128)(2,1)S(1)}, bf16[14,128,256]{2,1,0:T(8,128)(2,1)S(1)}, u32[]{:S(2)}, u32[]{:S(2)}) collective-permute-start(bf16[14,128,256]{2,1,0:T(8,128)(2,1)S(1)} %plain_first.1.refs_4_), channel_id=1, source_target_pairs={{24,32},{56,64},{88,96},{25,33},{57,65},{89,97},{26,34},{58,66},{9... | collective-permute-start | bytes 2752520 | tf_op jit(solution)/shard_map/ppermute | solution.py:608
  97.5 1.3 collective-permute-start.10
  98.8 5.2 %collective-permute-done.18.refs_9_ = bf16[4,256,256]{2,1,0:T(8,128)(2,1)S(1)} collective-permute-done((bf16[4,256,256]{2,1,0:T(8,128)(2,1)S(1)}, bf16[4,256,256]{2,1,0:T(8,128)(2,1)S(1)}, u32[]{:S(2)}, u32[]{:S(2)}) %collective-permute-start.18) | collective-permute-done | bytes 524320 | tf_op jit(solution)/shard_map/ppermute | solution.py:617
  104.0 1.7 collective-permute-start.17
  105.7 22.7 %collective-permute-done.17.refs_8_ = bf16[4,256,256]{2,1,0:T(8,128)(2,1)S(1)} collective-permute-done((bf16[4,256,256]{2,1,0:T(8,128)(2,1)S(1)}, bf16[4,256,256]{2,1,0:T(8,128)(2,1)S(1)}, u32[]{:S(2)}, u32[]{:S(2)}) %collective-permute-start.17) | collective-permute-done | bytes 524320 | tf_op jit(solution)/shard_map/ppermute | solution.py:617
  128.4 8.2 %gradient.2 = (f32[4,72,16,128]{3,2,1,0:T(8,128)S(1)}, f32[4,72,16,128]{3,2,1,0:T(8,128)S(1)}) custom-call(s32[72]{0:T(128)S(1)} %get-tuple-element.24.refs_1_.refs_0_, bf16[9472,256]{1,0:T(8,128)(2,1)S(1)} %get-tuple-element.25.refs_3_.refs_1_.refs_4_, bf16[14,128,256]{2,1,0:T(8,128)(2,1)S(1)} %collective-permute-done.10.refs_2_, ...), custom_call_target="tpu_custom_call" | custom-call | flops 1073741824 | bytes 16777216 | tf_op jit(solution)/shard_map/gradient/pallas_call | solution.py:488
  136.8 4.5 %collective-permute-done.20.other = f32[4,72,16,128]{3,2,1,0:T(8,128)S(1)} collective-permute-done((f32[4,72,16,128]{3,2,1,0:T(8,128)S(1)}, f32[4,72,16,128]{3,2,1,0:T(8,128)S(1)}, u32[]{:S(2)}, u32[]{:S(2)}) %collective-permute-start.20) | collective-permute-done | bytes 2359328 | tf_op jit(solution)/shard_map/ppermute | solution.py:653
  141.3 1.0 add_cores.2
  142.3 1.6 collective-permute-start.21
  144.0 2.9 %collective-permute-start.22 = (s16[77,16,128]{2,1,0:T(8,128)(2,1)S(1)}, s16[77,16,128]{2,1,0:T(8,128)(2,1)S(1)}, u32[]{:S(2)}, u32[]{:S(2)}) collective-permute-start(s16[77,16,128]{2,1,0:T(8,128)(2,1)S(1)} %get-tuple-element.31), channel_id=1, source_target_pairs={{0,4},{1,5},{2,6},{3,7},{4,0},{5,1},{6,2},{7,3},{8,12},{9,13},{10,... | collective-permute-start | bytes 946184 | tf_op jit(solution)/shard_map/ppermute | solution.py:658
  146.9 1.3 collective-permute-start.23
  148.2 4.9 %collective-permute-done.21.refs_3_ = s16[77,16,128]{2,1,0:T(8,128)(2,1)S(1)} collective-permute-done((s16[77,16,128]{2,1,0:T(8,128)(2,1)S(1)}, s16[77,16,128]{2,1,0:T(8,128)(2,1)S(1)}, u32[]{:S(2)}, u32[]{:S(2)}) %collective-permute-start.21) | collective-permute-done | bytes 315424 | tf_op jit(solution)/shard_map/ppermute | solution.py:657
  153.2 7.9 %collective-permute-done.22.refs_4_ = s16[77,16,128]{2,1,0:T(8,128)(2,1)S(1)} collective-permute-done((s16[77,16,128]{2,1,0:T(8,128)(2,1)S(1)}, s16[77,16,128]{2,1,0:T(8,128)(2,1)S(1)}, u32[]{:S(2)}, u32[]{:S(2)}) %collective-permute-start.22) | collective-permute-done | bytes 315424 | tf_op jit(solution)/shard_map/ppermute | solution.py:658
  161.1 1.5 prox.1
  162.6 1.3 collective-permute-start.26
  163.9 2.4 collective-permute-start.25
  166.3 1.6 collective-permute-start.24
  167.9 4.6 %collective-permute-done.26 = s16[77,16,128]{2,1,0:T(8,128)(2,1)S(1)} collective-permute-done((s16[77,16,128]{2,1,0:T(8,128)(2,1)S(1)}, s16[77,16,128]{2,1,0:T(8,128)(2,1)S(1)}, u32[]{:S(2)}, u32[]{:S(2)}) %collective-permute-start.26) | collective-permute-done | bytes 315424 | tf_op jit(solution)/shard_map/ppermute | solution.py:641
  172.5 7.9 %collective-permute-done.25 = s16[77,16,128]{2,1,0:T(8,128)(2,1)S(1)} collective-permute-done((s16[77,16,128]{2,1,0:T(8,128)(2,1)S(1)}, s16[77,16,128]{2,1,0:T(8,128)(2,1)S(1)}, u32[]{:S(2)}, u32[]{:S(2)}) %collective-permute-start.25) | collective-permute-done | bytes 315424 | tf_op jit(solution)/shard_map/ppermute | solution.py:640
  180.7 3.0 %collective-permute-done.27.refs_3_ = s16[4,77,16,128]{3,2,1,0:T(8,128)(2,1)S(1)} collective-permute-done((s16[4,77,16,128]{3,2,1,0:T(8,128)(2,1)S(1)}, s16[4,77,16,128]{3,2,1,0:T(8,128)(2,1)S(1)}, u32[]{:S(2)}, u32[]{:S(2)}) %collective-permute-start.27) | collective-permute-done | bytes 1261600 | tf_op jit(solution)/shard_map/ppermute | solution.py:644
  183.7 1.5 hub_later.1.refs_5_
  185.4 3.2 %collective-permute-start.32 = (bf16[256,256]{1,0:T(8,128)(2,1)S(1)}, bf16[256,256]{1,0:T(8,128)(2,1)S(1)}, u32[]{:S(2)}, u32[]{:S(2)}) collective-permute-start(bf16[256,256]{1,0:T(8,128)(2,1)S(1)} %hub_later.1.refs_5_), channel_id=1, source_target_pairs={{0,8},{8,16},{16,24},{24,0},{32,40},{40,48},{48,56},{56,32},{64,72... | collective-permute-start | bytes 393224 | tf_op jit(solution)/shard_map/ppermute | solution.py:615
  188.6 4.6 %collective-permute-done.34 = bf16[256,256]{1,0:T(8,128)(2,1)S(1)} collective-permute-done((bf16[256,256]{1,0:T(8,128)(2,1)S(1)}, bf16[256,256]{1,0:T(8,128)(2,1)S(1)}, u32[]{:S(2)}, u32[]{:S(2)}) %collective-permute-start.34) | collective-permute-done | bytes 131104 | tf_op jit(solution)/shard_map/ppermute | solution.py:615
  193.2 1.7 collective-permute-done.33
  195.1 3.5 %collective-permute-start.36 = (bf16[4,256,256]{2,1,0:T(8,128)(2,1)S(1)}, bf16[4,256,256]{2,1,0:T(8,128)(2,1)S(1)}, u32[]{:S(2)}, u32[]{:S(2)}) collective-permute-start(bf16[4,256,256]{2,1,0:T(8,128)(2,1)S(1)} %pad_maximum_fusion.2.refs_7_), channel_id=1, source_target_pairs={{0,96},{8,104},{16,112},{24,120},{32,0},{40,8},{48,16},{56,24},{64... | collective-permute-start | bytes 1572872 | tf_op jit(solution)/shard_map/ppermute | solution.py:617
  198.6 3.4 %plain_later.1.refs_4_ = bf16[14,128,256]{2,1,0:T(8,128)(2,1)S(1)} custom-call(s32[16]{0:T(128)S(1)} %copy-done.5, s32[72]{0:T(128)S(1)} %get-tuple-element.24.refs_1_.refs_0_, s16[4,77,16,128]{3,2,1,0:T(8,128)(2,1)S(1)} %pad_add_fusion.refs_2_, s16[4,77,16,128]{3,2,1,0:T(8,128)(2,1)S(1)} %collective-permute-done.27.refs_3_, ...), custom_call_target="tpu_custom_call" | custom-call | flops 536870912 | bytes 8388608 | tf_op jit(solution)/shard_map/plain_later/pallas_call | solution.py:417
  202.0 1.3 collective-permute-start.31
  203.3 1.3 collective-permute-start.30
  204.7 6.7 %collective-permute-start.29 = (bf16[14,128,256]{2,1,0:T(8,128)(2,1)S(1)}, bf16[14,128,256]{2,1,0:T(8,128)(2,1)S(1)}, u32[]{:S(2)}, u32[]{:S(2)}) collective-permute-start(bf16[14,128,256]{2,1,0:T(8,128)(2,1)S(1)} %plain_later.1.refs_4_), channel_id=1, source_target_pairs={{24,32},{56,64},{88,96},{25,33},{57,65},{89,97},{26,34},{58,66},{9... | collective-permute-start | bytes 2752520 | tf_op jit(solution)/shard_map/ppermute | solution.py:608
  211.4 1.3 collective-permute-start.28
  212.7 7.3 %collective-permute-done.36.refs_9_ = bf16[4,256,256]{2,1,0:T(8,128)(2,1)S(1)} collective-permute-done((bf16[4,256,256]{2,1,0:T(8,128)(2,1)S(1)}, bf16[4,256,256]{2,1,0:T(8,128)(2,1)S(1)}, u32[]{:S(2)}, u32[]{:S(2)}) %collective-permute-start.36) | collective-permute-done | bytes 524320 | tf_op jit(solution)/shard_map/ppermute | solution.py:617
  220.1 2.0 collective-permute-start.35
  222.1 20.9 %collective-permute-done.35.refs_8_ = bf16[4,256,256]{2,1,0:T(8,128)(2,1)S(1)} collective-permute-done((bf16[4,256,256]{2,1,0:T(8,128)(2,1)S(1)}, bf16[4,256,256]{2,1,0:T(8,128)(2,1)S(1)}, u32[]{:S(2)}, u32[]{:S(2)}) %collective-permute-start.35) | collective-permute-done | bytes 524320 | tf_op jit(solution)/shard_map/ppermute | solution.py:617
  243.0 8.2 %gradient.3 = (f32[4,72,16,128]{3,2,1,0:T(8,128)S(1)}, f32[4,72,16,128]{3,2,1,0:T(8,128)S(1)}) custom-call(s32[72]{0:T(128)S(1)} %get-tuple-element.24.refs_1_.refs_0_, bf16[9472,256]{1,0:T(8,128)(2,1)S(1)} %get-tuple-element.25.refs_3_.refs_1_.refs_4_, bf16[14,128,256]{2,1,0:T(8,128)(2,1)S(1)} %collective-permute-done.28.refs_2_, ...), custom_call_target="tpu_custom_call" | custom-call | flops 1073741824 | bytes 16777216 | tf_op jit(solution)/shard_map/gradient/pallas_call | solution.py:488
  251.3 4.5 %collective-permute-done.38.other = f32[4,72,16,128]{3,2,1,0:T(8,128)S(1)} collective-permute-done((f32[4,72,16,128]{3,2,1,0:T(8,128)S(1)}, f32[4,72,16,128]{3,2,1,0:T(8,128)S(1)}, u32[]{:S(2)}, u32[]{:S(2)}) %collective-permute-start.38) | collective-permute-done | bytes 2359328 | tf_op jit(solution)/shard_map/ppermute | solution.py:653
  255.8 1.0 add_cores.3
  256.9 1.3 collective-permute-start.39
  258.1 2.4 collective-permute-start.40
  261.4 6.7 %collective-permute-done.39.refs_3_ = s16[77,16,128]{2,1,0:T(8,128)(2,1)S(1)} collective-permute-done((s16[77,16,128]{2,1,0:T(8,128)(2,1)S(1)}, s16[77,16,128]{2,1,0:T(8,128)(2,1)S(1)}, u32[]{:S(2)}, u32[]{:S(2)}) %collective-permute-start.39) | collective-permute-done | bytes 315424 | tf_op jit(solution)/shard_map/ppermute | solution.py:657
  268.1 6.7 %collective-permute-done.40.refs_4_ = s16[77,16,128]{2,1,0:T(8,128)(2,1)S(1)} collective-permute-done((s16[77,16,128]{2,1,0:T(8,128)(2,1)S(1)}, s16[77,16,128]{2,1,0:T(8,128)(2,1)S(1)}, u32[]{:S(2)}, u32[]{:S(2)}) %collective-permute-start.40) | collective-permute-done | bytes 315424 | tf_op jit(solution)/shard_map/ppermute | solution.py:658
  275.0 2.2 prox_last.1
  (66 shorter events, 8.1 us)
Async XLA Ops:
  0.0 1.2 copy-start.2
  1.2 0.7 copy-start.4
  1.9 14.6 %copy-start.3 = (bf16[256,2048]{1,0:T(8,128)(2,1)S(1)}, bf16[256,2048]{1,0:T(8,128)(2,1)}, u32[]{:S(2)}) copy-start(bf16[256,2048]{1,0:T(8,128)(2,1)} %refs_1_.4) | copy-start | bytes 3145732
  1.9 14.6 %copy-start.5 = (s32[16]{0:T(128)S(1)}, s32[16]{0:T(128)}, u32[]{:S(2)}) copy-start(s32[16]{0:T(128)} %refs_0_.15) | copy-start | bytes 196
  2.8 8.1 %collective-permute-start.2 = (bf16[272,256]{1,0:T(8,128)(2,1)S(1)}, bf16[272,256]{1,0:T(8,128)(2,1)S(1)}, u32[]{:S(2)}, u32[]{:S(2)}) collective-permute-start(bf16[272,256]{1,0:T(8,128)(2,1)S(1)} %pack_hub.1.refs_2_), channel_id=1, source_target_pairs={{0,16},{8,24},{16,0},{24,8},{32,48},{40,56},{48,32},{56,40},{64,80... | collective-permute-start | bytes 417800 | tf_op jit(solution)/shard_map/ppermute | solution.py:615
  3.5 9.3 %collective-permute-start.1 = (bf16[272,256]{1,0:T(8,128)(2,1)S(1)}, bf16[272,256]{1,0:T(8,128)(2,1)S(1)}, u32[]{:S(2)}, u32[]{:S(2)}) collective-permute-start(bf16[272,256]{1,0:T(8,128)(2,1)S(1)} %pack_hub.1.refs_2_), channel_id=1, source_target_pairs={{0,24},{8,0},{16,8},{24,16},{32,56},{40,32},{48,40},{56,48},{64,88... | collective-permute-start | bytes 417800 | tf_op jit(solution)/shard_map/ppermute | solution.py:615
  3.5 9.3 %collective-permute-start = (bf16[272,256]{1,0:T(8,128)(2,1)S(1)}, bf16[272,256]{1,0:T(8,128)(2,1)S(1)}, u32[]{:S(2)}, u32[]{:S(2)}) collective-permute-start(bf16[272,256]{1,0:T(8,128)(2,1)S(1)} %pack_hub.1.refs_2_), channel_id=1, source_target_pairs={{0,8},{8,16},{16,24},{24,0},{32,40},{40,48},{48,56},{56,32},{64,72... | collective-permute-start | bytes 417800 | tf_op jit(solution)/shard_map/ppermute | solution.py:615
  12.9 28.8 %copy-start.6 = (s32[16,8]{0,1:T(8,128)S(1)}, s32[16,8]{0,1:T(8,128)}, u32[]{:S(2)}) copy-start(s32[16,8]{0,1:T(8,128)} %param.6) | copy-start | bytes 1540
  12.9 17.2 %collective-permute-start.5 = (bf16[4,272,256]{2,1,0:T(8,128)(2,1)S(1)}, bf16[4,272,256]{2,1,0:T(8,128)(2,1)}, u32[]{:S(2)}, u32[]{:S(2)}) collective-permute-start(bf16[4,272,256]{2,1,0:T(8,128)(2,1)S(1)} %pad_maximum_fusion.refs_9_), channel_id=1, source_target_pairs={{0,64},{8,72},{16,80},{24,88},{32,96},{40,104},{48,112},{56,120},{... | collective-permute-start | bytes 1671176 | tf_op jit(solution)/shard_map/ppermute | solution.py:617
  15.1 25.9 %collective-permute-start.4 = (bf16[4,272,256]{2,1,0:T(8,128)(2,1)S(1)}, bf16[4,272,256]{2,1,0:T(8,128)(2,1)}, u32[]{:S(2)}, u32[]{:S(2)}) collective-permute-start(bf16[4,272,256]{2,1,0:T(8,128)(2,1)S(1)} %pad_maximum_fusion.refs_9_), channel_id=1, source_target_pairs={{0,96},{8,104},{16,112},{24,120},{32,0},{40,8},{48,16},{56,24},{64... | collective-permute-start | bytes 1671176 | tf_op jit(solution)/shard_map/ppermute | solution.py:617
  17.7 44.1 %collective-permute-start.9 = (bf16[14,128,256]{2,1,0:T(8,128)(2,1)S(1)}, bf16[14,128,256]{2,1,0:T(8,128)(2,1)S(1)}, u32[]{:S(2)}, u32[]{:S(2)}) collective-permute-start(bf16[14,128,256]{2,1,0:T(8,128)(2,1)S(1)} %pack_plain.1.refs_6_), channel_id=1, source_target_pairs={{32,24},{64,56},{96,88},{33,25},{65,57},{97,89},{34,26},{66,58},{9... | collective-permute-start | bytes 2752520 | tf_op jit(solution)/shard_map/ppermute | solution.py:608
  19.0 42.8 %collective-permute-start.8 = (bf16[14,128,256]{2,1,0:T(8,128)(2,1)S(1)}, bf16[14,128,256]{2,1,0:T(8,128)(2,1)S(1)}, u32[]{:S(2)}, u32[]{:S(2)}) collective-permute-start(bf16[14,128,256]{2,1,0:T(8,128)(2,1)S(1)} %pack_plain.1.refs_6_), channel_id=1, source_target_pairs={{8,0},{16,8},{24,16},{40,32},{48,40},{56,48},{72,64},{80,72},{88,8... | collective-permute-start | bytes 2752520 | tf_op jit(solution)/shard_map/ppermute | solution.py:609
  20.8 41.0 %collective-permute-start.7 = (bf16[14,128,256]{2,1,0:T(8,128)(2,1)S(1)}, bf16[14,128,256]{2,1,0:T(8,128)(2,1)}, u32[]{:S(2)}, u32[]{:S(2)}) collective-permute-start(bf16[14,128,256]{2,1,0:T(8,128)(2,1)S(1)} %pack_plain.1.refs_6_), channel_id=1, source_target_pairs={{24,32},{56,64},{88,96},{25,33},{57,65},{89,97},{26,34},{58,66},{9... | collective-permute-start | bytes 2752520 | tf_op jit(solution)/shard_map/ppermute | solution.py:608
  30.1 31.7 %collective-permute-start.6 = (bf16[14,128,256]{2,1,0:T(8,128)(2,1)S(1)}, bf16[14,128,256]{2,1,0:T(8,128)(2,1)}, u32[]{:S(2)}, u32[]{:S(2)}) collective-permute-start(bf16[14,128,256]{2,1,0:T(8,128)(2,1)S(1)} %pack_plain.1.refs_6_), channel_id=1, source_target_pairs={{0,8},{8,16},{16,24},{32,40},{40,48},{48,56},{64,72},{72,80},{80,8... | collective-permute-start | bytes 2752520 | tf_op jit(solution)/shard_map/ppermute | solution.py:609
  41.0 19.7 %collective-permute-start.3 = (bf16[4,272,256]{2,1,0:T(8,128)(2,1)S(1)}, bf16[4,272,256]{2,1,0:T(8,128)(2,1)}, u32[]{:S(2)}, u32[]{:S(2)}) collective-permute-start(bf16[4,272,256]{2,1,0:T(8,128)(2,1)S(1)} %pad_maximum_fusion.refs_9_), channel_id=1, source_target_pairs={{0,32},{8,40},{16,48},{24,56},{32,64},{40,72},{48,80},{56,88},{64,... | collective-permute-start | bytes 1671176 | tf_op jit(solution)/shard_map/ppermute | solution.py:617
  61.8 3.4 %copy-start = (f32[16,8,128,128]{3,2,1,0:T(8,128)S(1)}, f32[16,8,128,128]{3,2,1,0:T(8,128)}, u32[]{:S(2)}) copy-start(f32[16,8,128,128]{3,2,1,0:T(8,128)} %refs_2_.1) | copy-start | bytes 25165828
  65.2 17.7 %copy-start.1 = (f32[16,8,128,128]{3,2,1,0:T(8,128)S(1)}, f32[16,8,128,128]{3,2,1,0:T(8,128)}, u32[]{:S(2)}) copy-start(f32[16,8,128,128]{3,2,1,0:T(8,128)} %refs_2_.1) | copy-start | bytes 25165828
  70.0 7.6 %collective-permute-start.16 = (bf16[256,256]{1,0:T(8,128)(2,1)S(1)}, bf16[256,256]{1,0:T(8,128)(2,1)S(1)}, u32[]{:S(2)}, u32[]{:S(2)}) collective-permute-start(bf16[256,256]{1,0:T(8,128)(2,1)S(1)} %get-tuple-element.26.refs_4_), channel_id=1, source_target_pairs={{0,16},{8,24},{16,0},{24,8},{32,48},{40,56},{48,32},{56,40},{64,80... | collective-permute-start | bytes 393224 | tf_op jit(solution)/shard_map/ppermute | solution.py:615
  70.1 8.6 %collective-permute-start.15 = (bf16[256,256]{1,0:T(8,128)(2,1)S(1)}, bf16[256,256]{1,0:T(8,128)(2,1)S(1)}, u32[]{:S(2)}, u32[]{:S(2)}) collective-permute-start(bf16[256,256]{1,0:T(8,128)(2,1)S(1)} %get-tuple-element.26.refs_4_), channel_id=1, source_target_pairs={{0,24},{8,0},{16,8},{24,16},{32,56},{40,32},{48,40},{56,48},{64,88... | collective-permute-start | bytes 393224 | tf_op jit(solution)/shard_map/ppermute | solution.py:615
  70.2 8.6 %collective-permute-start.14 = (bf16[256,256]{1,0:T(8,128)(2,1)S(1)}, bf16[256,256]{1,0:T(8,128)(2,1)S(1)}, u32[]{:S(2)}, u32[]{:S(2)}) collective-permute-start(bf16[256,256]{1,0:T(8,128)(2,1)S(1)} %get-tuple-element.26.refs_4_), channel_id=1, source_target_pairs={{0,8},{8,16},{16,24},{24,0},{32,40},{40,48},{48,56},{56,32},{64,72... | collective-permute-start | bytes 393224 | tf_op jit(solution)/shard_map/ppermute | solution.py:615
  78.8 18.7 %collective-permute-start.19 = (bf16[4,256,256]{2,1,0:T(8,128)(2,1)S(1)}, bf16[4,256,256]{2,1,0:T(8,128)(2,1)S(1)}, u32[]{:S(2)}, u32[]{:S(2)}) collective-permute-start(bf16[4,256,256]{2,1,0:T(8,128)(2,1)S(1)} %pad_maximum_fusion.1.refs_7_), channel_id=1, source_target_pairs={{0,64},{8,72},{16,80},{24,88},{32,96},{40,104},{48,112},{56,120},{... | collective-permute-start | bytes 1572872 | tf_op jit(solution)/shard_map/ppermute | solution.py:617
  78.9 25.1 %collective-permute-start.18 = (bf16[4,256,256]{2,1,0:T(8,128)(2,1)S(1)}, bf16[4,256,256]{2,1,0:T(8,128)(2,1)S(1)}, u32[]{:S(2)}, u32[]{:S(2)}) collective-permute-start(bf16[4,256,256]{2,1,0:T(8,128)(2,1)S(1)} %pad_maximum_fusion.1.refs_7_), channel_id=1, source_target_pairs={{0,96},{8,104},{16,112},{24,120},{32,0},{40,8},{48,16},{56,24},{64... | collective-permute-start | bytes 1572872 | tf_op jit(solution)/shard_map/ppermute | solution.py:617
  88.1 40.3 %collective-permute-start.13 = (bf16[14,128,256]{2,1,0:T(8,128)(2,1)S(1)}, bf16[14,128,256]{2,1,0:T(8,128)(2,1)S(1)}, u32[]{:S(2)}, u32[]{:S(2)}) collective-permute-start(bf16[14,128,256]{2,1,0:T(8,128)(2,1)S(1)} %plain_first.1.refs_4_), channel_id=1, source_target_pairs={{32,24},{64,56},{96,88},{33,25},{65,57},{97,89},{34,26},{66,58},{9... | collective-permute-start | bytes 2752520 | tf_op jit(solution)/shard_map/ppermute | solution.py:608
  89.4 39.0 %collective-permute-start.12 = (bf16[14,128,256]{2,1,0:T(8,128)(2,1)S(1)}, bf16[14,128,256]{2,1,0:T(8,128)(2,1)S(1)}, u32[]{:S(2)}, u32[]{:S(2)}) collective-permute-start(bf16[14,128,256]{2,1,0:T(8,128)(2,1)S(1)} %plain_first.1.refs_4_), channel_id=1, source_target_pairs={{8,0},{16,8},{24,16},{40,32},{48,40},{56,48},{72,64},{80,72},{88,8... | collective-permute-start | bytes 2752520 | tf_op jit(solution)/shard_map/ppermute | solution.py:609
  90.8 37.7 %collective-permute-start.11 = (bf16[14,128,256]{2,1,0:T(8,128)(2,1)S(1)}, bf16[14,128,256]{2,1,0:T(8,128)(2,1)S(1)}, u32[]{:S(2)}, u32[]{:S(2)}) collective-permute-start(bf16[14,128,256]{2,1,0:T(8,128)(2,1)S(1)} %plain_first.1.refs_4_), channel_id=1, source_target_pairs={{24,32},{56,64},{88,96},{25,33},{57,65},{89,97},{26,34},{58,66},{9... | collective-permute-start | bytes 2752520 | tf_op jit(solution)/shard_map/ppermute | solution.py:608
  97.5 31.0 %collective-permute-start.10 = (bf16[14,128,256]{2,1,0:T(8,128)(2,1)S(1)}, bf16[14,128,256]{2,1,0:T(8,128)(2,1)S(1)}, u32[]{:S(2)}, u32[]{:S(2)}) collective-permute-start(bf16[14,128,256]{2,1,0:T(8,128)(2,1)S(1)} %plain_first.1.refs_4_), channel_id=1, source_target_pairs={{0,8},{8,16},{16,24},{32,40},{40,48},{48,56},{64,72},{72,80},{80,8... | collective-permute-start | bytes 2752520 | tf_op jit(solution)/shard_map/ppermute | solution.py:609
  104.0 24.4 %collective-permute-start.17 = (bf16[4,256,256]{2,1,0:T(8,128)(2,1)S(1)}, bf16[4,256,256]{2,1,0:T(8,128)(2,1)S(1)}, u32[]{:S(2)}, u32[]{:S(2)}) collective-permute-start(bf16[4,256,256]{2,1,0:T(8,128)(2,1)S(1)} %pad_maximum_fusion.1.refs_7_), channel_id=1, source_target_pairs={{0,32},{8,40},{16,48},{24,56},{32,64},{40,72},{48,80},{56,88},{64,... | collective-permute-start | bytes 1572872 | tf_op jit(solution)/shard_map/ppermute | solution.py:617
  136.7 4.6 %collective-permute-start.20 = (f32[4,72,16,128]{3,2,1,0:T(8,128)S(1)}, f32[4,72,16,128]{3,2,1,0:T(8,128)S(1)}, u32[]{:S(2)}, u32[]{:S(2)}) collective-permute-start(f32[4,72,16,128]{3,2,1,0:T(8,128)S(1)} %get-tuple-element.28), channel_id=1, source_target_pairs={{0,1},{1,0},{2,3},{3,2},{4,5},{5,4},{6,7},{7,6},{8,9},{9,8},{10,11... | collective-permute-start | bytes 7077896 | tf_op jit(solution)/shard_map/ppermute | solution.py:653
  142.3 10.8 %collective-permute-start.21 = (s16[77,16,128]{2,1,0:T(8,128)(2,1)S(1)}, s16[77,16,128]{2,1,0:T(8,128)(2,1)S(1)}, u32[]{:S(2)}, u32[]{:S(2)}) collective-permute-start(s16[77,16,128]{2,1,0:T(8,128)(2,1)S(1)} %get-tuple-element.30), channel_id=1, source_target_pairs={{0,2},{1,3},{2,4},{3,5},{4,6},{5,7},{6,0},{7,1},{8,10},{9,11},{10,... | collective-permute-start | bytes 946184 | tf_op jit(solution)/shard_map/ppermute | solution.py:657
  144.0 17.1 %collective-permute-start.22 = (s16[77,16,128]{2,1,0:T(8,128)(2,1)S(1)}, s16[77,16,128]{2,1,0:T(8,128)(2,1)S(1)}, u32[]{:S(2)}, u32[]{:S(2)}) collective-permute-start(s16[77,16,128]{2,1,0:T(8,128)(2,1)S(1)} %get-tuple-element.31), channel_id=1, source_target_pairs={{0,4},{1,5},{2,6},{3,7},{4,0},{5,1},{6,2},{7,3},{8,12},{9,13},{10,... | collective-permute-start | bytes 946184 | tf_op jit(solution)/shard_map/ppermute | solution.py:658
  146.9 14.2 %collective-permute-start.23 = (s16[77,16,128]{2,1,0:T(8,128)(2,1)S(1)}, s16[77,16,128]{2,1,0:T(8,128)(2,1)S(1)}, u32[]{:S(2)}, u32[]{:S(2)}) collective-permute-start(s16[77,16,128]{2,1,0:T(8,128)(2,1)S(1)} %get-tuple-element.32), channel_id=1, source_target_pairs={{0,6},{1,7},{2,0},{3,1},{4,2},{5,3},{6,4},{7,5},{8,14},{9,15},{10,... | collective-permute-start | bytes 946184 | tf_op jit(solution)/shard_map/ppermute | solution.py:659
  162.6 9.9 %collective-permute-start.26 = (s16[77,16,128]{2,1,0:T(8,128)(2,1)S(1)}, s16[77,16,128]{2,1,0:T(8,128)(2,1)S(1)}, u32[]{:S(2)}, u32[]{:S(2)}) collective-permute-start(s16[77,16,128]{2,1,0:T(8,128)(2,1)S(1)} %get-tuple-element.34), channel_id=1, source_target_pairs={{0,2},{1,3},{2,4},{3,5},{4,6},{5,7},{6,0},{7,1},{8,10},{9,11},{10,... | collective-permute-start | bytes 946184 | tf_op jit(solution)/shard_map/ppermute | solution.py:641
  163.9 16.5 %collective-permute-start.25 = (s16[77,16,128]{2,1,0:T(8,128)(2,1)S(1)}, s16[77,16,128]{2,1,0:T(8,128)(2,1)S(1)}, u32[]{:S(2)}, u32[]{:S(2)}) collective-permute-start(s16[77,16,128]{2,1,0:T(8,128)(2,1)S(1)} %get-tuple-element.34), channel_id=1, source_target_pairs={{0,4},{1,5},{2,6},{3,7},{4,0},{5,1},{6,2},{7,3},{8,12},{9,13},{10,... | collective-permute-start | bytes 946184 | tf_op jit(solution)/shard_map/ppermute | solution.py:640
  166.3 14.1 %collective-permute-start.24 = (s16[77,16,128]{2,1,0:T(8,128)(2,1)S(1)}, s16[77,16,128]{2,1,0:T(8,128)(2,1)S(1)}, u32[]{:S(2)}, u32[]{:S(2)}) collective-permute-start(s16[77,16,128]{2,1,0:T(8,128)(2,1)S(1)} %get-tuple-element.34), channel_id=1, source_target_pairs={{0,6},{1,7},{2,0},{3,1},{4,2},{5,3},{6,4},{7,5},{8,14},{9,15},{10,... | collective-permute-start | bytes 946184 | tf_op jit(solution)/shard_map/ppermute | solution.py:639
  180.7 3.0 %collective-permute-start.27 = (s16[4,77,16,128]{3,2,1,0:T(8,128)(2,1)S(1)}, s16[4,77,16,128]{3,2,1,0:T(8,128)(2,1)S(1)}, u32[]{:S(2)}, u32[]{:S(2)}) collective-permute-start(s16[4,77,16,128]{3,2,1,0:T(8,128)(2,1)S(1)} %pad_add_fusion.refs_2_), channel_id=1, source_target_pairs={{0,1},{1,0},{2,3},{3,2},{4,5},{5,4},{6,7},{7,6},{8,9},{9,8},{10,11... | collective-permute-start | bytes 3784712 | tf_op jit(solution)/shard_map/ppermute | solution.py:644
  185.2 8.0 %collective-permute-start.34 = (bf16[256,256]{1,0:T(8,128)(2,1)S(1)}, bf16[256,256]{1,0:T(8,128)(2,1)S(1)}, u32[]{:S(2)}, u32[]{:S(2)}) collective-permute-start(bf16[256,256]{1,0:T(8,128)(2,1)S(1)} %hub_later.1.refs_5_), channel_id=1, source_target_pairs={{0,16},{8,24},{16,0},{24,8},{32,48},{40,56},{48,32},{56,40},{64,80... | collective-permute-start | bytes 393224 | tf_op jit(solution)/shard_map/ppermute | solution.py:615
  185.3 9.6 %collective-permute-start.33 = (bf16[256,256]{1,0:T(8,128)(2,1)S(1)}, bf16[256,256]{1,0:T(8,128)(2,1)S(1)}, u32[]{:S(2)}, u32[]{:S(2)}) collective-permute-start(bf16[256,256]{1,0:T(8,128)(2,1)S(1)} %hub_later.1.refs_5_), channel_id=1, source_target_pairs={{0,24},{8,0},{16,8},{24,16},{32,56},{40,32},{48,40},{56,48},{64,88... | collective-permute-start | bytes 393224 | tf_op jit(solution)/shard_map/ppermute | solution.py:615
  185.4 9.5 %collective-permute-start.32 = (bf16[256,256]{1,0:T(8,128)(2,1)S(1)}, bf16[256,256]{1,0:T(8,128)(2,1)S(1)}, u32[]{:S(2)}, u32[]{:S(2)}) collective-permute-start(bf16[256,256]{1,0:T(8,128)(2,1)S(1)} %hub_later.1.refs_5_), channel_id=1, source_target_pairs={{0,8},{8,16},{16,24},{24,0},{32,40},{40,48},{48,56},{56,32},{64,72... | collective-permute-start | bytes 393224 | tf_op jit(solution)/shard_map/ppermute | solution.py:615
  195.0 16.4 %collective-permute-start.37 = (bf16[4,256,256]{2,1,0:T(8,128)(2,1)S(1)}, bf16[4,256,256]{2,1,0:T(8,128)(2,1)S(1)}, u32[]{:S(2)}, u32[]{:S(2)}) collective-permute-start(bf16[4,256,256]{2,1,0:T(8,128)(2,1)S(1)} %pad_maximum_fusion.2.refs_7_), channel_id=1, source_target_pairs={{0,64},{8,72},{16,80},{24,88},{32,96},{40,104},{48,112},{56,120},{... | collective-permute-start | bytes 1572872 | tf_op jit(solution)/shard_map/ppermute | solution.py:617
  195.1 24.9 %collective-permute-start.36 = (bf16[4,256,256]{2,1,0:T(8,128)(2,1)S(1)}, bf16[4,256,256]{2,1,0:T(8,128)(2,1)S(1)}, u32[]{:S(2)}, u32[]{:S(2)}) collective-permute-start(bf16[4,256,256]{2,1,0:T(8,128)(2,1)S(1)} %pad_maximum_fusion.2.refs_7_), channel_id=1, source_target_pairs={{0,96},{8,104},{16,112},{24,120},{32,0},{40,8},{48,16},{56,24},{64... | collective-permute-start | bytes 1572872 | tf_op jit(solution)/shard_map/ppermute | solution.py:617
  202.0 40.9 %collective-permute-start.31 = (bf16[14,128,256]{2,1,0:T(8,128)(2,1)S(1)}, bf16[14,128,256]{2,1,0:T(8,128)(2,1)S(1)}, u32[]{:S(2)}, u32[]{:S(2)}) collective-permute-start(bf16[14,128,256]{2,1,0:T(8,128)(2,1)S(1)} %plain_later.1.refs_4_), channel_id=1, source_target_pairs={{32,24},{64,56},{96,88},{33,25},{65,57},{97,89},{34,26},{66,58},{9... | collective-permute-start | bytes 2752520 | tf_op jit(solution)/shard_map/ppermute | solution.py:608
  203.3 39.6 %collective-permute-start.30 = (bf16[14,128,256]{2,1,0:T(8,128)(2,1)S(1)}, bf16[14,128,256]{2,1,0:T(8,128)(2,1)S(1)}, u32[]{:S(2)}, u32[]{:S(2)}) collective-permute-start(bf16[14,128,256]{2,1,0:T(8,128)(2,1)S(1)} %plain_later.1.refs_4_), channel_id=1, source_target_pairs={{8,0},{16,8},{24,16},{40,32},{48,40},{56,48},{72,64},{80,72},{88,8... | collective-permute-start | bytes 2752520 | tf_op jit(solution)/shard_map/ppermute | solution.py:609
  204.7 38.3 %collective-permute-start.29 = (bf16[14,128,256]{2,1,0:T(8,128)(2,1)S(1)}, bf16[14,128,256]{2,1,0:T(8,128)(2,1)S(1)}, u32[]{:S(2)}, u32[]{:S(2)}) collective-permute-start(bf16[14,128,256]{2,1,0:T(8,128)(2,1)S(1)} %plain_later.1.refs_4_), channel_id=1, source_target_pairs={{24,32},{56,64},{88,96},{25,33},{57,65},{89,97},{26,34},{58,66},{9... | collective-permute-start | bytes 2752520 | tf_op jit(solution)/shard_map/ppermute | solution.py:608
  211.4 31.6 %collective-permute-start.28 = (bf16[14,128,256]{2,1,0:T(8,128)(2,1)S(1)}, bf16[14,128,256]{2,1,0:T(8,128)(2,1)S(1)}, u32[]{:S(2)}, u32[]{:S(2)}) collective-permute-start(bf16[14,128,256]{2,1,0:T(8,128)(2,1)S(1)} %plain_later.1.refs_4_), channel_id=1, source_target_pairs={{0,8},{8,16},{16,24},{32,40},{40,48},{48,56},{64,72},{72,80},{80,8... | collective-permute-start | bytes 2752520 | tf_op jit(solution)/shard_map/ppermute | solution.py:609
  220.1 22.9 %collective-permute-start.35 = (bf16[4,256,256]{2,1,0:T(8,128)(2,1)S(1)}, bf16[4,256,256]{2,1,0:T(8,128)(2,1)S(1)}, u32[]{:S(2)}, u32[]{:S(2)}) collective-permute-start(bf16[4,256,256]{2,1,0:T(8,128)(2,1)S(1)} %pad_maximum_fusion.2.refs_7_), channel_id=1, source_target_pairs={{0,32},{8,40},{16,48},{24,56},{32,64},{40,72},{48,80},{56,88},{64,... | collective-permute-start | bytes 1572872 | tf_op jit(solution)/shard_map/ppermute | solution.py:617
  251.2 4.6 %collective-permute-start.38 = (f32[4,72,16,128]{3,2,1,0:T(8,128)S(1)}, f32[4,72,16,128]{3,2,1,0:T(8,128)S(1)}, u32[]{:S(2)}, u32[]{:S(2)}) collective-permute-start(f32[4,72,16,128]{3,2,1,0:T(8,128)S(1)} %get-tuple-element.36), channel_id=1, source_target_pairs={{0,1},{1,0},{2,3},{3,2},{4,5},{5,4},{6,7},{7,6},{8,9},{9,8},{10,11... | collective-permute-start | bytes 7077896 | tf_op jit(solution)/shard_map/ppermute | solution.py:653
  256.9 11.2 %collective-permute-start.39 = (s16[77,16,128]{2,1,0:T(8,128)(2,1)S(1)}, s16[77,16,128]{2,1,0:T(8,128)(2,1)S(1)}, u32[]{:S(2)}, u32[]{:S(2)}) collective-permute-start(s16[77,16,128]{2,1,0:T(8,128)(2,1)S(1)} %get-tuple-element.38), channel_id=1, source_target_pairs={{0,2},{1,3},{2,4},{3,5},{4,6},{5,7},{6,0},{7,1},{8,10},{9,11},{10,... | collective-permute-start | bytes 946184 | tf_op jit(solution)/shard_map/ppermute | solution.py:657
  258.1 16.6 %collective-permute-start.40 = (s16[77,16,128]{2,1,0:T(8,128)(2,1)S(1)}, s16[77,16,128]{2,1,0:T(8,128)(2,1)S(1)}, u32[]{:S(2)}, u32[]{:S(2)}) collective-permute-start(s16[77,16,128]{2,1,0:T(8,128)(2,1)S(1)} %get-tuple-element.39), channel_id=1, source_target_pairs={{0,4},{1,5},{2,6},{3,7},{4,0},{5,1},{6,2},{7,3},{8,12},{9,13},{10,... | collective-permute-start | bytes 946184 | tf_op jit(solution)/shard_map/ppermute | solution.py:658
  260.6 14.5 %collective-permute-start.41 = (s16[77,16,128]{2,1,0:T(8,128)(2,1)S(1)}, s16[77,16,128]{2,1,0:T(8,128)(2,1)S(1)}, u32[]{:S(2)}, u32[]{:S(2)}) collective-permute-start(s16[77,16,128]{2,1,0:T(8,128)(2,1)S(1)} %get-tuple-element.40), channel_id=1, source_target_pairs={{0,6},{1,7},{2,0},{3,1},{4,2},{5,3},{6,4},{7,5},{8,14},{9,15},{10,... | collective-permute-start | bytes 946184 | tf_op jit(solution)/shard_map/ppermute | solution.py:659
where the time goes:
time: 278 us; the launch traced here: 277 us
  waiting for transfers between devices  154 us (55%)
  starting transfers between devices  75 us (27%)
  Pallas kernels  39.3 us (14%)
  local copies, waits for them, and re-layouts  8.14 us (3%)
    ppermute x9, waiting for transfers between devices, share_hubs(): lax.ppermute(column, 'var', var_shift(d, 0))  85.2 us
    ppermute x6, starting transfers between devices, share_near(): crossing = lax.ppermute(value, 'var', edge)  24.4 us
    ppermute x9, waiting for transfers between devices, share_hubs(): lax.ppermute(value, 'var', var_shift(0, d))  17.7 us
    pallas_call x2, Pallas kernels, gradient(): pl.pallas_call(lambda *refs: gradient_kernel(scale, slots, *refs), out_sh...  16.5 us
    ppermute x9, starting transfers between devices, share_hubs(): lax.ppermute(column, 'var', var_shift(d, 0))  15.6 us
    ppermute x2, waiting for transfers between devices, per_device(): lax.ppermute(across, 'samp', samp_shift(2, 0))  14.6 us
    ppermute x2, waiting for transfers between devices, per_device(): lax.ppermute(up, 'samp', samp_shift(1, 0))  11.6 us
    ppermute x9, starting transfers between devices, share_hubs(): lax.ppermute(value, 'var', var_shift(0, d))  10.6 us
  transfers between devices with their start and end apart: 42, of which 23 were waited for; matrix products, arithmetic and copies ran while one was open for 1% of the time, Pallas kernels for 4%

commit v1 on v0

--- a/solution.py
+++ b/solution.py
@@ -120,18 +120,20 @@
 
 class Gather:
     def __init__(self, near, hubs, table, sem, bs):
-        below, below_edge, own, above, above_edge = near
-        plain = own.shape[0]
-        size = plain * bs
+        below, own, above, crossing, turn = near
+        size = own.shape[0] * bs
         z = lax.axis_index("var") % SIDE
 
         def copy(ref, at):
-            return pltpu.make_async_copy(ref.reshape(size, ref.shape[2]), table.at[pl.ds(at, size), :], sem)
-
-        self.choices = [
-            (z == 0, copy(below, 0), copy(below_edge, 0)),
-            (z == SIDE - 1, copy(above, 2 * size), copy(above_edge, 2 * size)),
-        ]
+            rows = ref.shape[0] * bs
+            return pltpu.make_async_copy(
+                ref.reshape(rows, ref.shape[2]), table.at[pl.ds(at, rows), :], sem
+            )
+
+        self.choices = []
+        for edge, usual, at in ((z == 0, below, 0), (z == SIDE - 1, above, 2 * size)):
+            pair = [copy(crossing, at), copy(turn, at + crossing.shape[0] * bs)]
+            self.choices.append((edge, copy(usual, at), pair))
         self.copies = [copy(own, size)]
         at = 3 * size
         for ref in hubs:
@@ -148,8 +150,9 @@
     def start(self):
         for copy in self.copies:
             copy.start()
-        for edge, usual, other in self.choices:
-            pl.when(edge)(other.start)
+        for edge, usual, pair in self.choices:
+            for other in pair:
+                pl.when(edge)(other.start)
             pl.when(jnp.logical_not(edge))(usual.start)
 
     def wait(self):
@@ -238,9 +241,9 @@
 
 def first_hub_kernel(*refs):
     counts, pattern, ids, omega = refs[:4]
-    near, hubs = refs[4:9], refs[9:13]
-    out, lookup, table, rows_out = refs[13:17]
-    order, inverse, tiles, table_sem, tile_sem = refs[17:]
+    near, hubs = refs[4:9], refs[9:14]
+    out, lookup, table, rows_out = refs[14:18]
+    order, inverse, tiles, table_sem, tile_sem = refs[18:]
     rows, slots = pattern.shape
     bs, share = tiles.shape[1], rows_out.shape[1]
     row_order(counts, order, slots)
@@ -278,7 +281,7 @@
             jax.ShapeDtypeStruct((table, local), BF),
             jax.ShapeDtypeStruct((total, bs // part_count, bs), F32),
         ),
-        in_specs=[SMEM, SMEM, SMEM] + [ANY] * 10,
+        in_specs=[SMEM, SMEM, SMEM] + [ANY] * 11,
         out_specs=(VMEM, SMEM, VMEM, VMEM),
         scratch_shapes=[
             pltpu.SMEM((rows,), jnp.int32),
@@ -436,9 +439,9 @@
 
 def gradient_kernel(scale, slots, *refs):
     lookup, x_table = refs[:2]
-    near, hubs = refs[2:7], refs[7:11]
-    keep, send, m_table, sem = refs[11:]
-    plain, bs, _ = near[0].shape
+    near, hubs = refs[2:7], refs[7:12]
+    keep, send, m_table, sem = refs[12:]
+    plain, bs, _ = near[1].shape
     gather = Gather(near, hubs, m_table, sem, bs)
     gather.start()
     gather.wait()
@@ -488,7 +491,7 @@
     return pl.pallas_call(
         lambda *refs: gradient_kernel(scale, slots, *refs),
         out_shape=(shape, shape),
-        in_specs=[SMEM, VMEM] + [ANY] * 9,
+        in_specs=[SMEM, VMEM] + [ANY] * 10,
         out_specs=(VMEM, VMEM),
         scratch_shapes=[pltpu.VMEM(table.shape, BF), pltpu.SemaphoreType.DMA],
         compiler_params=grant(24),
@@ -599,22 +602,36 @@
 
 
 def share_near(value):
+    last = lax.axis_size("var") // SIDE - 1
     size = lax.axis_size("var")
-    up = [(i, i + 1) for i in range(size - 1)]
-    moves = []
-    for pairs in (up, [(j, i) for i, j in up]):
-        inner = [(i, j) for i, j in pairs if i // SIDE == j // SIDE]
-        edge = [(i, j) for i, j in pairs if i // SIDE != j // SIDE]
-        crossing = lax.ppermute(value, "var", edge)
-        moves.append((crossing, lax.ppermute(value, "var", inner)))
-    (below_edge, below), (above_edge, above) = moves
-    return below, below_edge, value, above, above_edge
+    far = SIDE - 1
+    direct, there, over = [], [], []
+    for x in range(last):
+        low, high = x * SIDE, (x + 1) * SIDE
+        direct += [(low + far, high), (high, low + far)]
+        there += [(low + far, low), (high, high + far)]
+        over += [(low, high), (high + far, low + far)]
+    half = value.shape[0] // 2
+    crossing = lax.ppermute(value[:half], "var", direct)
+    turn = lax.ppermute(value[half:], "var", there)
+    turn = lax.ppermute(turn, "var", over)
+    up = [(i, i + 1) for i in range(size - 1) if (i + 1) % SIDE]
+    below = lax.ppermute(value, "var", up)
+    above = lax.ppermute(value, "var", [(j, i) for i, j in up])
+    return below, value, above, crossing, turn
 
 
 def share_hubs(value):
     by_z = [value] + [lax.ppermute(value, "var", var_shift(0, d)) for d in (1, -1, 2)]
     column = jnp.stack(by_z)
-    return [column] + [lax.ppermute(column, "var", var_shift(d, 0)) for d in (1, -1, 2)]
+    half = SIDE // 2
+    ahead = lax.ppermute(column, "var", var_shift(1, 0))
+    behind = lax.ppermute(column, "var", var_shift(-1, 0))
+    across = [
+        lax.ppermute(ahead[:half], "var", var_shift(1, 0)),
+        lax.ppermute(behind[half:], "var", var_shift(-1, 0)),
+    ]
+    return [column, ahead, behind] + across
 
 
 def per_device(data, omega, pattern, counts):
@@ -625,7 +642,7 @@
     x_hubs = share_hubs(x_hub)
     x_own = pack_plain(data, counts, slots, bs, x_hub)
     x_near = share_near(x_own)
-    ids = jnp.stack([g[:, HUB_DEV * bs : HUB_DEV * bs + HUB_DEV, 0] for g in x_hubs])
+    ids = jnp.concatenate([g[:, HUB_DEV * bs : HUB_DEV * bs + HUB_DEV, 0] for g in x_hubs])
     ids = ids.reshape(-1).astype(jnp.int32)
     for iteration in range(ITERS):
         if iteration == 0:

time: 278 us -> 249 us (0.90)
  the two profiles are of different devices: /device:TPU:98 before, /device:TPU:1 now
where the time goes in v1:
time: 249 us
  starting transfers between devices  99.8 us (40%)
  waiting for transfers between devices  98 us (39%)
  Pallas kernels  40.5 us (16%)
  local copies, waits for them, and re-layouts  9.36 us (4%)
    ppermute x3, waiting for transfers between devices, share_hubs(): lax.ppermute(ahead[:half], 'var', var_shift(1, 0))  22.2 us
    pallas_call x2, Pallas kernels, gradient(): pl.pallas_call(lambda *refs: gradient_kernel(scale, slots, *refs), out_sh...  17.1 us
    ppermute x3, starting transfers between devices, share_hubs(): lax.ppermute(ahead[:half], 'var', var_shift(1, 0))  15.8 us
    ppermute x2, waiting for transfers between devices, per_device(): lax.ppermute(across, 'samp', samp_shift(2, 0))  15 us
    ppermute x3, starting transfers between devices, share_near(): turn = lax.ppermute(turn, 'var', over)  13.5 us
    ppermute x3, starting transfers between devices, share_near(): below = lax.ppermute(value, 'var', up)  13 us
    ppermute x2, waiting for transfers between devices, per_device(): lax.ppermute(up, 'samp', samp_shift(1, 0))  11.2 us
    ppermute x9, starting transfers between devices, share_hubs(): lax.ppermute(value, 'var', var_shift(0, d))  9.19 us
  transfers between devices with their start and end apart: 48, of which 23 were waited for; matrix products, arithmetic and copies ran while one was open for 2% of the time, Pallas kernels for 4%

profile of v1, /device:TPU:1, one launch (start us, length us, event | category | flops | bytes accessed | tf_op | source)
XLA Modules:
  0.0 248.5 jit_solution(6531765033830761992)
XLA Ops:
  0.0 1.2 copy-done.2
  2.8 4.5 %collective-permute-start.2 = (bf16[272,256]{1,0:T(8,128)(2,1)S(1)}, bf16[272,256]{1,0:T(8,128)(2,1)S(1)}, u32[]{:S(2)}, u32[]{:S(2)}) collective-permute-start(bf16[272,256]{1,0:T(8,128)(2,1)S(1)} %pack_hub.1.refs_2_), channel_id=1, source_target_pairs={{0,16},{8,24},{16,0},{24,8},{32,48},{40,56},{48,32},{56,40},{64,80... | collective-permute-start | bytes 417800 | tf_op jit(solution)/shard_map/ppermute | solution.py:625
  8.8 1.2 pack_plain.1.refs_5_
  10.7 3.5 %collective-permute-done.1 = bf16[272,256]{1,0:T(8,128)(2,1)S(1)} collective-permute-done((bf16[272,256]{1,0:T(8,128)(2,1)S(1)}, bf16[272,256]{1,0:T(8,128)(2,1)S(1)}, u32[]{:S(2)}, u32[]{:S(2)}) %collective-permute-start.1) | collective-permute-done | bytes 139296 | tf_op jit(solution)/shard_map/ppermute | solution.py:625
  14.3 2.5 %collective-permute-start.4 = (bf16[4,272,256]{2,1,0:T(8,128)(2,1)S(1)}, bf16[4,272,256]{2,1,0:T(8,128)(2,1)S(1)}, u32[]{:S(2)}, u32[]{:S(2)}) collective-permute-start(bf16[4,272,256]{2,1,0:T(8,128)(2,1)S(1)} %pad_maximum_fusion.refs_9_), channel_id=1, source_target_pairs={{0,96},{8,104},{16,112},{24,120},{32,0},{40,8},{48,16},{56,24},{64... | collective-permute-start | bytes 1671176 | tf_op jit(solution)/shard_map/ppermute | solution.py:629
  17.7 1.3 collective-permute-start.10
  19.0 1.3 collective-permute-start.8
  20.3 4.9 %collective-permute-start.7 = (bf16[14,128,256]{2,1,0:T(8,128)(2,1)S(1)}, bf16[14,128,256]{2,1,0:T(8,128)(2,1)}, u32[]{:S(2)}, u32[]{:S(2)}) collective-permute-start(bf16[14,128,256]{2,1,0:T(8,128)(2,1)S(1)} %pack_plain.1.refs_5_), channel_id=1, source_target_pairs={{0,8},{8,16},{16,24},{32,40},{40,48},{48,56},{64,72},{72,80},{80,8... | collective-permute-start | bytes 2752520 | tf_op jit(solution)/shard_map/ppermute | solution.py:619
  25.2 2.1 collective-permute-done.4.refs_11_
  27.4 5.3 %collective-permute-start.6 = (bf16[2,272,256]{2,1,0:T(8,128)(2,1)S(1)}, bf16[2,272,256]{2,1,0:T(8,128)(2,1)}, u32[]{:S(2)}, u32[]{:S(2)}) collective-permute-start(bf16[2,272,256]{2,1,0:T(8,128)(2,1)S(1)} %slice.73), channel_id=1, source_target_pairs={{0,96},{8,104},{16,112},{24,120},{32,0},{40,8},{48,16},{56,24},{64... | collective-permute-start | bytes 835592 | tf_op jit(solution)/shard_map/ppermute | solution.py:632
  32.7 1.5 collective-permute-start.9
  34.1 6.9 %collective-permute-start.11 = (bf16[7,128,256]{2,1,0:T(8,128)(2,1)}, bf16[7,128,256]{2,1,0:T(8,128)(2,1)}, u32[]{:S(2)}, u32[]{:S(2)}) collective-permute-start(bf16[7,128,256]{2,1,0:T(8,128)(2,1)} %collective-permute-done.10), channel_id=1, source_target_pairs={{0,32},{56,24},{32,64},{88,56},{64,96},{120,88},{1,33},{57,25},{33... | collective-permute-start | bytes 1376264 | tf_op jit(solution)/shard_map/ppermute | solution.py:617
  43.0 11.5 %collective-permute-done.5.refs_12_ = bf16[2,272,256]{2,1,0:T(8,128)(2,1)} collective-permute-done((bf16[2,272,256]{2,1,0:T(8,128)(2,1)}, bf16[2,272,256]{2,1,0:T(8,128)(2,1)}, u32[]{:S(2)}, u32[]{:S(2)}) %collective-permute-start.5) | collective-permute-done | bytes 278560 | tf_op jit(solution)/shard_map/ppermute | solution.py:631
  55.7 3.4 %copy-done = f32[16,8,128,128]{3,2,1,0:T(8,128)S(1)} copy-done((f32[16,8,128,128]{3,2,1,0:T(8,128)S(1)}, f32[16,8,128,128]{3,2,1,0:T(8,128)}, u32[]{:S(2)}) %copy-start) | copy-done | bytes 8388632
  59.1 5.4 %hub_first.1 = (bf16[256,256]{1,0:T(8,128)(2,1)S(1)}, s32[72]{0:T(128)S(1)}, bf16[9472,256]{1,0:T(8,128)(2,1)S(1)}, f32[72,16,128]{2,1,0:T(8,128)S(1)}) custom-call(s32[16]{0:T(128)S(1)} %copy-done.4, s32[16,8]{1,0:T(8,128)S(1)} %copy.18.refs_1_, s32[32]{0:T(128)S(1)} %reshape.3.refs_2_, f32[16,8,128,128]{3,2,1,0:T(8,128)S(1)} %copy-done, ...), custom_call_target="tpu_custom_call" | custom-call | flops 268435456 | bytes 12582912 | tf_op jit(solution)/shard_map/hub_first/pallas_call | solution.py:276
  64.7 1.5 collective-permute-start.17
  66.1 5.2 %plain_first.1.refs_3_ = bf16[14,128,256]{2,1,0:T(8,128)(2,1)S(1)} custom-call(s32[16]{0:T(128)S(1)} %copy-done.4, s32[72]{0:T(128)S(1)} %get-tuple-element.24.refs_1_.refs_0_, f32[16,8,128,128]{3,2,1,0:T(8,128)S(1)} %copy-done.1, bf16[9472,256]{1,0:T(8,128)(2,1)S(1)} %get-tuple-element.25.refs_3_.refs_1_.refs_4_, bf16[256,256]{1,0:T(8,128)(2,1)S(1)} %get-tuple-element.26.refs_4_), custom_call_target="tpu_custom_call" | custom-call | flops 536870912 | bytes 10485760 | tf_op jit(solution)/shard_map/plain_first/pallas_call | solution.py:320
  71.4 1.3 collective-permute-start.15
  72.8 4.7 %collective-permute-start.21 = (bf16[4,256,256]{2,1,0:T(8,128)(2,1)S(1)}, bf16[4,256,256]{2,1,0:T(8,128)(2,1)S(1)}, u32[]{:S(2)}, u32[]{:S(2)}) collective-permute-start(bf16[4,256,256]{2,1,0:T(8,128)(2,1)S(1)} %pad_maximum_fusion.1.refs_7_), channel_id=1, source_target_pairs={{0,96},{8,104},{16,112},{24,120},{32,0},{40,8},{48,16},{56,24},{64... | collective-permute-start | bytes 1572872 | tf_op jit(solution)/shard_map/ppermute | solution.py:629
  77.6 1.3 collective-permute-start.13
  78.9 4.0 %collective-permute-start.12 = (bf16[14,128,256]{2,1,0:T(8,128)(2,1)S(1)}, bf16[14,128,256]{2,1,0:T(8,128)(2,1)S(1)}, u32[]{:S(2)}, u32[]{:S(2)}) collective-permute-start(bf16[14,128,256]{2,1,0:T(8,128)(2,1)S(1)} %plain_first.1.refs_3_), channel_id=1, source_target_pairs={{0,8},{8,16},{16,24},{32,40},{40,48},{48,56},{64,72},{72,80},{80,8... | collective-permute-start | bytes 2752520 | tf_op jit(solution)/shard_map/ppermute | solution.py:619
  84.1 2.2 collective-permute-done.21.refs_9_
  86.2 3.2 %collective-permute-start.16 = (bf16[7,128,256]{2,1,0:T(8,128)(2,1)S(1)}, bf16[7,128,256]{2,1,0:T(8,128)(2,1)S(1)}, u32[]{:S(2)}, u32[]{:S(2)}) collective-permute-start(bf16[7,128,256]{2,1,0:T(8,128)(2,1)S(1)} %collective-permute-done.15), channel_id=1, source_target_pairs={{0,32},{56,24},{32,64},{88,56},{64,96},{120,88},{1,33},{57,25},{33... | collective-permute-start | bytes 1376264 | tf_op jit(solution)/shard_map/ppermute | solution.py:617
  89.5 3.5 %collective-permute-done.20.refs_8_ = bf16[4,256,256]{2,1,0:T(8,128)(2,1)S(1)} collective-permute-done((bf16[4,256,256]{2,1,0:T(8,128)(2,1)S(1)}, bf16[4,256,256]{2,1,0:T(8,128)(2,1)S(1)}, u32[]{:S(2)}, u32[]{:S(2)}) %collective-permute-start.20) | collective-permute-done | bytes 524320 | tf_op jit(solution)/shard_map/ppermute | solution.py:628
  93.0 9.1 %collective-permute-start.22 = (bf16[2,256,256]{2,1,0:T(8,128)(2,1)S(1)}, bf16[2,256,256]{2,1,0:T(8,128)(2,1)S(1)}, u32[]{:S(2)}, u32[]{:S(2)}) collective-permute-start(bf16[2,256,256]{2,1,0:T(8,128)(2,1)S(1)} %slice.79), channel_id=1, source_target_pairs={{0,32},{8,40},{16,48},{24,56},{32,64},{40,72},{48,80},{56,88},{64,... | collective-permute-start | bytes 786440 | tf_op jit(solution)/shard_map/ppermute | solution.py:631
  102.1 5.3 %collective-permute-done.22.refs_10_ = bf16[2,256,256]{2,1,0:T(8,128)(2,1)S(1)} collective-permute-done((bf16[2,256,256]{2,1,0:T(8,128)(2,1)S(1)}, bf16[2,256,256]{2,1,0:T(8,128)(2,1)S(1)}, u32[]{:S(2)}, u32[]{:S(2)}) %collective-permute-start.22) | collective-permute-done | bytes 262176 | tf_op jit(solution)/shard_map/ppermute | solution.py:631
  107.4 8.5 %gradient.2 = (f32[4,72,16,128]{3,2,1,0:T(8,128)S(1)}, f32[4,72,16,128]{3,2,1,0:T(8,128)S(1)}) custom-call(s32[72]{0:T(128)S(1)} %get-tuple-element.24.refs_1_.refs_0_, bf16[9472,256]{1,0:T(8,128)(2,1)S(1)} %get-tuple-element.25.refs_3_.refs_1_.refs_4_, bf16[14,128,256]{2,1,0:T(8,128)(2,1)S(1)} %collective-permute-done.12.refs_2_, ...), custom_call_target="tpu_custom_call" | custom-call | flops 1073741824 | bytes 16777216 | tf_op jit(solution)/shard_map/gradient/pallas_call | solution.py:491
  115.9 5.5 %collective-permute-start.24 = (f32[4,72,16,128]{3,2,1,0:T(8,128)S(1)}, f32[4,72,16,128]{3,2,1,0:T(8,128)S(1)}, u32[]{:S(2)}, u32[]{:S(2)}) collective-permute-start(f32[4,72,16,128]{3,2,1,0:T(8,128)S(1)} %get-tuple-element.28), channel_id=1, source_target_pairs={{0,1},{1,0},{2,3},{3,2},{4,5},{5,4},{6,7},{7,6},{8,9},{9,8},{10,11... | collective-permute-start | bytes 7077896 | tf_op jit(solution)/shard_map/ppermute | solution.py:670
  121.4 4.2 %collective-permute-done.24.other = f32[4,72,16,128]{3,2,1,0:T(8,128)S(1)} collective-permute-done((f32[4,72,16,128]{3,2,1,0:T(8,128)S(1)}, f32[4,72,16,128]{3,2,1,0:T(8,128)S(1)}, u32[]{:S(2)}, u32[]{:S(2)}) %collective-permute-start.24) | collective-permute-done | bytes 2359328 | tf_op jit(solution)/shard_map/ppermute | solution.py:670
  125.6 1.0 add_cores.2
  126.6 1.4 collective-permute-start.25
  128.0 2.6 %collective-permute-start.26 = (s16[77,16,128]{2,1,0:T(8,128)(2,1)S(1)}, s16[77,16,128]{2,1,0:T(8,128)(2,1)S(1)}, u32[]{:S(2)}, u32[]{:S(2)}) collective-permute-start(s16[77,16,128]{2,1,0:T(8,128)(2,1)S(1)} %get-tuple-element.31), channel_id=1, source_target_pairs={{0,4},{1,5},{2,6},{3,7},{4,0},{5,1},{6,2},{7,3},{8,12},{9,13},{10,... | collective-permute-start | bytes 946184 | tf_op jit(solution)/shard_map/ppermute | solution.py:675
  130.6 1.1 collective-permute-start.27
  131.7 5.0 %collective-permute-done.25.refs_3_ = s16[77,16,128]{2,1,0:T(8,128)(2,1)S(1)} collective-permute-done((s16[77,16,128]{2,1,0:T(8,128)(2,1)S(1)}, s16[77,16,128]{2,1,0:T(8,128)(2,1)S(1)}, u32[]{:S(2)}, u32[]{:S(2)}) %collective-permute-start.25) | collective-permute-done | bytes 315424 | tf_op jit(solution)/shard_map/ppermute | solution.py:674
  136.6 7.9 %collective-permute-done.26.refs_4_ = s16[77,16,128]{2,1,0:T(8,128)(2,1)S(1)} collective-permute-done((s16[77,16,128]{2,1,0:T(8,128)(2,1)S(1)}, s16[77,16,128]{2,1,0:T(8,128)(2,1)S(1)}, u32[]{:S(2)}, u32[]{:S(2)}) %collective-permute-start.26) | collective-permute-done | bytes 315424 | tf_op jit(solution)/shard_map/ppermute | solution.py:675
  144.5 1.5 prox.1
  146.0 1.1 collective-permute-start.30
  147.1 2.8 %collective-permute-start.29 = (s16[77,16,128]{2,1,0:T(8,128)(2,1)S(1)}, s16[77,16,128]{2,1,0:T(8,128)(2,1)S(1)}, u32[]{:S(2)}, u32[]{:S(2)}) collective-permute-start(s16[77,16,128]{2,1,0:T(8,128)(2,1)S(1)} %get-tuple-element.34), channel_id=1, source_target_pairs={{0,4},{1,5},{2,6},{3,7},{4,0},{5,1},{6,2},{7,3},{8,12},{9,13},{10,... | collective-permute-start | bytes 946184 | tf_op jit(solution)/shard_map/ppermute | solution.py:657
  150.2 4.9 %collective-permute-done.30 = s16[77,16,128]{2,1,0:T(8,128)(2,1)S(1)} collective-permute-done((s16[77,16,128]{2,1,0:T(8,128)(2,1)S(1)}, s16[77,16,128]{2,1,0:T(8,128)(2,1)S(1)}, u32[]{:S(2)}, u32[]{:S(2)}) %collective-permute-start.30) | collective-permute-done | bytes 315424 | tf_op jit(solution)/shard_map/ppermute | solution.py:658
  155.1 8.6 %collective-permute-done.29 = s16[77,16,128]{2,1,0:T(8,128)(2,1)S(1)} collective-permute-done((s16[77,16,128]{2,1,0:T(8,128)(2,1)S(1)}, s16[77,16,128]{2,1,0:T(8,128)(2,1)S(1)}, u32[]{:S(2)}, u32[]{:S(2)}) %collective-permute-start.29) | collective-permute-done | bytes 315424 | tf_op jit(solution)/shard_map/ppermute | solution.py:657
  164.0 1.4 collective-permute-start.31
  165.4 2.6 %collective-permute-done.31.refs_3_ = s16[4,77,16,128]{3,2,1,0:T(8,128)(2,1)S(1)} collective-permute-done((s16[4,77,16,128]{3,2,1,0:T(8,128)(2,1)S(1)}, s16[4,77,16,128]{3,2,1,0:T(8,128)(2,1)S(1)}, u32[]{:S(2)}, u32[]{:S(2)}) %collective-permute-start.31) | collective-permute-done | bytes 1261600 | tf_op jit(solution)/shard_map/ppermute | solution.py:661
  168.0 1.5 hub_later.1.refs_5_
  169.8 1.3 collective-permute-start.37
  171.1 3.4 %plain_later.1.refs_3_ = bf16[14,128,256]{2,1,0:T(8,128)(2,1)S(1)} custom-call(s32[16]{0:T(128)S(1)} %copy-done.4, s32[72]{0:T(128)S(1)} %get-tuple-element.24.refs_1_.refs_0_, s16[4,77,16,128]{3,2,1,0:T(8,128)(2,1)S(1)} %pad_add_fusion.refs_2_, s16[4,77,16,128]{3,2,1,0:T(8,128)(2,1)S(1)} %collective-permute-done.31.refs_3_, ...), custom_call_target="tpu_custom_call" | custom-call | flops 536870912 | bytes 8388608 | tf_op jit(solution)/shard_map/plain_later/pallas_call | solution.py:420
  174.6 1.3 collective-permute-start.35
  176.4 2.9 %collective-permute-done.37 = bf16[256,256]{1,0:T(8,128)(2,1)S(1)} collective-permute-done((bf16[256,256]{1,0:T(8,128)(2,1)S(1)}, bf16[256,256]{1,0:T(8,128)(2,1)S(1)}, u32[]{:S(2)}, u32[]{:S(2)}) %collective-permute-start.37) | collective-permute-done | bytes 131104 | tf_op jit(solution)/shard_map/ppermute | solution.py:625
  179.4 1.8 collective-permute-start.41
  181.2 1.3 collective-permute-start.33
  182.5 4.0 %collective-permute-start.32 = (bf16[14,128,256]{2,1,0:T(8,128)(2,1)S(1)}, bf16[14,128,256]{2,1,0:T(8,128)(2,1)S(1)}, u32[]{:S(2)}, u32[]{:S(2)}) collective-permute-start(bf16[14,128,256]{2,1,0:T(8,128)(2,1)S(1)} %plain_later.1.refs_3_), channel_id=1, source_target_pairs={{0,8},{8,16},{16,24},{32,40},{40,48},{48,56},{64,72},{72,80},{80,8... | collective-permute-start | bytes 2752520 | tf_op jit(solution)/shard_map/ppermute | solution.py:619
  186.6 2.3 collective-permute-done.35
  189.6 2.9 %collective-permute-done.41.refs_9_ = bf16[4,256,256]{2,1,0:T(8,128)(2,1)S(1)} collective-permute-done((bf16[4,256,256]{2,1,0:T(8,128)(2,1)S(1)}, bf16[4,256,256]{2,1,0:T(8,128)(2,1)S(1)}, u32[]{:S(2)}, u32[]{:S(2)}) %collective-permute-start.41) | collective-permute-done | bytes 524320 | tf_op jit(solution)/shard_map/ppermute | solution.py:629
  192.5 3.3 %collective-permute-start.36 = (bf16[7,128,256]{2,1,0:T(8,128)(2,1)S(1)}, bf16[7,128,256]{2,1,0:T(8,128)(2,1)S(1)}, u32[]{:S(2)}, u32[]{:S(2)}) collective-permute-start(bf16[7,128,256]{2,1,0:T(8,128)(2,1)S(1)} %collective-permute-done.35), channel_id=1, source_target_pairs={{0,32},{56,24},{32,64},{88,56},{64,96},{120,88},{1,33},{57,25},{33... | collective-permute-start | bytes 1376264 | tf_op jit(solution)/shard_map/ppermute | solution.py:617
  195.8 4.2 %collective-permute-done.40.refs_8_ = bf16[4,256,256]{2,1,0:T(8,128)(2,1)S(1)} collective-permute-done((bf16[4,256,256]{2,1,0:T(8,128)(2,1)S(1)}, bf16[4,256,256]{2,1,0:T(8,128)(2,1)S(1)}, u32[]{:S(2)}, u32[]{:S(2)}) %collective-permute-start.40) | collective-permute-done | bytes 524320 | tf_op jit(solution)/shard_map/ppermute | solution.py:628
  200.2 6.7 %collective-permute-start.42 = (bf16[2,256,256]{2,1,0:T(8,128)(2,1)S(1)}, bf16[2,256,256]{2,1,0:T(8,128)(2,1)S(1)}, u32[]{:S(2)}, u32[]{:S(2)}) collective-permute-start(bf16[2,256,256]{2,1,0:T(8,128)(2,1)S(1)} %slice.83), channel_id=1, source_target_pairs={{0,32},{8,40},{16,48},{24,56},{32,64},{40,72},{48,80},{56,88},{64,... | collective-permute-start | bytes 786440 | tf_op jit(solution)/shard_map/ppermute | solution.py:631
  207.0 5.4 %collective-permute-done.42.refs_10_ = bf16[2,256,256]{2,1,0:T(8,128)(2,1)S(1)} collective-permute-done((bf16[2,256,256]{2,1,0:T(8,128)(2,1)S(1)}, bf16[2,256,256]{2,1,0:T(8,128)(2,1)S(1)}, u32[]{:S(2)}, u32[]{:S(2)}) %collective-permute-start.42) | collective-permute-done | bytes 262176 | tf_op jit(solution)/shard_map/ppermute | solution.py:631
  212.4 8.5 %gradient.3 = (f32[4,72,16,128]{3,2,1,0:T(8,128)S(1)}, f32[4,72,16,128]{3,2,1,0:T(8,128)S(1)}) custom-call(s32[72]{0:T(128)S(1)} %get-tuple-element.24.refs_1_.refs_0_, bf16[9472,256]{1,0:T(8,128)(2,1)S(1)} %get-tuple-element.25.refs_3_.refs_1_.refs_4_, bf16[14,128,256]{2,1,0:T(8,128)(2,1)S(1)} %collective-permute-done.32.refs_2_, ...), custom_call_target="tpu_custom_call" | custom-call | flops 1073741824 | bytes 16777216 | tf_op jit(solution)/shard_map/gradient/pallas_call | solution.py:491
  220.9 3.1 %collective-permute-start.44 = (f32[4,72,16,128]{3,2,1,0:T(8,128)S(1)}, f32[4,72,16,128]{3,2,1,0:T(8,128)S(1)}, u32[]{:S(2)}, u32[]{:S(2)}) collective-permute-start(f32[4,72,16,128]{3,2,1,0:T(8,128)S(1)} %get-tuple-element.36), channel_id=1, source_target_pairs={{0,1},{1,0},{2,3},{3,2},{4,5},{5,4},{6,7},{7,6},{8,9},{9,8},{10,11... | collective-permute-start | bytes 7077896 | tf_op jit(solution)/shard_map/ppermute | solution.py:670
  224.0 4.2 %collective-permute-done.44.other = f32[4,72,16,128]{3,2,1,0:T(8,128)S(1)} collective-permute-done((f32[4,72,16,128]{3,2,1,0:T(8,128)S(1)}, f32[4,72,16,128]{3,2,1,0:T(8,128)S(1)}, u32[]{:S(2)}, u32[]{:S(2)}) %collective-permute-start.44) | collective-permute-done | bytes 2359328 | tf_op jit(solution)/shard_map/ppermute | solution.py:670
  228.2 1.0 add_cores.3
  230.2 2.2 collective-permute-start.46
  232.9 6.2 %collective-permute-done.45.refs_3_ = s16[77,16,128]{2,1,0:T(8,128)(2,1)S(1)} collective-permute-done((s16[77,16,128]{2,1,0:T(8,128)(2,1)S(1)}, s16[77,16,128]{2,1,0:T(8,128)(2,1)S(1)}, u32[]{:S(2)}, u32[]{:S(2)}) %collective-permute-start.45) | collective-permute-done | bytes 315424 | tf_op jit(solution)/shard_map/ppermute | solution.py:674
  239.2 7.1 %collective-permute-done.46.refs_4_ = s16[77,16,128]{2,1,0:T(8,128)(2,1)S(1)} collective-permute-done((s16[77,16,128]{2,1,0:T(8,128)(2,1)S(1)}, s16[77,16,128]{2,1,0:T(8,128)(2,1)S(1)}, u32[]{:S(2)}, u32[]{:S(2)}) %collective-permute-start.46) | collective-permute-done | bytes 315424 | tf_op jit(solution)/shard_map/ppermute | solution.py:675
  246.3 2.2 prox_last.1
  (84 shorter events, 13.4 us)
Async XLA Ops:
  0.0 1.2 copy-start.2
  1.2 0.7 copy-start.3
  2.8 7.9 %collective-permute-start.2 = (bf16[272,256]{1,0:T(8,128)(2,1)S(1)}, bf16[272,256]{1,0:T(8,128)(2,1)S(1)}, u32[]{:S(2)}, u32[]{:S(2)}) collective-permute-start(bf16[272,256]{1,0:T(8,128)(2,1)S(1)} %pack_hub.1.refs_2_), channel_id=1, source_target_pairs={{0,16},{8,24},{16,0},{24,8},{32,48},{40,56},{48,32},{56,40},{64,80... | collective-permute-start | bytes 417800 | tf_op jit(solution)/shard_map/ppermute | solution.py:625
  7.3 6.9 %collective-permute-start.1 = (bf16[272,256]{1,0:T(8,128)(2,1)S(1)}, bf16[272,256]{1,0:T(8,128)(2,1)S(1)}, u32[]{:S(2)}, u32[]{:S(2)}) collective-permute-start(bf16[272,256]{1,0:T(8,128)(2,1)S(1)} %pack_hub.1.refs_2_), channel_id=1, source_target_pairs={{0,24},{8,0},{16,8},{24,16},{32,56},{40,32},{48,40},{56,48},{64,88... | collective-permute-start | bytes 417800 | tf_op jit(solution)/shard_map/ppermute | solution.py:625
  7.7 6.5 %collective-permute-start = (bf16[272,256]{1,0:T(8,128)(2,1)S(1)}, bf16[272,256]{1,0:T(8,128)(2,1)S(1)}, u32[]{:S(2)}, u32[]{:S(2)}) collective-permute-start(bf16[272,256]{1,0:T(8,128)(2,1)S(1)} %pack_hub.1.refs_2_), channel_id=1, source_target_pairs={{0,8},{8,16},{16,24},{24,0},{32,40},{40,48},{48,56},{56,32},{64,72... | collective-permute-start | bytes 417800 | tf_op jit(solution)/shard_map/ppermute | solution.py:625
  14.3 27.5 %copy-start.5 = (s32[16,8]{0,1:T(8,128)S(1)}, s32[16,8]{0,1:T(8,128)}, u32[]{:S(2)}) copy-start(s32[16,8]{0,1:T(8,128)} %param.6) | copy-start | bytes 1540
  14.3 41.4 %copy-start.4 = (s32[16]{0:T(128)S(1)}, s32[16]{0:T(128)}, u32[]{:S(2)}) copy-start(s32[16]{0:T(128)} %refs_0_.15) | copy-start | bytes 196
  14.3 13.0 %collective-permute-start.4 = (bf16[4,272,256]{2,1,0:T(8,128)(2,1)S(1)}, bf16[4,272,256]{2,1,0:T(8,128)(2,1)S(1)}, u32[]{:S(2)}, u32[]{:S(2)}) collective-permute-start(bf16[4,272,256]{2,1,0:T(8,128)(2,1)S(1)} %pad_maximum_fusion.refs_9_), channel_id=1, source_target_pairs={{0,96},{8,104},{16,112},{24,120},{32,0},{40,8},{48,16},{56,24},{64... | collective-permute-start | bytes 1671176 | tf_op jit(solution)/shard_map/ppermute | solution.py:629
  16.9 17.3 %collective-permute-start.3 = (bf16[4,272,256]{2,1,0:T(8,128)(2,1)S(1)}, bf16[4,272,256]{2,1,0:T(8,128)(2,1)S(1)}, u32[]{:S(2)}, u32[]{:S(2)}) collective-permute-start(bf16[4,272,256]{2,1,0:T(8,128)(2,1)S(1)} %pad_maximum_fusion.refs_9_), channel_id=1, source_target_pairs={{0,32},{8,40},{16,48},{24,56},{32,64},{40,72},{48,80},{56,88},{64,... | collective-permute-start | bytes 1671176 | tf_op jit(solution)/shard_map/ppermute | solution.py:628
  17.7 15.0 %collective-permute-start.10 = (bf16[7,128,256]{2,1,0:T(8,128)(2,1)S(1)}, bf16[7,128,256]{2,1,0:T(8,128)(2,1)}, u32[]{:S(2)}, u32[]{:S(2)}) collective-permute-start(bf16[7,128,256]{2,1,0:T(8,128)(2,1)S(1)} %get-tuple-element.45), channel_id=1, source_target_pairs={{24,0},{32,56},{56,32},{64,88},{88,64},{96,120},{25,1},{33,57},{57... | collective-permute-start | bytes 1376264 | tf_op jit(solution)/shard_map/ppermute | solution.py:616
  19.0 36.7 %collective-permute-start.8 = (bf16[14,128,256]{2,1,0:T(8,128)(2,1)S(1)}, bf16[14,128,256]{2,1,0:T(8,128)(2,1)S(1)}, u32[]{:S(2)}, u32[]{:S(2)}) collective-permute-start(bf16[14,128,256]{2,1,0:T(8,128)(2,1)S(1)} %pack_plain.1.refs_5_), channel_id=1, source_target_pairs={{8,0},{16,8},{24,16},{40,32},{48,40},{56,48},{72,64},{80,72},{88,8... | collective-permute-start | bytes 2752520 | tf_op jit(solution)/shard_map/ppermute | solution.py:620
  20.3 35.4 %collective-permute-start.7 = (bf16[14,128,256]{2,1,0:T(8,128)(2,1)S(1)}, bf16[14,128,256]{2,1,0:T(8,128)(2,1)}, u32[]{:S(2)}, u32[]{:S(2)}) collective-permute-start(bf16[14,128,256]{2,1,0:T(8,128)(2,1)S(1)} %pack_plain.1.refs_5_), channel_id=1, source_target_pairs={{0,8},{8,16},{16,24},{32,40},{40,48},{48,56},{64,72},{72,80},{80,8... | collective-permute-start | bytes 2752520 | tf_op jit(solution)/shard_map/ppermute | solution.py:619
  27.4 14.4 %collective-permute-start.6 = (bf16[2,272,256]{2,1,0:T(8,128)(2,1)S(1)}, bf16[2,272,256]{2,1,0:T(8,128)(2,1)}, u32[]{:S(2)}, u32[]{:S(2)}) collective-permute-start(bf16[2,272,256]{2,1,0:T(8,128)(2,1)S(1)} %slice.73), channel_id=1, source_target_pairs={{0,96},{8,104},{16,112},{24,120},{32,0},{40,8},{48,16},{56,24},{64... | collective-permute-start | bytes 835592 | tf_op jit(solution)/shard_map/ppermute | solution.py:632
  32.7 23.0 %collective-permute-start.9 = (bf16[7,128,256]{2,1,0:T(8,128)(2,1)}, bf16[7,128,256]{2,1,0:T(8,128)(2,1)}, u32[]{:S(2)}, u32[]{:S(2)}) collective-permute-start(bf16[7,128,256]{2,1,0:T(8,128)(2,1)} %get-tuple-element.46), channel_id=1, source_target_pairs={{24,32},{32,24},{56,64},{64,56},{88,96},{96,88},{25,33},{33,25},{5... | collective-permute-start | bytes 1376264 | tf_op jit(solution)/shard_map/ppermute | solution.py:615
  34.1 21.5 %collective-permute-start.11 = (bf16[7,128,256]{2,1,0:T(8,128)(2,1)}, bf16[7,128,256]{2,1,0:T(8,128)(2,1)}, u32[]{:S(2)}, u32[]{:S(2)}) collective-permute-start(bf16[7,128,256]{2,1,0:T(8,128)(2,1)} %collective-permute-done.10), channel_id=1, source_target_pairs={{0,32},{56,24},{32,64},{88,56},{64,96},{120,88},{1,33},{57,25},{33... | collective-permute-start | bytes 1376264 | tf_op jit(solution)/shard_map/ppermute | solution.py:617
  41.8 12.8 %collective-permute-start.5 = (bf16[2,272,256]{2,1,0:T(8,128)(2,1)}, bf16[2,272,256]{2,1,0:T(8,128)(2,1)}, u32[]{:S(2)}, u32[]{:S(2)}) collective-permute-start(bf16[2,272,256]{2,1,0:T(8,128)(2,1)} %slice.71), channel_id=1, source_target_pairs={{0,32},{8,40},{16,48},{24,56},{32,64},{40,72},{48,80},{56,88},{64,... | collective-permute-start | bytes 835592 | tf_op jit(solution)/shard_map/ppermute | solution.py:631
  55.7 3.4 %copy-start = (f32[16,8,128,128]{3,2,1,0:T(8,128)S(1)}, f32[16,8,128,128]{3,2,1,0:T(8,128)}, u32[]{:S(2)}) copy-start(f32[16,8,128,128]{3,2,1,0:T(8,128)} %refs_2_.1) | copy-start | bytes 25165828
  59.1 7.0 %copy-start.1 = (f32[16,8,128,128]{3,2,1,0:T(8,128)S(1)}, f32[16,8,128,128]{3,2,1,0:T(8,128)}, u32[]{:S(2)}) copy-start(f32[16,8,128,128]{3,2,1,0:T(8,128)} %refs_2_.1) | copy-start | bytes 25165828
  64.5 8.2 %collective-permute-start.19 = (bf16[256,256]{1,0:T(8,128)(2,1)S(1)}, bf16[256,256]{1,0:T(8,128)(2,1)S(1)}, u32[]{:S(2)}, u32[]{:S(2)}) collective-permute-start(bf16[256,256]{1,0:T(8,128)(2,1)S(1)} %get-tuple-element.26.refs_4_), channel_id=1, source_target_pairs={{0,16},{8,24},{16,0},{24,8},{32,48},{40,56},{48,32},{56,40},{64,80... | collective-permute-start | bytes 393224 | tf_op jit(solution)/shard_map/ppermute | solution.py:625
  64.6 8.2 %collective-permute-start.18 = (bf16[256,256]{1,0:T(8,128)(2,1)S(1)}, bf16[256,256]{1,0:T(8,128)(2,1)S(1)}, u32[]{:S(2)}, u32[]{:S(2)}) collective-permute-start(bf16[256,256]{1,0:T(8,128)(2,1)S(1)} %get-tuple-element.26.refs_4_), channel_id=1, source_target_pairs={{0,24},{8,0},{16,8},{24,16},{32,56},{40,32},{48,40},{56,48},{64,88... | collective-permute-start | bytes 393224 | tf_op jit(solution)/shard_map/ppermute | solution.py:625
  64.7 8.1 %collective-permute-start.17 = (bf16[256,256]{1,0:T(8,128)(2,1)S(1)}, bf16[256,256]{1,0:T(8,128)(2,1)S(1)}, u32[]{:S(2)}, u32[]{:S(2)}) collective-permute-start(bf16[256,256]{1,0:T(8,128)(2,1)S(1)} %get-tuple-element.26.refs_4_), channel_id=1, source_target_pairs={{0,8},{8,16},{16,24},{24,0},{32,40},{40,48},{48,56},{56,32},{64,72... | collective-permute-start | bytes 393224 | tf_op jit(solution)/shard_map/ppermute | solution.py:625
  71.4 11.9 %collective-permute-start.15 = (bf16[7,128,256]{2,1,0:T(8,128)(2,1)S(1)}, bf16[7,128,256]{2,1,0:T(8,128)(2,1)S(1)}, u32[]{:S(2)}, u32[]{:S(2)}) collective-permute-start(bf16[7,128,256]{2,1,0:T(8,128)(2,1)S(1)} %get-tuple-element.43), channel_id=1, source_target_pairs={{24,0},{32,56},{56,32},{64,88},{88,64},{96,120},{25,1},{33,57},{57... | collective-permute-start | bytes 1376264 | tf_op jit(solution)/shard_map/ppermute | solution.py:616
  72.8 13.4 %collective-permute-start.21 = (bf16[4,256,256]{2,1,0:T(8,128)(2,1)S(1)}, bf16[4,256,256]{2,1,0:T(8,128)(2,1)S(1)}, u32[]{:S(2)}, u32[]{:S(2)}) collective-permute-start(bf16[4,256,256]{2,1,0:T(8,128)(2,1)S(1)} %pad_maximum_fusion.1.refs_7_), channel_id=1, source_target_pairs={{0,96},{8,104},{16,112},{24,120},{32,0},{40,8},{48,16},{56,24},{64... | collective-permute-start | bytes 1572872 | tf_op jit(solution)/shard_map/ppermute | solution.py:629
  77.6 29.8 %collective-permute-start.13 = (bf16[14,128,256]{2,1,0:T(8,128)(2,1)S(1)}, bf16[14,128,256]{2,1,0:T(8,128)(2,1)S(1)}, u32[]{:S(2)}, u32[]{:S(2)}) collective-permute-start(bf16[14,128,256]{2,1,0:T(8,128)(2,1)S(1)} %plain_first.1.refs_3_), channel_id=1, source_target_pairs={{8,0},{16,8},{24,16},{40,32},{48,40},{56,48},{72,64},{80,72},{88,8... | collective-permute-start | bytes 2752520 | tf_op jit(solution)/shard_map/ppermute | solution.py:620
  78.9 28.5 %collective-permute-start.12 = (bf16[14,128,256]{2,1,0:T(8,128)(2,1)S(1)}, bf16[14,128,256]{2,1,0:T(8,128)(2,1)S(1)}, u32[]{:S(2)}, u32[]{:S(2)}) collective-permute-start(bf16[14,128,256]{2,1,0:T(8,128)(2,1)S(1)} %plain_first.1.refs_3_), channel_id=1, source_target_pairs={{0,8},{8,16},{16,24},{32,40},{40,48},{48,56},{64,72},{72,80},{80,8... | collective-permute-start | bytes 2752520 | tf_op jit(solution)/shard_map/ppermute | solution.py:619
  82.9 10.0 %collective-permute-start.20 = (bf16[4,256,256]{2,1,0:T(8,128)(2,1)S(1)}, bf16[4,256,256]{2,1,0:T(8,128)(2,1)S(1)}, u32[]{:S(2)}, u32[]{:S(2)}) collective-permute-start(bf16[4,256,256]{2,1,0:T(8,128)(2,1)S(1)} %pad_maximum_fusion.1.refs_7_), channel_id=1, source_target_pairs={{0,32},{8,40},{16,48},{24,56},{32,64},{40,72},{48,80},{56,88},{64,... | collective-permute-start | bytes 1572872 | tf_op jit(solution)/shard_map/ppermute | solution.py:628
  83.4 9.6 %collective-permute-start.14 = (bf16[7,128,256]{2,1,0:T(8,128)(2,1)S(1)}, bf16[7,128,256]{2,1,0:T(8,128)(2,1)S(1)}, u32[]{:S(2)}, u32[]{:S(2)}) collective-permute-start(bf16[7,128,256]{2,1,0:T(8,128)(2,1)S(1)} %get-tuple-element.44), channel_id=1, source_target_pairs={{24,32},{32,24},{56,64},{64,56},{88,96},{96,88},{25,33},{33,25},{5... | collective-permute-start | bytes 1376264 | tf_op jit(solution)/shard_map/ppermute | solution.py:615
  86.2 21.2 %collective-permute-start.16 = (bf16[7,128,256]{2,1,0:T(8,128)(2,1)S(1)}, bf16[7,128,256]{2,1,0:T(8,128)(2,1)S(1)}, u32[]{:S(2)}, u32[]{:S(2)}) collective-permute-start(bf16[7,128,256]{2,1,0:T(8,128)(2,1)S(1)} %collective-permute-done.15), channel_id=1, source_target_pairs={{0,32},{56,24},{32,64},{88,56},{64,96},{120,88},{1,33},{57,25},{33... | collective-permute-start | bytes 1376264 | tf_op jit(solution)/shard_map/ppermute | solution.py:617
  92.9 9.2 %collective-permute-start.23 = (bf16[2,256,256]{2,1,0:T(8,128)(2,1)S(1)}, bf16[2,256,256]{2,1,0:T(8,128)(2,1)S(1)}, u32[]{:S(2)}, u32[]{:S(2)}) collective-permute-start(bf16[2,256,256]{2,1,0:T(8,128)(2,1)S(1)} %slice.80), channel_id=1, source_target_pairs={{0,96},{8,104},{16,112},{24,120},{32,0},{40,8},{48,16},{56,24},{64... | collective-permute-start | bytes 786440 | tf_op jit(solution)/shard_map/ppermute | solution.py:632
  93.0 14.4 %collective-permute-start.22 = (bf16[2,256,256]{2,1,0:T(8,128)(2,1)S(1)}, bf16[2,256,256]{2,1,0:T(8,128)(2,1)S(1)}, u32[]{:S(2)}, u32[]{:S(2)}) collective-permute-start(bf16[2,256,256]{2,1,0:T(8,128)(2,1)S(1)} %slice.79), channel_id=1, source_target_pairs={{0,32},{8,40},{16,48},{24,56},{32,64},{40,72},{48,80},{56,88},{64,... | collective-permute-start | bytes 786440 | tf_op jit(solution)/shard_map/ppermute | solution.py:631
  115.9 9.6 %collective-permute-start.24 = (f32[4,72,16,128]{3,2,1,0:T(8,128)S(1)}, f32[4,72,16,128]{3,2,1,0:T(8,128)S(1)}, u32[]{:S(2)}, u32[]{:S(2)}) collective-permute-start(f32[4,72,16,128]{3,2,1,0:T(8,128)S(1)} %get-tuple-element.28), channel_id=1, source_target_pairs={{0,1},{1,0},{2,3},{3,2},{4,5},{5,4},{6,7},{7,6},{8,9},{9,8},{10,11... | collective-permute-start | bytes 7077896 | tf_op jit(solution)/shard_map/ppermute | solution.py:670
  126.6 10.0 %collective-permute-start.25 = (s16[77,16,128]{2,1,0:T(8,128)(2,1)S(1)}, s16[77,16,128]{2,1,0:T(8,128)(2,1)S(1)}, u32[]{:S(2)}, u32[]{:S(2)}) collective-permute-start(s16[77,16,128]{2,1,0:T(8,128)(2,1)S(1)} %get-tuple-element.30), channel_id=1, source_target_pairs={{0,2},{1,3},{2,4},{3,5},{4,6},{5,7},{6,0},{7,1},{8,10},{9,11},{10,... | collective-permute-start | bytes 946184 | tf_op jit(solution)/shard_map/ppermute | solution.py:674
  128.0 16.6 %collective-permute-start.26 = (s16[77,16,128]{2,1,0:T(8,128)(2,1)S(1)}, s16[77,16,128]{2,1,0:T(8,128)(2,1)S(1)}, u32[]{:S(2)}, u32[]{:S(2)}) collective-permute-start(s16[77,16,128]{2,1,0:T(8,128)(2,1)S(1)} %get-tuple-element.31), channel_id=1, source_target_pairs={{0,4},{1,5},{2,6},{3,7},{4,0},{5,1},{6,2},{7,3},{8,12},{9,13},{10,... | collective-permute-start | bytes 946184 | tf_op jit(solution)/shard_map/ppermute | solution.py:675
  130.6 13.9 %collective-permute-start.27 = (s16[77,16,128]{2,1,0:T(8,128)(2,1)S(1)}, s16[77,16,128]{2,1,0:T(8,128)(2,1)S(1)}, u32[]{:S(2)}, u32[]{:S(2)}) collective-permute-start(s16[77,16,128]{2,1,0:T(8,128)(2,1)S(1)} %get-tuple-element.32), channel_id=1, source_target_pairs={{0,6},{1,7},{2,0},{3,1},{4,2},{5,3},{6,4},{7,5},{8,14},{9,15},{10,... | collective-permute-start | bytes 946184 | tf_op jit(solution)/shard_map/ppermute | solution.py:676
  146.0 9.1 %collective-permute-start.30 = (s16[77,16,128]{2,1,0:T(8,128)(2,1)S(1)}, s16[77,16,128]{2,1,0:T(8,128)(2,1)S(1)}, u32[]{:S(2)}, u32[]{:S(2)}) collective-permute-start(s16[77,16,128]{2,1,0:T(8,128)(2,1)S(1)} %get-tuple-element.34), channel_id=1, source_target_pairs={{0,2},{1,3},{2,4},{3,5},{4,6},{5,7},{6,0},{7,1},{8,10},{9,11},{10,... | collective-permute-start | bytes 946184 | tf_op jit(solution)/shard_map/ppermute | solution.py:658
  147.1 16.6 %collective-permute-start.29 = (s16[77,16,128]{2,1,0:T(8,128)(2,1)S(1)}, s16[77,16,128]{2,1,0:T(8,128)(2,1)S(1)}, u32[]{:S(2)}, u32[]{:S(2)}) collective-permute-start(s16[77,16,128]{2,1,0:T(8,128)(2,1)S(1)} %get-tuple-element.34), channel_id=1, source_target_pairs={{0,4},{1,5},{2,6},{3,7},{4,0},{5,1},{6,2},{7,3},{8,12},{9,13},{10,... | collective-permute-start | bytes 946184 | tf_op jit(solution)/shard_map/ppermute | solution.py:657
  149.9 13.8 %collective-permute-start.28 = (s16[77,16,128]{2,1,0:T(8,128)(2,1)S(1)}, s16[77,16,128]{2,1,0:T(8,128)(2,1)S(1)}, u32[]{:S(2)}, u32[]{:S(2)}) collective-permute-start(s16[77,16,128]{2,1,0:T(8,128)(2,1)S(1)} %get-tuple-element.34), channel_id=1, source_target_pairs={{0,6},{1,7},{2,0},{3,1},{4,2},{5,3},{6,4},{7,5},{8,14},{9,15},{10,... | collective-permute-start | bytes 946184 | tf_op jit(solution)/shard_map/ppermute | solution.py:656
  164.0 4.0 %collective-permute-start.31 = (s16[4,77,16,128]{3,2,1,0:T(8,128)(2,1)S(1)}, s16[4,77,16,128]{3,2,1,0:T(8,128)(2,1)S(1)}, u32[]{:S(2)}, u32[]{:S(2)}) collective-permute-start(s16[4,77,16,128]{3,2,1,0:T(8,128)(2,1)S(1)} %pad_add_fusion.refs_2_), channel_id=1, source_target_pairs={{0,1},{1,0},{2,3},{3,2},{4,5},{5,4},{6,7},{7,6},{8,9},{9,8},{10,11... | collective-permute-start | bytes 3784712 | tf_op jit(solution)/shard_map/ppermute | solution.py:661
  169.5 6.4 %collective-permute-start.39 = (bf16[256,256]{1,0:T(8,128)(2,1)S(1)}, bf16[256,256]{1,0:T(8,128)(2,1)S(1)}, u32[]{:S(2)}, u32[]{:S(2)}) collective-permute-start(bf16[256,256]{1,0:T(8,128)(2,1)S(1)} %hub_later.1.refs_5_), channel_id=1, source_target_pairs={{0,16},{8,24},{16,0},{24,8},{32,48},{40,56},{48,32},{56,40},{64,80... | collective-permute-start | bytes 393224 | tf_op jit(solution)/shard_map/ppermute | solution.py:625
  169.6 6.8 %collective-permute-start.38 = (bf16[256,256]{1,0:T(8,128)(2,1)S(1)}, bf16[256,256]{1,0:T(8,128)(2,1)S(1)}, u32[]{:S(2)}, u32[]{:S(2)}) collective-permute-start(bf16[256,256]{1,0:T(8,128)(2,1)S(1)} %hub_later.1.refs_5_), channel_id=1, source_target_pairs={{0,24},{8,0},{16,8},{24,16},{32,56},{40,32},{48,40},{56,48},{64,88... | collective-permute-start | bytes 393224 | tf_op jit(solution)/shard_map/ppermute | solution.py:625
  169.8 9.5 %collective-permute-start.37 = (bf16[256,256]{1,0:T(8,128)(2,1)S(1)}, bf16[256,256]{1,0:T(8,128)(2,1)S(1)}, u32[]{:S(2)}, u32[]{:S(2)}) collective-permute-start(bf16[256,256]{1,0:T(8,128)(2,1)S(1)} %hub_later.1.refs_5_), channel_id=1, source_target_pairs={{0,8},{8,16},{16,24},{24,0},{32,40},{40,48},{48,56},{56,32},{64,72... | collective-permute-start | bytes 393224 | tf_op jit(solution)/shard_map/ppermute | solution.py:625
  174.6 14.2 %collective-permute-start.35 = (bf16[7,128,256]{2,1,0:T(8,128)(2,1)S(1)}, bf16[7,128,256]{2,1,0:T(8,128)(2,1)S(1)}, u32[]{:S(2)}, u32[]{:S(2)}) collective-permute-start(bf16[7,128,256]{2,1,0:T(8,128)(2,1)S(1)} %get-tuple-element.41), channel_id=1, source_target_pairs={{24,0},{32,56},{56,32},{64,88},{88,64},{96,120},{25,1},{33,57},{57... | collective-permute-start | bytes 1376264 | tf_op jit(solution)/shard_map/ppermute | solution.py:616
  179.4 13.1 %collective-permute-start.41 = (bf16[4,256,256]{2,1,0:T(8,128)(2,1)S(1)}, bf16[4,256,256]{2,1,0:T(8,128)(2,1)S(1)}, u32[]{:S(2)}, u32[]{:S(2)}) collective-permute-start(bf16[4,256,256]{2,1,0:T(8,128)(2,1)S(1)} %pad_maximum_fusion.2.refs_7_), channel_id=1, source_target_pairs={{0,96},{8,104},{16,112},{24,120},{32,0},{40,8},{48,16},{56,24},{64... | collective-permute-start | bytes 1572872 | tf_op jit(solution)/shard_map/ppermute | solution.py:629
  181.2 31.2 %collective-permute-start.33 = (bf16[14,128,256]{2,1,0:T(8,128)(2,1)S(1)}, bf16[14,128,256]{2,1,0:T(8,128)(2,1)S(1)}, u32[]{:S(2)}, u32[]{:S(2)}) collective-permute-start(bf16[14,128,256]{2,1,0:T(8,128)(2,1)S(1)} %plain_later.1.refs_3_), channel_id=1, source_target_pairs={{8,0},{16,8},{24,16},{40,32},{48,40},{56,48},{72,64},{80,72},{88,8... | collective-permute-start | bytes 2752520 | tf_op jit(solution)/shard_map/ppermute | solution.py:620
  182.5 29.9 %collective-permute-start.32 = (bf16[14,128,256]{2,1,0:T(8,128)(2,1)S(1)}, bf16[14,128,256]{2,1,0:T(8,128)(2,1)S(1)}, u32[]{:S(2)}, u32[]{:S(2)}) collective-permute-start(bf16[14,128,256]{2,1,0:T(8,128)(2,1)S(1)} %plain_later.1.refs_3_), channel_id=1, source_target_pairs={{0,8},{8,16},{16,24},{32,40},{40,48},{48,56},{64,72},{72,80},{80,8... | collective-permute-start | bytes 2752520 | tf_op jit(solution)/shard_map/ppermute | solution.py:619
  186.5 13.4 %collective-permute-start.40 = (bf16[4,256,256]{2,1,0:T(8,128)(2,1)S(1)}, bf16[4,256,256]{2,1,0:T(8,128)(2,1)S(1)}, u32[]{:S(2)}, u32[]{:S(2)}) collective-permute-start(bf16[4,256,256]{2,1,0:T(8,128)(2,1)S(1)} %pad_maximum_fusion.2.refs_7_), channel_id=1, source_target_pairs={{0,32},{8,40},{16,48},{24,56},{32,64},{40,72},{48,80},{56,88},{64,... | collective-permute-start | bytes 1572872 | tf_op jit(solution)/shard_map/ppermute | solution.py:628
  188.9 11.3 %collective-permute-start.34 = (bf16[7,128,256]{2,1,0:T(8,128)(2,1)S(1)}, bf16[7,128,256]{2,1,0:T(8,128)(2,1)S(1)}, u32[]{:S(2)}, u32[]{:S(2)}) collective-permute-start(bf16[7,128,256]{2,1,0:T(8,128)(2,1)S(1)} %get-tuple-element.42), channel_id=1, source_target_pairs={{24,32},{32,24},{56,64},{64,56},{88,96},{96,88},{25,33},{33,25},{5... | collective-permute-start | bytes 1376264 | tf_op jit(solution)/shard_map/ppermute | solution.py:615
  192.5 19.9 %collective-permute-start.36 = (bf16[7,128,256]{2,1,0:T(8,128)(2,1)S(1)}, bf16[7,128,256]{2,1,0:T(8,128)(2,1)S(1)}, u32[]{:S(2)}, u32[]{:S(2)}) collective-permute-start(bf16[7,128,256]{2,1,0:T(8,128)(2,1)S(1)} %collective-permute-done.35), channel_id=1, source_target_pairs={{0,32},{56,24},{32,64},{88,56},{64,96},{120,88},{1,33},{57,25},{33... | collective-permute-start | bytes 1376264 | tf_op jit(solution)/shard_map/ppermute | solution.py:617
  200.0 7.0 %collective-permute-start.43 = (bf16[2,256,256]{2,1,0:T(8,128)(2,1)S(1)}, bf16[2,256,256]{2,1,0:T(8,128)(2,1)S(1)}, u32[]{:S(2)}, u32[]{:S(2)}) collective-permute-start(bf16[2,256,256]{2,1,0:T(8,128)(2,1)S(1)} %slice.84), channel_id=1, source_target_pairs={{0,96},{8,104},{16,112},{24,120},{32,0},{40,8},{48,16},{56,24},{64... | collective-permute-start | bytes 786440 | tf_op jit(solution)/shard_map/ppermute | solution.py:632
  200.2 12.1 %collective-permute-start.42 = (bf16[2,256,256]{2,1,0:T(8,128)(2,1)S(1)}, bf16[2,256,256]{2,1,0:T(8,128)(2,1)S(1)}, u32[]{:S(2)}, u32[]{:S(2)}) collective-permute-start(bf16[2,256,256]{2,1,0:T(8,128)(2,1)S(1)} %slice.83), channel_id=1, source_target_pairs={{0,32},{8,40},{16,48},{24,56},{32,64},{40,72},{48,80},{56,88},{64,... | collective-permute-start | bytes 786440 | tf_op jit(solution)/shard_map/ppermute | solution.py:631
  220.9 7.3 %collective-permute-start.44 = (f32[4,72,16,128]{3,2,1,0:T(8,128)S(1)}, f32[4,72,16,128]{3,2,1,0:T(8,128)S(1)}, u32[]{:S(2)}, u32[]{:S(2)}) collective-permute-start(f32[4,72,16,128]{3,2,1,0:T(8,128)S(1)} %get-tuple-element.36), channel_id=1, source_target_pairs={{0,1},{1,0},{2,3},{3,2},{4,5},{5,4},{6,7},{7,6},{8,9},{9,8},{10,11... | collective-permute-start | bytes 7077896 | tf_op jit(solution)/shard_map/ppermute | solution.py:670
  229.3 9.9 %collective-permute-start.45 = (s16[77,16,128]{2,1,0:T(8,128)(2,1)S(1)}, s16[77,16,128]{2,1,0:T(8,128)(2,1)S(1)}, u32[]{:S(2)}, u32[]{:S(2)}) collective-permute-start(s16[77,16,128]{2,1,0:T(8,128)(2,1)S(1)} %get-tuple-element.38), channel_id=1, source_target_pairs={{0,2},{1,3},{2,4},{3,5},{4,6},{5,7},{6,0},{7,1},{8,10},{9,11},{10,... | collective-permute-start | bytes 946184 | tf_op jit(solution)/shard_map/ppermute | solution.py:674
  230.2 16.1 %collective-permute-start.46 = (s16[77,16,128]{2,1,0:T(8,128)(2,1)S(1)}, s16[77,16,128]{2,1,0:T(8,128)(2,1)S(1)}, u32[]{:S(2)}, u32[]{:S(2)}) collective-permute-start(s16[77,16,128]{2,1,0:T(8,128)(2,1)S(1)} %get-tuple-element.39), channel_id=1, source_target_pairs={{0,4},{1,5},{2,6},{3,7},{4,0},{5,1},{6,2},{7,3},{8,12},{9,13},{10,... | collective-permute-start | bytes 946184 | tf_op jit(solution)/shard_map/ppermute | solution.py:675
  232.4 13.9 %collective-permute-start.47 = (s16[77,16,128]{2,1,0:T(8,128)(2,1)S(1)}, s16[77,16,128]{2,1,0:T(8,128)(2,1)S(1)}, u32[]{:S(2)}, u32[]{:S(2)}) collective-permute-start(s16[77,16,128]{2,1,0:T(8,128)(2,1)S(1)} %get-tuple-element.40), channel_id=1, source_target_pairs={{0,6},{1,7},{2,0},{3,1},{4,2},{5,3},{6,4},{7,5},{8,14},{9,15},{10,... | collective-permute-start | bytes 946184 | tf_op jit(solution)/shard_map/ppermute | solution.py:676

commit v2 on v1

--- a/solution.py
+++ b/solution.py
@@ -194,8 +194,8 @@
             lookup[slot_base(p, slots) + k] = jnp.clip(c, 0, total - 1)
 
 
-def image_group(tile_of, blocks_of, live, bs):
-    high, low, blocks = [], [], []
+def halves(tile_of, live):
+    high, low = [], []
     for k in range(GROUP):
         tile = tile_of(k)
         if live is not None:
@@ -203,74 +203,109 @@
         top = tile.astype(BF)
         high.append(top)
         low.append((tile - top.astype(F32)).astype(BF))
-        blocks.append(blocks_of(k))
-    left = jnp.concatenate([jnp.concatenate(high, axis=1), jnp.concatenate(low, axis=1)], axis=0)
+    return jnp.concatenate([jnp.concatenate(high, axis=1), jnp.concatenate(low, axis=1)], axis=0)
+
+
+def image_group(left, lookup, table, start, bs):
+    blocks = [table[aligned(lookup[start + k], bs), :] for k in range(GROUP)]
     both = jnp.dot(left, jnp.concatenate(blocks, axis=0), preferred_element_type=F32)
     return both[:bs] + both[bs:]
 
 
-def hub_images(tile_of, lookup, table, out, slots, bs):
+def hub_images(left_of, lookup, table, out, slots, bs):
     for p in range(HUB_DEV):
         total = None
         for start in range(p * slots, (p + 1) * slots, GROUP):
-            part = image_group(
-                lambda k: tile_of(start + k),
-                lambda k: table[aligned(lookup[start + k], bs), :],
-                None,
-                bs,
-            )
+            part = image_group(left_of(start // GROUP), lookup, table, start, bs)
             total = part if total is None else total + part
         out[p * bs : (p + 1) * bs, :] = total.astype(BF)
 
 
-def plain_images(counts, order, ready, tile_of, lookup, table, out, slots, bs):
+def plain_images(left_of, lookup, table, out, slots, bs):
+    first = HUB_DEV * slots
+
     def one(p, _):
-        ready(p)
-        start = HUB_DEV * slots + p * HALF
-        image = image_group(
-            lambda k: tile_of(p * HALF + k),
-            lambda k: table[aligned(lookup[start + k], bs), :],
-            counts[order[HUB_DEV + p]],
-            bs,
-        )
-        out[p] = image.astype(BF)
+        left = left_of(p)
+        out[p] = image_group(left, lookup, table, first + p * HALF, bs).astype(BF)
         return 0
 
     lax.fori_loop(0, out.shape[0], one, 0, unroll=2)
 
 
-def first_hub_kernel(*refs):
-    counts, pattern, ids, omega = refs[:4]
-    near, hubs = refs[4:9], refs[9:14]
-    out, lookup, table, rows_out = refs[14:18]
-    order, inverse, tiles, table_sem, tile_sem = refs[18:]
-    rows, slots = pattern.shape
-    bs, share = tiles.shape[1], rows_out.shape[1]
+def prep_kernel(counts, omega, left_hub, left, rows_out, order, tiles, part_sem, sems):
+    rows, slots, _, _ = omega.shape
+    share = rows_out.shape[1]
     row_order(counts, order, slots)
-    gather = Gather(near, hubs, table, table_sem, bs)
-    gather.start()
     part = aligned(lax.axis_index("samp"), share)
-    moves = []
+    whole, parts = [], []
     for p in range(rows):
         n = slots if p < HUB_DEV else HALF
         at = pl.ds(slot_base(p, slots), n)
-        moves.append(
-            pltpu.make_async_copy(omega.at[order[p], pl.ds(0, n), part], rows_out.at[at], tile_sem)
+        whole.append(
+            pltpu.make_async_copy(omega.at[order[p], pl.ds(0, n)], tiles.at[at], sems.at[p])
         )
-        if p < HUB_DEV:
-            moves.append(pltpu.make_async_copy(omega.at[order[p]], tiles.at[at], tile_sem))
-    for move in moves:
+        parts.append(
+            pltpu.make_async_copy(omega.at[order[p], pl.ds(0, n), part], rows_out.at[at], part_sem)
+        )
+    for move in whole + parts:
         move.start()
-    fill_lookup(pattern, ids, order, inverse, lookup)
-    for move in moves:
+    for p in range(rows):
+        whole[p].wait()
+        start = slot_base(p, slots)
+        live = None if p < HUB_DEV else counts[order[p]]
+        for s in range(start, start + (slots if p < HUB_DEV else HALF), GROUP):
+            g = s // GROUP
+            if p < HUB_DEV:
+                left_hub[g] = halves(lambda k: tiles[s + k], live)
+            else:
+                left[g - left_hub.shape[0]] = halves(lambda k: tiles[s + k], live)
+    for move in parts:
         move.wait()
-    gather.wait()
-    hub_images(lambda s: tiles[s], lookup, table, out, slots, bs)
-
-
-def first_hub(counts, pattern, ids, omega, near, hubs, part_count):
+
+
+def prep(counts, omega, part_count):
     rows, slots, bs, _ = omega.shape
     total = HUB_DEV * slots + (rows - HUB_DEV) * HALF
+    return pl.pallas_call(
+        prep_kernel,
+        out_shape=(
+            jax.ShapeDtypeStruct((HUB_DEV * slots // GROUP, 2 * bs, GROUP * bs), BF),
+            jax.ShapeDtypeStruct((rows - HUB_DEV, 2 * bs, GROUP * bs), BF),
+            jax.ShapeDtypeStruct((total, bs // part_count, bs), F32),
+        ),
+        in_specs=[SMEM, ANY],
+        out_specs=(VMEM, VMEM, VMEM),
+        scratch_shapes=[
+            pltpu.SMEM((rows,), jnp.int32),
+            pltpu.VMEM((total, bs, bs), F32),
+            pltpu.SemaphoreType.DMA,
+            pltpu.SemaphoreType.DMA((rows,)),
+        ],
+        compiler_params=grant(48),
+        cost_estimate=cost(1 << 24, 12 << 20),
+        name="prep",
+    )(counts, omega)
+
+
+def first_hub_kernel(*refs):
+    counts, pattern, ids, left = refs[:4]
+    near, hubs = refs[4:9], refs[9:14]
+    out, lookup, table = refs[14:17]
+    order, inverse, sem = refs[17:]
+    slots = pattern.shape[1]
+    bs = left.shape[1] // 2
+    row_order(counts, order, slots)
+    gather = Gather(near, hubs, table, sem, bs)
+    gather.start()
+    fill_lookup(pattern, ids, order, inverse, lookup)
+    gather.wait()
+    hub_images(lambda g: left[g], lookup, table, out, slots, bs)
+
+
+def first_hub(counts, pattern, ids, left, near, hubs):
+    rows, slots = pattern.shape
+    total = HUB_DEV * slots + (rows - HUB_DEV) * HALF
+    bs = left.shape[1] // 2
     local = hubs[0].shape[2]
     table = (3 * (rows - HUB_DEV) + SIDE * SIDE * HUB_DEV) * bs
     return pl.pallas_call(
@@ -279,58 +314,37 @@
             jax.ShapeDtypeStruct((HUB_DEV * bs, local), BF),
             jax.ShapeDtypeStruct((total,), jnp.int32),
             jax.ShapeDtypeStruct((table, local), BF),
-            jax.ShapeDtypeStruct((total, bs // part_count, bs), F32),
         ),
-        in_specs=[SMEM, SMEM, SMEM] + [ANY] * 11,
-        out_specs=(VMEM, SMEM, VMEM, VMEM),
+        in_specs=[SMEM, SMEM, SMEM, VMEM] + [ANY] * 10,
+        out_specs=(VMEM, SMEM, VMEM),
         scratch_shapes=[
             pltpu.SMEM((rows,), jnp.int32),
             pltpu.SMEM((rows * (SIDE * SIDE + 2),), jnp.int32),
-            pltpu.VMEM((HUB_DEV * slots, bs, bs), F32),
-            pltpu.SemaphoreType.DMA,
             pltpu.SemaphoreType.DMA,
         ],
-        compiler_params=grant(16),
+        compiler_params=grant(12),
         cost_estimate=cost(1 << 28, 12 << 20),
         name="hub_first",
-    )(counts, pattern, ids, omega, *near, *hubs)
-
-
-def first_plain_kernel(slots, *refs):
-    counts, lookup, omega, table, _, out = refs[:6]
-    order, tiles, sems = refs[6:]
-    bs = tiles.shape[1]
-    row_order(counts, order, slots)
-
-    def move(p):
-        return pltpu.make_async_copy(
-            omega.at[order[HUB_DEV + p], pl.ds(0, HALF)], tiles.at[pl.ds(p * HALF, HALF)], sems.at[p]
-        )
-
-    for p in range(out.shape[0]):
-        move(p).start()
-    plain_images(
-        counts, order, lambda p: move(p).wait(), lambda s: tiles[s], lookup, table, out, slots, bs
-    )
-
-
-def first_plain(counts, lookup, omega, table, after):
-    rows, slots, bs, _ = omega.shape
-    plain = rows - HUB_DEV
+    )(counts, pattern, ids, left, *near, *hubs)
+
+
+def first_plain_kernel(slots, lookup, left, table, _, out):
+    bs = out.shape[1]
+    plain_images(lambda p: left[p], lookup, table, out, slots, bs)
+
+
+def first_plain(lookup, left, table, slots, after):
+    bs = left.shape[1] // 2
+    plain = (lookup.shape[0] - HUB_DEV * slots) // HALF
     return pl.pallas_call(
         lambda *refs: first_plain_kernel(slots, *refs),
         out_shape=jax.ShapeDtypeStruct((plain, bs, table.shape[1]), BF),
-        in_specs=[SMEM, SMEM, ANY, VMEM, ANY],
+        in_specs=[SMEM, VMEM, VMEM, ANY],
         out_specs=VMEM,
-        scratch_shapes=[
-            pltpu.SMEM((rows,), jnp.int32),
-            pltpu.VMEM((plain * HALF, bs, bs), F32),
-            pltpu.SemaphoreType.DMA((plain,)),
-        ],
-        compiler_params=grant(16),
+        compiler_params=grant(12),
         cost_estimate=cost(1 << 29, 10 << 20),
         name="plain_first",
-    )(counts, lookup, omega, table, after)
+    )(lookup, left, table, after)
 
 
 def wire_scales(tail, scales):
@@ -402,10 +416,17 @@
         return jnp.concatenate(rows, axis=0)
 
     if hub:
-        hub_images(tile_of, lookup, table, out, slots, bs)
+        hub_images(
+            lambda g: halves(lambda k: tile_of(g * GROUP + k), None), lookup, table, out, slots, bs
+        )
     else:
         plain_images(
-            counts, order, lambda p: None, tile_of, lookup, table, out, slots, bs
+            lambda p: halves(lambda k: tile_of(p * HALF + k), counts[order[HUB_DEV + p]]),
+            lookup,
+            table,
+            out,
+            slots,
+            bs,
         )
 
 
@@ -437,10 +458,57 @@
     )(counts, lookup, mine, partner, table, counts if hub else after)
 
 
+def groups(slots, plain, term):
+    for p in range(HUB_DEV):
+        for start in range(p * slots, (p + 1) * slots, GROUP):
+            term(start, 3 * plain + p)
+
+    def step(p, _):
+        term(HUB_DEV * slots + p * HALF, plain + p)
+        return 0
+
+    lax.fori_loop(0, plain, step, 0, unroll=2)
+
+
+def product(own, lookup, table, start, bs):
+    right = [table[aligned(lookup[start + k], bs), :] for k in range(GROUP)]
+    return lax.dot_general(
+        own, jnp.concatenate(right, axis=0), (((1,), (1,)), ((), ())), preferred_element_type=F32
+    )
+
+
+def firsts_kernel(slots, lookup, x_table, m_own, m_hub, out):
+    plain, bs, _ = m_own.shape
+    for p in range(HUB_DEV):
+        for start in range(p * slots, (p + 1) * slots, GROUP):
+            own = m_hub[p * bs : (p + 1) * bs, :]
+            out[start // GROUP] = product(own, lookup, x_table, start, bs)
+
+    def step(p, _):
+        start = HUB_DEV * slots + p * HALF
+        out[HUB_DEV * slots // GROUP + p] = product(m_own[p], lookup, x_table, start, bs)
+        return 0
+
+    lax.fori_loop(0, plain, step, 0, unroll=2)
+
+
+def first_terms(lookup, table, m_own, m_hub, slots):
+    bs = m_own.shape[1]
+    return pl.pallas_call(
+        lambda *refs: firsts_kernel(slots, *refs),
+        out_shape=jax.ShapeDtypeStruct((lookup.shape[0] // GROUP, bs, GROUP * bs), F32),
+        in_specs=[SMEM, VMEM, VMEM, VMEM],
+        out_specs=VMEM,
+        compiler_params=grant(12),
+        cost_estimate=cost(1 << 29, 10 << 20),
+        name="firsts",
+    )(lookup, table, m_own, m_hub)
+
+
 def gradient_kernel(scale, slots, *refs):
-    lookup, x_table = refs[:2]
-    near, hubs = refs[2:7], refs[7:12]
-    keep, send, m_table, sem = refs[12:]
+    lookup, x_table, firsts = refs[:3]
+    near, hubs = refs[3:8], refs[8:13]
+    keep, send, m_table, sem = refs[13:]
     plain, bs, _ = near[1].shape
     gather = Gather(near, hubs, m_table, sem, bs)
     gather.start()
@@ -450,19 +518,8 @@
     share = keep.shape[2]
 
     def group(start, own):
-        mine = aligned(own, bs)
-        left = jnp.concatenate([m_table[mine, :], x_table[mine, :]], axis=1)
-        right = []
-        for k in range(GROUP):
-            at = aligned(lookup[start + k], bs)
-            right.append(jnp.concatenate([x_table[at, :], m_table[at, :]], axis=1))
-        both = lax.dot_general(
-            left,
-            jnp.concatenate(right, axis=0),
-            (((1,), (1,)), ((), ())),
-            preferred_element_type=F32,
-        )
-        both = both * scale
+        term = product(x_table[aligned(own, bs), :], lookup, m_table, start, bs)
+        both = (firsts[start // GROUP] + term) * scale
         for k in range(GROUP):
             tile = both[:, k * bs : (k + 1) * bs].reshape(SIDE, CORES, share, bs)
             even, odd = tile[:, 0], tile[:, 1]
@@ -473,31 +530,23 @@
                 keep[to, start + k] = stay[g]
                 send[to, start + k] = leave[g]
 
-    for p in range(HUB_DEV):
-        for start in range(p * slots, (p + 1) * slots, GROUP):
-            group(start, 3 * plain + p)
-
-    def step(p, _):
-        group(HUB_DEV * slots + p * HALF, plain + p)
-        return 0
-
-    lax.fori_loop(0, plain, step, 0, unroll=2)
-
-
-def gradient(lookup, table, near, hubs, scale, slots, part_count):
+    groups(slots, plain, group)
+
+
+def gradient(lookup, table, firsts, near, hubs, scale, slots, part_count):
     total = lookup.shape[0]
-    bs = near[0].shape[1]
+    bs = firsts.shape[1]
     shape = jax.ShapeDtypeStruct((SIDE, total, bs // part_count, bs), F32)
     return pl.pallas_call(
         lambda *refs: gradient_kernel(scale, slots, *refs),
         out_shape=(shape, shape),
-        in_specs=[SMEM, VMEM] + [ANY] * 10,
+        in_specs=[SMEM, VMEM, VMEM] + [ANY] * 10,
         out_specs=(VMEM, VMEM),
         scratch_shapes=[pltpu.VMEM(table.shape, BF), pltpu.SemaphoreType.DMA],
-        compiler_params=grant(24),
+        compiler_params=grant(20),
         cost_estimate=cost(1 << 30, 16 << 20),
         name="gradient",
-    )(lookup, table, *near, *hubs)
+    )(lookup, table, firsts, *near, *hubs)
 
 
 def add_kernel(keep, other, own, *refs):
@@ -642,13 +691,12 @@
     x_hubs = share_hubs(x_hub)
     x_own = pack_plain(data, counts, slots, bs, x_hub)
     x_near = share_near(x_own)
+    left_hub, left, tiles = prep(counts, omega, parts)
     ids = jnp.concatenate([g[:, HUB_DEV * bs : HUB_DEV * bs + HUB_DEV, 0] for g in x_hubs])
     ids = ids.reshape(-1).astype(jnp.int32)
     for iteration in range(ITERS):
         if iteration == 0:
-            m_hub, lookup, table, tiles = first_hub(
-                counts, pattern, ids, omega, x_near, x_hubs, parts
-            )
+            m_hub, lookup, table = first_hub(counts, pattern, ids, left_hub, x_near, x_hubs)
         else:
             mine = jnp.stack(
                 [
@@ -662,11 +710,12 @@
             m_hub = later_image(counts, lookup, mine, partner, table, slots, None)
         m_hubs = share_hubs(m_hub)
         if iteration == 0:
-            m_own = first_plain(counts, lookup, omega, table, m_hub)
+            m_own = first_plain(lookup, left, table, slots, m_hub)
         else:
             m_own = later_image(counts, lookup, mine, partner, table, slots, m_hub)
         m_near = share_near(m_own)
-        keep, leave = gradient(lookup, table, m_near, m_hubs, scale, slots, parts)
+        firsts = first_terms(lookup, table, m_own, m_hub, slots)
+        keep, leave = gradient(lookup, table, firsts, m_near, m_hubs, scale, slots, parts)
         other = lax.ppermute(leave, "samp", samp_shift(0, 1))
         own, up, across, down = add_cores(keep, other)
         terms = (

time: 249 us -> 241 us (0.968)
  waiting for transfers between devices: 98 us -> 85.4 us
  Pallas kernels: 40.5 us -> 44.7 us
    ppermute x3, waiting for transfers between devices: 22.2 us -> 8.75 us  [share_hubs(): lax.ppermute(ahead[:half], 'var', var_shift(1, 0))]
    pallas_call x0 -> x3, Pallas kernels: none -> 9.79 us  [the longest x2 6.39 us: first_terms(): pl.pallas_call(lambda *refs: firsts_kernel(slots, *refs), out_shape=jax.S...]
    pallas_call x2, Pallas kernels: 17.1 us -> 14.1 us  [gradient(): pl.pallas_call(lambda *refs: gradient_kernel(scale, slots, *refs), out_sh...]
    pallas_call x1, Pallas kernels: 5.22 us -> 2.67 us  [first_plain(): pl.pallas_call(lambda *refs: first_plain_kernel(slots, *refs), out_shape=...]
    unnamed x13 -> x21, local copies, waits for them, and re-layouts: 5.34 us -> 6.79 us
  transfers between devices with their start and end apart: 48 -> 48, of which waited for: 23 -> 24; matrix products, arithmetic and copies ran while one was open for 2% -> 2% of each run, Pallas kernels for 4% -> 7%
where the time goes in v2:
time: 241 us
  starting transfers between devices  98.8 us (41%)
  waiting for transfers between devices  85.4 us (35%)
  Pallas kernels  44.7 us (19%)
  local copies, waits for them, and re-layouts  10.8 us (4%)
    ppermute x3, starting transfers between devices, share_hubs(): lax.ppermute(ahead[:half], 'var', var_shift(1, 0))  15.9 us
    ppermute x2, waiting for transfers between devices, per_device(): lax.ppermute(across, 'samp', samp_shift(2, 0))  15 us
    pallas_call x2, Pallas kernels, gradient(): pl.pallas_call(lambda *refs: gradient_kernel(scale, slots, *refs), out_sh...  14.1 us
    ppermute x3, starting transfers between devices, share_near(): turn = lax.ppermute(turn, 'var', over)  13.6 us
    ppermute x3, starting transfers between devices, share_near(): below = lax.ppermute(value, 'var', up)  13 us
    ppermute x2, waiting for transfers between devices, per_device(): lax.ppermute(up, 'samp', samp_shift(1, 0))  11.2 us
    ppermute x9, starting transfers between devices, share_hubs(): lax.ppermute(value, 'var', var_shift(0, d))  9.19 us
    ppermute x3, waiting for transfers between devices, share_hubs(): lax.ppermute(ahead[:half], 'var', var_shift(1, 0))  8.75 us
  transfers between devices with their start and end apart: 48, of which 24 were waited for; matrix products, arithmetic and copies ran while one was open for 2% of the time, Pallas kernels for 7%

profile of v2, /device:TPU:1, one launch (start us, length us, event | category | flops | bytes accessed | tf_op | source)
XLA Modules:
  0.0 240.6 jit_solution(5243914034526788823)
XLA Ops:
  0.0 1.2 copy-done
  2.8 4.5 %collective-permute-start.2 = (bf16[272,256]{1,0:T(8,128)(2,1)S(1)}, bf16[272,256]{1,0:T(8,128)(2,1)S(1)}, u32[]{:S(2)}, u32[]{:S(2)}) collective-permute-start(bf16[272,256]{1,0:T(8,128)(2,1)S(1)} %pack_hub.1.refs_2_), channel_id=1, source_target_pairs={{0,16},{8,24},{16,0},{24,8},{32,48},{40,56},{48,32},{56,40},{64,80... | collective-permute-start | bytes 417800 | tf_op jit(solution)/shard_map/ppermute | solution.py:674
  8.8 1.2 pack_plain.1.refs_5_
  10.7 3.5 %collective-permute-done.1 = bf16[272,256]{1,0:T(8,128)(2,1)S(1)} collective-permute-done((bf16[272,256]{1,0:T(8,128)(2,1)S(1)}, bf16[272,256]{1,0:T(8,128)(2,1)S(1)}, u32[]{:S(2)}, u32[]{:S(2)}) %collective-permute-start.1) | collective-permute-done | bytes 139296 | tf_op jit(solution)/shard_map/ppermute | solution.py:674
  14.3 2.5 %collective-permute-start.4 = (bf16[4,272,256]{2,1,0:T(8,128)(2,1)S(1)}, bf16[4,272,256]{2,1,0:T(8,128)(2,1)S(1)}, u32[]{:S(2)}, u32[]{:S(2)}) collective-permute-start(bf16[4,272,256]{2,1,0:T(8,128)(2,1)S(1)} %pad_maximum_fusion.refs_9_), channel_id=1, source_target_pairs={{0,96},{8,104},{16,112},{24,120},{32,0},{40,8},{48,16},{56,24},{64... | collective-permute-start | bytes 1671176 | tf_op jit(solution)/shard_map/ppermute | solution.py:678
  17.7 1.3 collective-permute-start.10
  19.0 1.3 collective-permute-start.8
  20.3 5.0 %collective-permute-start.7 = (bf16[14,128,256]{2,1,0:T(8,128)(2,1)S(1)}, bf16[14,128,256]{2,1,0:T(8,128)(2,1)}, u32[]{:S(2)}, u32[]{:S(2)}) collective-permute-start(bf16[14,128,256]{2,1,0:T(8,128)(2,1)S(1)} %pack_plain.1.refs_5_), channel_id=1, source_target_pairs={{0,8},{8,16},{16,24},{32,40},{40,48},{48,56},{64,72},{72,80},{80,8... | collective-permute-start | bytes 2752520 | tf_op jit(solution)/shard_map/ppermute | solution.py:668
  25.2 2.1 collective-permute-done.4.refs_11_
  27.4 5.3 %collective-permute-start.6 = (bf16[2,272,256]{2,1,0:T(8,128)(2,1)S(1)}, bf16[2,272,256]{2,1,0:T(8,128)(2,1)}, u32[]{:S(2)}, u32[]{:S(2)}) collective-permute-start(bf16[2,272,256]{2,1,0:T(8,128)(2,1)S(1)} %slice.73), channel_id=1, source_target_pairs={{0,96},{8,104},{16,112},{24,120},{32,0},{40,8},{48,16},{56,24},{64... | collective-permute-start | bytes 835592 | tf_op jit(solution)/shard_map/ppermute | solution.py:681
  32.7 1.4 collective-permute-start.9
  34.1 6.9 %collective-permute-start.11 = (bf16[7,128,256]{2,1,0:T(8,128)(2,1)}, bf16[7,128,256]{2,1,0:T(8,128)(2,1)}, u32[]{:S(2)}, u32[]{:S(2)}) collective-permute-start(bf16[7,128,256]{2,1,0:T(8,128)(2,1)} %collective-permute-done.10), channel_id=1, source_target_pairs={{0,32},{56,24},{32,64},{88,56},{64,96},{120,88},{1,33},{57,25},{33... | collective-permute-start | bytes 1376264 | tf_op jit(solution)/shard_map/ppermute | solution.py:666
  41.8 3.4 %prep.1 = (bf16[4,256,512]{2,1,0:T(8,128)(2,1)S(1)}, bf16[14,256,512]{2,1,0:T(8,128)(2,1)S(1)}, f32[72,16,128]{2,1,0:T(8,128)S(1)}) custom-call(s32[16]{0:T(128)S(1)} %copy-done.8, f32[16,8,128,128]{3,2,1,0:T(8,128)} %omega.1), custom_call_target="tpu_custom_call" | custom-call | flops 16777216 | bytes 12582912 | tf_op jit(solution)/shard_map/prep/pallas_call | solution.py:269
  45.2 1.8 copy-done.1
  50.0 4.6 %collective-permute-done.5.refs_12_ = bf16[2,272,256]{2,1,0:T(8,128)(2,1)} collective-permute-done((bf16[2,272,256]{2,1,0:T(8,128)(2,1)}, bf16[2,272,256]{2,1,0:T(8,128)(2,1)}, u32[]{:S(2)}, u32[]{:S(2)}) %collective-permute-start.5) | collective-permute-done | bytes 278560 | tf_op jit(solution)/shard_map/ppermute | solution.py:680
  55.7 1.2 copy-done.4
  56.9 5.3 %hub_first.1 = (bf16[256,256]{1,0:T(8,128)(2,1)S(1)}, s32[72]{0:T(128)S(1)}, bf16[9472,256]{1,0:T(8,128)(2,1)S(1)}) custom-call(s32[16]{0:T(128)S(1)} %copy-done.8, s32[16,8]{1,0:T(8,128)S(1)} %copy.18.refs_1_, s32[32]{0:T(128)S(1)} %reshape.3.refs_2_, bf16[4,256,512]{2,1,0:T(8,128)(2,1)S(1)} %copy-done.4, ...), custom_call_target="tpu_custom_call" | custom-call | flops 268435456 | bytes 12582912 | tf_op jit(solution)/shard_map/hub_first/pallas_call | solution.py:311
  62.4 1.5 collective-permute-start.17
  63.8 2.7 %plain_first.1.refs_2_.refs_4_ = bf16[14,128,256]{2,1,0:T(8,128)(2,1)S(1)} custom-call(s32[72]{0:T(128)S(1)} %get-tuple-element.27.refs_0_.refs_1_, bf16[14,256,512]{2,1,0:T(8,128)(2,1)S(1)} %copy-done.2, bf16[9472,256]{1,0:T(8,128)(2,1)S(1)} %get-tuple-element.28.refs_2_.refs_1_.refs_4_, bf16[256,256]{1,0:T(8,128)(2,1)S(1)} %get-tuple-element.30.refs_3_), custom_call_target="tpu_custom_call" | custom-call | flops 536870912 | bytes 10485760 | tf_op jit(solution)/shard_map/plain_first/pallas_call | solution.py:339
  66.6 1.3 collective-permute-start.15
  69.1 3.7 %collective-permute-start.21 = (bf16[4,256,256]{2,1,0:T(8,128)(2,1)S(1)}, bf16[4,256,256]{2,1,0:T(8,128)(2,1)S(1)}, u32[]{:S(2)}, u32[]{:S(2)}) collective-permute-start(bf16[4,256,256]{2,1,0:T(8,128)(2,1)S(1)} %pad_maximum_fusion.1.refs_8_), channel_id=1, source_target_pairs={{0,96},{8,104},{16,112},{24,120},{32,0},{40,8},{48,16},{56,24},{64... | collective-permute-start | bytes 1572872 | tf_op jit(solution)/shard_map/ppermute | solution.py:678
  72.7 1.3 collective-permute-start.13
  74.0 4.0 %collective-permute-start.12 = (bf16[14,128,256]{2,1,0:T(8,128)(2,1)S(1)}, bf16[14,128,256]{2,1,0:T(8,128)(2,1)S(1)}, u32[]{:S(2)}, u32[]{:S(2)}) collective-permute-start(bf16[14,128,256]{2,1,0:T(8,128)(2,1)S(1)} %plain_first.1.refs_2_.refs_4_), channel_id=1, source_target_pairs={{0,8},{8,16},{16,24},{32,40},{40,48},{48,56},{64,72},{72,80},{80,8... | collective-permute-start | bytes 2752520 | tf_op jit(solution)/shard_map/ppermute | solution.py:668
  79.3 2.1 collective-permute-done.21.refs_10_
  81.4 3.3 %collective-permute-start.16 = (bf16[7,128,256]{2,1,0:T(8,128)(2,1)S(1)}, bf16[7,128,256]{2,1,0:T(8,128)(2,1)S(1)}, u32[]{:S(2)}, u32[]{:S(2)}) collective-permute-start(bf16[7,128,256]{2,1,0:T(8,128)(2,1)S(1)} %collective-permute-done.15), channel_id=1, source_target_pairs={{0,32},{56,24},{32,64},{88,56},{64,96},{120,88},{1,33},{57,25},{33... | collective-permute-start | bytes 1376264 | tf_op jit(solution)/shard_map/ppermute | solution.py:666
  84.7 3.4 %collective-permute-done.20.refs_9_ = bf16[4,256,256]{2,1,0:T(8,128)(2,1)S(1)} collective-permute-done((bf16[4,256,256]{2,1,0:T(8,128)(2,1)S(1)}, bf16[4,256,256]{2,1,0:T(8,128)(2,1)S(1)}, u32[]{:S(2)}, u32[]{:S(2)}) %collective-permute-start.20) | collective-permute-done | bytes 524320 | tf_op jit(solution)/shard_map/ppermute | solution.py:677
  88.1 9.2 %collective-permute-start.22 = (bf16[2,256,256]{2,1,0:T(8,128)(2,1)S(1)}, bf16[2,256,256]{2,1,0:T(8,128)(2,1)S(1)}, u32[]{:S(2)}, u32[]{:S(2)}) collective-permute-start(bf16[2,256,256]{2,1,0:T(8,128)(2,1)S(1)} %slice.79), channel_id=1, source_target_pairs={{0,32},{8,40},{16,48},{24,56},{32,64},{40,72},{48,80},{56,88},{64,... | collective-permute-start | bytes 786440 | tf_op jit(solution)/shard_map/ppermute | solution.py:680
  97.3 3.2 %firsts.2.refs_2_ = f32[18,128,512]{2,1,0:T(8,128)S(1)} custom-call(s32[72]{0:T(128)S(1)} %get-tuple-element.27.refs_0_.refs_1_, bf16[9472,256]{1,0:T(8,128)(2,1)S(1)} %get-tuple-element.28.refs_2_.refs_1_.refs_4_, bf16[14,128,256]{2,1,0:T(8,128)(2,1)S(1)} %plain_first.1.refs_2_.refs_4_, bf16[256,256]{1,0:T(8,128)(2,1)S(1)} %get-tuple-element.30.refs_3_), custom_call_target="tpu_custom_call" | custom-call | flops 536870912 | bytes 10485760 | tf_op jit(solution)/shard_map/firsts/pallas_call | solution.py:497
  100.6 2.0 collective-permute-done.22.refs_11_
  102.5 7.1 %gradient.2 = (f32[4,72,16,128]{3,2,1,0:T(8,128)S(1)}, f32[4,72,16,128]{3,2,1,0:T(8,128)S(1)}) custom-call(s32[72]{0:T(128)S(1)} %get-tuple-element.27.refs_0_.refs_1_, bf16[9472,256]{1,0:T(8,128)(2,1)S(1)} %get-tuple-element.28.refs_2_.refs_1_.refs_4_, f32[18,128,512]{2,1,0:T(8,128)S(1)} %firsts.2.refs_2_, ...), custom_call_target="tpu_custom_call" | custom-call | flops 1073741824 | bytes 16777216 | tf_op jit(solution)/shard_map/gradient/pallas_call | solution.py:540
  109.6 5.5 %collective-permute-start.24 = (f32[4,72,16,128]{3,2,1,0:T(8,128)S(1)}, f32[4,72,16,128]{3,2,1,0:T(8,128)S(1)}, u32[]{:S(2)}, u32[]{:S(2)}) collective-permute-start(f32[4,72,16,128]{3,2,1,0:T(8,128)S(1)} %get-tuple-element.32), channel_id=1, source_target_pairs={{0,1},{1,0},{2,3},{3,2},{4,5},{5,4},{6,7},{7,6},{8,9},{9,8},{10,11... | collective-permute-start | bytes 7077896 | tf_op jit(solution)/shard_map/ppermute | solution.py:719
  115.1 4.2 %collective-permute-done.24.other = f32[4,72,16,128]{3,2,1,0:T(8,128)S(1)} collective-permute-done((f32[4,72,16,128]{3,2,1,0:T(8,128)S(1)}, f32[4,72,16,128]{3,2,1,0:T(8,128)S(1)}, u32[]{:S(2)}, u32[]{:S(2)}) %collective-permute-start.24) | collective-permute-done | bytes 2359328 | tf_op jit(solution)/shard_map/ppermute | solution.py:719
  120.3 1.4 collective-permute-start.25
  121.6 2.6 %collective-permute-start.26 = (s16[77,16,128]{2,1,0:T(8,128)(2,1)S(1)}, s16[77,16,128]{2,1,0:T(8,128)(2,1)S(1)}, u32[]{:S(2)}, u32[]{:S(2)}) collective-permute-start(s16[77,16,128]{2,1,0:T(8,128)(2,1)S(1)} %get-tuple-element.35), channel_id=1, source_target_pairs={{0,4},{1,5},{2,6},{3,7},{4,0},{5,1},{6,2},{7,3},{8,12},{9,13},{10,... | collective-permute-start | bytes 946184 | tf_op jit(solution)/shard_map/ppermute | solution.py:724
  125.3 5.0 %collective-permute-done.25.refs_3_ = s16[77,16,128]{2,1,0:T(8,128)(2,1)S(1)} collective-permute-done((s16[77,16,128]{2,1,0:T(8,128)(2,1)S(1)}, s16[77,16,128]{2,1,0:T(8,128)(2,1)S(1)}, u32[]{:S(2)}, u32[]{:S(2)}) %collective-permute-start.25) | collective-permute-done | bytes 315424 | tf_op jit(solution)/shard_map/ppermute | solution.py:723
  130.3 7.9 %collective-permute-done.26.refs_4_ = s16[77,16,128]{2,1,0:T(8,128)(2,1)S(1)} collective-permute-done((s16[77,16,128]{2,1,0:T(8,128)(2,1)S(1)}, s16[77,16,128]{2,1,0:T(8,128)(2,1)S(1)}, u32[]{:S(2)}, u32[]{:S(2)}) %collective-permute-start.26) | collective-permute-done | bytes 315424 | tf_op jit(solution)/shard_map/ppermute | solution.py:724
  138.2 1.5 prox.1
  140.7 2.8 %collective-permute-start.29 = (s16[77,16,128]{2,1,0:T(8,128)(2,1)S(1)}, s16[77,16,128]{2,1,0:T(8,128)(2,1)S(1)}, u32[]{:S(2)}, u32[]{:S(2)}) collective-permute-start(s16[77,16,128]{2,1,0:T(8,128)(2,1)S(1)} %get-tuple-element.38), channel_id=1, source_target_pairs={{0,4},{1,5},{2,6},{3,7},{4,0},{5,1},{6,2},{7,3},{8,12},{9,13},{10,... | collective-permute-start | bytes 946184 | tf_op jit(solution)/shard_map/ppermute | solution.py:705
  143.9 4.9 %collective-permute-done.30 = s16[77,16,128]{2,1,0:T(8,128)(2,1)S(1)} collective-permute-done((s16[77,16,128]{2,1,0:T(8,128)(2,1)S(1)}, s16[77,16,128]{2,1,0:T(8,128)(2,1)S(1)}, u32[]{:S(2)}, u32[]{:S(2)}) %collective-permute-start.30) | collective-permute-done | bytes 315424 | tf_op jit(solution)/shard_map/ppermute | solution.py:706
  148.7 8.6 %collective-permute-done.29 = s16[77,16,128]{2,1,0:T(8,128)(2,1)S(1)} collective-permute-done((s16[77,16,128]{2,1,0:T(8,128)(2,1)S(1)}, s16[77,16,128]{2,1,0:T(8,128)(2,1)S(1)}, u32[]{:S(2)}, u32[]{:S(2)}) %collective-permute-start.29) | collective-permute-done | bytes 315424 | tf_op jit(solution)/shard_map/ppermute | solution.py:705
  157.6 1.4 collective-permute-start.31
  159.0 2.6 %collective-permute-done.31.refs_3_ = s16[4,77,16,128]{3,2,1,0:T(8,128)(2,1)S(1)} collective-permute-done((s16[4,77,16,128]{3,2,1,0:T(8,128)(2,1)S(1)}, s16[4,77,16,128]{3,2,1,0:T(8,128)(2,1)S(1)}, u32[]{:S(2)}, u32[]{:S(2)}) %collective-permute-start.31) | collective-permute-done | bytes 1261600 | tf_op jit(solution)/shard_map/ppermute | solution.py:709
  161.6 1.5 hub_later.1.refs_5_.refs_3_
  163.5 1.3 collective-permute-start.37
  164.7 3.4 %plain_later.1.refs_2_.refs_4_ = bf16[14,128,256]{2,1,0:T(8,128)(2,1)S(1)} custom-call(s32[16]{0:T(128)S(1)} %copy-done.8, s32[72]{0:T(128)S(1)} %get-tuple-element.27.refs_0_.refs_1_, s16[4,77,16,128]{3,2,1,0:T(8,128)(2,1)S(1)} %pad_add_fusion.refs_2_, s16[4,77,16,128]{3,2,1,0:T(8,128)(2,1)S(1)} %collective-permute-done.31.refs_3_, ...), custom_call_target="tpu_custom_call" | custom-call | flops 536870912 | bytes 8388608 | tf_op jit(solution)/shard_map/plain_later/pallas_call | solution.py:441
  168.3 1.3 collective-permute-start.35
  170.0 2.9 %collective-permute-done.37 = bf16[256,256]{1,0:T(8,128)(2,1)S(1)} collective-permute-done((bf16[256,256]{1,0:T(8,128)(2,1)S(1)}, bf16[256,256]{1,0:T(8,128)(2,1)S(1)}, u32[]{:S(2)}, u32[]{:S(2)}) %collective-permute-start.37) | collective-permute-done | bytes 131104 | tf_op jit(solution)/shard_map/ppermute | solution.py:674
  173.0 1.8 collective-permute-start.41
  174.8 1.3 collective-permute-start.33
  176.1 4.0 %collective-permute-start.32 = (bf16[14,128,256]{2,1,0:T(8,128)(2,1)S(1)}, bf16[14,128,256]{2,1,0:T(8,128)(2,1)S(1)}, u32[]{:S(2)}, u32[]{:S(2)}) collective-permute-start(bf16[14,128,256]{2,1,0:T(8,128)(2,1)S(1)} %plain_later.1.refs_2_.refs_4_), channel_id=1, source_target_pairs={{0,8},{8,16},{16,24},{32,40},{40,48},{48,56},{64,72},{72,80},{80,8... | collective-permute-start | bytes 2752520 | tf_op jit(solution)/shard_map/ppermute | solution.py:668
  180.2 2.3 collective-permute-done.35
  183.2 2.9 %collective-permute-done.41.refs_10_ = bf16[4,256,256]{2,1,0:T(8,128)(2,1)S(1)} collective-permute-done((bf16[4,256,256]{2,1,0:T(8,128)(2,1)S(1)}, bf16[4,256,256]{2,1,0:T(8,128)(2,1)S(1)}, u32[]{:S(2)}, u32[]{:S(2)}) %collective-permute-start.41) | collective-permute-done | bytes 524320 | tf_op jit(solution)/shard_map/ppermute | solution.py:678
  186.1 3.3 %collective-permute-start.36 = (bf16[7,128,256]{2,1,0:T(8,128)(2,1)S(1)}, bf16[7,128,256]{2,1,0:T(8,128)(2,1)S(1)}, u32[]{:S(2)}, u32[]{:S(2)}) collective-permute-start(bf16[7,128,256]{2,1,0:T(8,128)(2,1)S(1)} %collective-permute-done.35), channel_id=1, source_target_pairs={{0,32},{56,24},{32,64},{88,56},{64,96},{120,88},{1,33},{57,25},{33... | collective-permute-start | bytes 1376264 | tf_op jit(solution)/shard_map/ppermute | solution.py:666
  189.4 4.1 %collective-permute-done.40.refs_9_ = bf16[4,256,256]{2,1,0:T(8,128)(2,1)S(1)} collective-permute-done((bf16[4,256,256]{2,1,0:T(8,128)(2,1)S(1)}, bf16[4,256,256]{2,1,0:T(8,128)(2,1)S(1)}, u32[]{:S(2)}, u32[]{:S(2)}) %collective-permute-start.40) | collective-permute-done | bytes 524320 | tf_op jit(solution)/shard_map/ppermute | solution.py:677
  193.9 6.7 %collective-permute-start.42 = (bf16[2,256,256]{2,1,0:T(8,128)(2,1)S(1)}, bf16[2,256,256]{2,1,0:T(8,128)(2,1)S(1)}, u32[]{:S(2)}, u32[]{:S(2)}) collective-permute-start(bf16[2,256,256]{2,1,0:T(8,128)(2,1)S(1)} %slice.83), channel_id=1, source_target_pairs={{0,32},{8,40},{16,48},{24,56},{32,64},{40,72},{48,80},{56,88},{64,... | collective-permute-start | bytes 786440 | tf_op jit(solution)/shard_map/ppermute | solution.py:680
  200.6 3.2 %firsts.3.refs_2_ = f32[18,128,512]{2,1,0:T(8,128)S(1)} custom-call(s32[72]{0:T(128)S(1)} %get-tuple-element.27.refs_0_.refs_1_, bf16[9472,256]{1,0:T(8,128)(2,1)S(1)} %get-tuple-element.28.refs_2_.refs_1_.refs_4_, bf16[14,128,256]{2,1,0:T(8,128)(2,1)S(1)} %plain_later.1.refs_2_.refs_4_, bf16[256,256]{1,0:T(8,128)(2,1)S(1)} %hub_later.1.refs_5_.refs_3_), custom_call_target="tpu_custom_call" | custom-call | flops 536870912 | bytes 10485760 | tf_op jit(solution)/shard_map/firsts/pallas_call | solution.py:497
  203.8 2.2 collective-permute-done.42.refs_11_
  206.0 7.1 %gradient.3 = (f32[4,72,16,128]{3,2,1,0:T(8,128)S(1)}, f32[4,72,16,128]{3,2,1,0:T(8,128)S(1)}) custom-call(s32[72]{0:T(128)S(1)} %get-tuple-element.27.refs_0_.refs_1_, bf16[9472,256]{1,0:T(8,128)(2,1)S(1)} %get-tuple-element.28.refs_2_.refs_1_.refs_4_, f32[18,128,512]{2,1,0:T(8,128)S(1)} %firsts.3.refs_2_, ...), custom_call_target="tpu_custom_call" | custom-call | flops 1073741824 | bytes 16777216 | tf_op jit(solution)/shard_map/gradient/pallas_call | solution.py:540
  213.1 3.1 %collective-permute-start.44 = (f32[4,72,16,128]{3,2,1,0:T(8,128)S(1)}, f32[4,72,16,128]{3,2,1,0:T(8,128)S(1)}, u32[]{:S(2)}, u32[]{:S(2)}) collective-permute-start(f32[4,72,16,128]{3,2,1,0:T(8,128)S(1)} %get-tuple-element.40), channel_id=1, source_target_pairs={{0,1},{1,0},{2,3},{3,2},{4,5},{5,4},{6,7},{7,6},{8,9},{9,8},{10,11... | collective-permute-start | bytes 7077896 | tf_op jit(solution)/shard_map/ppermute | solution.py:719
  216.2 4.2 %collective-permute-done.44.other = f32[4,72,16,128]{3,2,1,0:T(8,128)S(1)} collective-permute-done((f32[4,72,16,128]{3,2,1,0:T(8,128)S(1)}, f32[4,72,16,128]{3,2,1,0:T(8,128)S(1)}, u32[]{:S(2)}, u32[]{:S(2)}) %collective-permute-start.44) | collective-permute-done | bytes 2359328 | tf_op jit(solution)/shard_map/ppermute | solution.py:719
  222.4 2.1 collective-permute-start.46
  225.1 6.2 %collective-permute-done.45.refs_3_ = s16[77,16,128]{2,1,0:T(8,128)(2,1)S(1)} collective-permute-done((s16[77,16,128]{2,1,0:T(8,128)(2,1)S(1)}, s16[77,16,128]{2,1,0:T(8,128)(2,1)S(1)}, u32[]{:S(2)}, u32[]{:S(2)}) %collective-permute-start.45) | collective-permute-done | bytes 315424 | tf_op jit(solution)/shard_map/ppermute | solution.py:723
  231.3 7.1 %collective-permute-done.46.refs_4_ = s16[77,16,128]{2,1,0:T(8,128)(2,1)S(1)} collective-permute-done((s16[77,16,128]{2,1,0:T(8,128)(2,1)S(1)}, s16[77,16,128]{2,1,0:T(8,128)(2,1)S(1)}, u32[]{:S(2)}, u32[]{:S(2)}) %collective-permute-start.46) | collective-permute-done | bytes 315424 | tf_op jit(solution)/shard_map/ppermute | solution.py:724
  238.4 2.2 prox_last.1
  (95 shorter events, 20.6 us)
Async XLA Ops:
  0.0 1.2 copy-start
  1.2 0.7 copy-start.7
  2.8 7.9 %collective-permute-start.2 = (bf16[272,256]{1,0:T(8,128)(2,1)S(1)}, bf16[272,256]{1,0:T(8,128)(2,1)S(1)}, u32[]{:S(2)}, u32[]{:S(2)}) collective-permute-start(bf16[272,256]{1,0:T(8,128)(2,1)S(1)} %pack_hub.1.refs_2_), channel_id=1, source_target_pairs={{0,16},{8,24},{16,0},{24,8},{32,48},{40,56},{48,32},{56,40},{64,80... | collective-permute-start | bytes 417800 | tf_op jit(solution)/shard_map/ppermute | solution.py:674
  7.3 6.9 %collective-permute-start.1 = (bf16[272,256]{1,0:T(8,128)(2,1)S(1)}, bf16[272,256]{1,0:T(8,128)(2,1)S(1)}, u32[]{:S(2)}, u32[]{:S(2)}) collective-permute-start(bf16[272,256]{1,0:T(8,128)(2,1)S(1)} %pack_hub.1.refs_2_), channel_id=1, source_target_pairs={{0,24},{8,0},{16,8},{24,16},{32,56},{40,32},{48,40},{56,48},{64,88... | collective-permute-start | bytes 417800 | tf_op jit(solution)/shard_map/ppermute | solution.py:674
  7.7 6.5 %collective-permute-start = (bf16[272,256]{1,0:T(8,128)(2,1)S(1)}, bf16[272,256]{1,0:T(8,128)(2,1)S(1)}, u32[]{:S(2)}, u32[]{:S(2)}) collective-permute-start(bf16[272,256]{1,0:T(8,128)(2,1)S(1)} %pack_hub.1.refs_2_), channel_id=1, source_target_pairs={{0,8},{8,16},{16,24},{24,0},{32,40},{40,48},{48,56},{56,32},{64,72... | collective-permute-start | bytes 417800 | tf_op jit(solution)/shard_map/ppermute | solution.py:674
  9.9 31.8 %copy-start.9 = (s32[16,8]{0,1:T(8,128)S(1)}, s32[16,8]{0,1:T(8,128)}, u32[]{:S(2)}) copy-start(s32[16,8]{0,1:T(8,128)} %param.6) | copy-start | bytes 1540
  9.9 31.9 %copy-start.8 = (s32[16]{0:T(128)S(1)}, s32[16]{0:T(128)}, u32[]{:S(2)}) copy-start(s32[16]{0:T(128)} %refs_0_.13) | copy-start | bytes 196
  14.3 13.0 %collective-permute-start.4 = (bf16[4,272,256]{2,1,0:T(8,128)(2,1)S(1)}, bf16[4,272,256]{2,1,0:T(8,128)(2,1)S(1)}, u32[]{:S(2)}, u32[]{:S(2)}) collective-permute-start(bf16[4,272,256]{2,1,0:T(8,128)(2,1)S(1)} %pad_maximum_fusion.refs_9_), channel_id=1, source_target_pairs={{0,96},{8,104},{16,112},{24,120},{32,0},{40,8},{48,16},{56,24},{64... | collective-permute-start | bytes 1671176 | tf_op jit(solution)/shard_map/ppermute | solution.py:678
  16.8 17.3 %collective-permute-start.3 = (bf16[4,272,256]{2,1,0:T(8,128)(2,1)S(1)}, bf16[4,272,256]{2,1,0:T(8,128)(2,1)S(1)}, u32[]{:S(2)}, u32[]{:S(2)}) collective-permute-start(bf16[4,272,256]{2,1,0:T(8,128)(2,1)S(1)} %pad_maximum_fusion.refs_9_), channel_id=1, source_target_pairs={{0,32},{8,40},{16,48},{24,56},{32,64},{40,72},{48,80},{56,88},{64,... | collective-permute-start | bytes 1671176 | tf_op jit(solution)/shard_map/ppermute | solution.py:677
  17.7 15.0 %collective-permute-start.10 = (bf16[7,128,256]{2,1,0:T(8,128)(2,1)S(1)}, bf16[7,128,256]{2,1,0:T(8,128)(2,1)}, u32[]{:S(2)}, u32[]{:S(2)}) collective-permute-start(bf16[7,128,256]{2,1,0:T(8,128)(2,1)S(1)} %get-tuple-element.49), channel_id=1, source_target_pairs={{24,0},{32,56},{56,32},{64,88},{88,64},{96,120},{25,1},{33,57},{57... | collective-permute-start | bytes 1376264 | tf_op jit(solution)/shard_map/ppermute | solution.py:665
  19.0 36.7 %collective-permute-start.8 = (bf16[14,128,256]{2,1,0:T(8,128)(2,1)S(1)}, bf16[14,128,256]{2,1,0:T(8,128)(2,1)S(1)}, u32[]{:S(2)}, u32[]{:S(2)}) collective-permute-start(bf16[14,128,256]{2,1,0:T(8,128)(2,1)S(1)} %pack_plain.1.refs_5_), channel_id=1, source_target_pairs={{8,0},{16,8},{24,16},{40,32},{48,40},{56,48},{72,64},{80,72},{88,8... | collective-permute-start | bytes 2752520 | tf_op jit(solution)/shard_map/ppermute | solution.py:669
  20.3 35.4 %collective-permute-start.7 = (bf16[14,128,256]{2,1,0:T(8,128)(2,1)S(1)}, bf16[14,128,256]{2,1,0:T(8,128)(2,1)}, u32[]{:S(2)}, u32[]{:S(2)}) collective-permute-start(bf16[14,128,256]{2,1,0:T(8,128)(2,1)S(1)} %pack_plain.1.refs_5_), channel_id=1, source_target_pairs={{0,8},{8,16},{16,24},{32,40},{40,48},{48,56},{64,72},{72,80},{80,8... | collective-permute-start | bytes 2752520 | tf_op jit(solution)/shard_map/ppermute | solution.py:668
  27.4 14.4 %collective-permute-start.6 = (bf16[2,272,256]{2,1,0:T(8,128)(2,1)S(1)}, bf16[2,272,256]{2,1,0:T(8,128)(2,1)}, u32[]{:S(2)}, u32[]{:S(2)}) collective-permute-start(bf16[2,272,256]{2,1,0:T(8,128)(2,1)S(1)} %slice.73), channel_id=1, source_target_pairs={{0,96},{8,104},{16,112},{24,120},{32,0},{40,8},{48,16},{56,24},{64... | collective-permute-start | bytes 835592 | tf_op jit(solution)/shard_map/ppermute | solution.py:681
  32.7 23.0 %collective-permute-start.9 = (bf16[7,128,256]{2,1,0:T(8,128)(2,1)}, bf16[7,128,256]{2,1,0:T(8,128)(2,1)}, u32[]{:S(2)}, u32[]{:S(2)}) collective-permute-start(bf16[7,128,256]{2,1,0:T(8,128)(2,1)} %get-tuple-element.50), channel_id=1, source_target_pairs={{24,32},{32,24},{56,64},{64,56},{88,96},{96,88},{25,33},{33,25},{5... | collective-permute-start | bytes 1376264 | tf_op jit(solution)/shard_map/ppermute | solution.py:664
  34.1 21.5 %collective-permute-start.11 = (bf16[7,128,256]{2,1,0:T(8,128)(2,1)}, bf16[7,128,256]{2,1,0:T(8,128)(2,1)}, u32[]{:S(2)}, u32[]{:S(2)}) collective-permute-start(bf16[7,128,256]{2,1,0:T(8,128)(2,1)} %collective-permute-done.10), channel_id=1, source_target_pairs={{0,32},{56,24},{32,64},{88,56},{64,96},{120,88},{1,33},{57,25},{33... | collective-permute-start | bytes 1376264 | tf_op jit(solution)/shard_map/ppermute | solution.py:666
  41.7 12.8 %collective-permute-start.5 = (bf16[2,272,256]{2,1,0:T(8,128)(2,1)}, bf16[2,272,256]{2,1,0:T(8,128)(2,1)}, u32[]{:S(2)}, u32[]{:S(2)}) collective-permute-start(bf16[2,272,256]{2,1,0:T(8,128)(2,1)} %slice.71), channel_id=1, source_target_pairs={{0,32},{8,40},{16,48},{24,56},{32,64},{40,72},{48,80},{56,88},{64,... | collective-permute-start | bytes 835592 | tf_op jit(solution)/shard_map/ppermute | solution.py:680
  45.2 1.8 copy-start.1
  47.0 1.0 copy-start.3
  48.0 0.8 copy-start.5
  55.7 1.2 copy-start.4
  56.9 6.9 %copy-start.2 = (bf16[14,256,512]{2,1,0:T(8,128)(2,1)S(1)}, bf16[14,256,512]{2,1,0:T(8,128)(2,1)}, u32[]{:S(2)}) copy-start(bf16[14,256,512]{2,1,0:T(8,128)(2,1)} %copy-done.1) | copy-start | bytes 11010052
  62.2 5.7 %collective-permute-start.19 = (bf16[256,256]{1,0:T(8,128)(2,1)S(1)}, bf16[256,256]{1,0:T(8,128)(2,1)S(1)}, u32[]{:S(2)}, u32[]{:S(2)}) collective-permute-start(bf16[256,256]{1,0:T(8,128)(2,1)S(1)} %get-tuple-element.30.refs_3_), channel_id=1, source_target_pairs={{0,16},{8,24},{16,0},{24,8},{32,48},{40,56},{48,32},{56,40},{64,80... | collective-permute-start | bytes 393224 | tf_op jit(solution)/shard_map/ppermute | solution.py:674
  62.3 5.6 %collective-permute-start.18 = (bf16[256,256]{1,0:T(8,128)(2,1)S(1)}, bf16[256,256]{1,0:T(8,128)(2,1)S(1)}, u32[]{:S(2)}, u32[]{:S(2)}) collective-permute-start(bf16[256,256]{1,0:T(8,128)(2,1)S(1)} %get-tuple-element.30.refs_3_), channel_id=1, source_target_pairs={{0,24},{8,0},{16,8},{24,16},{32,56},{40,32},{48,40},{56,48},{64,88... | collective-permute-start | bytes 393224 | tf_op jit(solution)/shard_map/ppermute | solution.py:674
  62.4 6.6 %collective-permute-start.17 = (bf16[256,256]{1,0:T(8,128)(2,1)S(1)}, bf16[256,256]{1,0:T(8,128)(2,1)S(1)}, u32[]{:S(2)}, u32[]{:S(2)}) collective-permute-start(bf16[256,256]{1,0:T(8,128)(2,1)S(1)} %get-tuple-element.30.refs_3_), channel_id=1, source_target_pairs={{0,8},{8,16},{16,24},{24,0},{32,40},{40,48},{48,56},{56,32},{64,72... | collective-permute-start | bytes 393224 | tf_op jit(solution)/shard_map/ppermute | solution.py:674
  66.6 12.0 %collective-permute-start.15 = (bf16[7,128,256]{2,1,0:T(8,128)(2,1)S(1)}, bf16[7,128,256]{2,1,0:T(8,128)(2,1)S(1)}, u32[]{:S(2)}, u32[]{:S(2)}) collective-permute-start(bf16[7,128,256]{2,1,0:T(8,128)(2,1)S(1)} %get-tuple-element.47), channel_id=1, source_target_pairs={{24,0},{32,56},{56,32},{64,88},{88,64},{96,120},{25,1},{33,57},{57... | collective-permute-start | bytes 1376264 | tf_op jit(solution)/shard_map/ppermute | solution.py:665
  69.1 12.3 %collective-permute-start.21 = (bf16[4,256,256]{2,1,0:T(8,128)(2,1)S(1)}, bf16[4,256,256]{2,1,0:T(8,128)(2,1)S(1)}, u32[]{:S(2)}, u32[]{:S(2)}) collective-permute-start(bf16[4,256,256]{2,1,0:T(8,128)(2,1)S(1)} %pad_maximum_fusion.1.refs_8_), channel_id=1, source_target_pairs={{0,96},{8,104},{16,112},{24,120},{32,0},{40,8},{48,16},{56,24},{64... | collective-permute-start | bytes 1572872 | tf_op jit(solution)/shard_map/ppermute | solution.py:678
  72.7 29.8 %collective-permute-start.13 = (bf16[14,128,256]{2,1,0:T(8,128)(2,1)S(1)}, bf16[14,128,256]{2,1,0:T(8,128)(2,1)S(1)}, u32[]{:S(2)}, u32[]{:S(2)}) collective-permute-start(bf16[14,128,256]{2,1,0:T(8,128)(2,1)S(1)} %plain_first.1.refs_2_.refs_4_), channel_id=1, source_target_pairs={{8,0},{16,8},{24,16},{40,32},{48,40},{56,48},{72,64},{80,72},{88,8... | collective-permute-start | bytes 2752520 | tf_op jit(solution)/shard_map/ppermute | solution.py:669
  74.0 28.5 %collective-permute-start.12 = (bf16[14,128,256]{2,1,0:T(8,128)(2,1)S(1)}, bf16[14,128,256]{2,1,0:T(8,128)(2,1)S(1)}, u32[]{:S(2)}, u32[]{:S(2)}) collective-permute-start(bf16[14,128,256]{2,1,0:T(8,128)(2,1)S(1)} %plain_first.1.refs_2_.refs_4_), channel_id=1, source_target_pairs={{0,8},{8,16},{16,24},{32,40},{40,48},{48,56},{64,72},{72,80},{80,8... | collective-permute-start | bytes 2752520 | tf_op jit(solution)/shard_map/ppermute | solution.py:668
  78.1 10.0 %collective-permute-start.20 = (bf16[4,256,256]{2,1,0:T(8,128)(2,1)S(1)}, bf16[4,256,256]{2,1,0:T(8,128)(2,1)S(1)}, u32[]{:S(2)}, u32[]{:S(2)}) collective-permute-start(bf16[4,256,256]{2,1,0:T(8,128)(2,1)S(1)} %pad_maximum_fusion.1.refs_8_), channel_id=1, source_target_pairs={{0,32},{8,40},{16,48},{24,56},{32,64},{40,72},{48,80},{56,88},{64,... | collective-permute-start | bytes 1572872 | tf_op jit(solution)/shard_map/ppermute | solution.py:677
  78.6 9.5 %collective-permute-start.14 = (bf16[7,128,256]{2,1,0:T(8,128)(2,1)S(1)}, bf16[7,128,256]{2,1,0:T(8,128)(2,1)S(1)}, u32[]{:S(2)}, u32[]{:S(2)}) collective-permute-start(bf16[7,128,256]{2,1,0:T(8,128)(2,1)S(1)} %get-tuple-element.48), channel_id=1, source_target_pairs={{24,32},{32,24},{56,64},{64,56},{88,96},{96,88},{25,33},{33,25},{5... | collective-permute-start | bytes 1376264 | tf_op jit(solution)/shard_map/ppermute | solution.py:664
  81.4 21.2 %collective-permute-start.16 = (bf16[7,128,256]{2,1,0:T(8,128)(2,1)S(1)}, bf16[7,128,256]{2,1,0:T(8,128)(2,1)S(1)}, u32[]{:S(2)}, u32[]{:S(2)}) collective-permute-start(bf16[7,128,256]{2,1,0:T(8,128)(2,1)S(1)} %collective-permute-done.15), channel_id=1, source_target_pairs={{0,32},{56,24},{32,64},{88,56},{64,96},{120,88},{1,33},{57,25},{33... | collective-permute-start | bytes 1376264 | tf_op jit(solution)/shard_map/ppermute | solution.py:666
  88.1 12.5 %collective-permute-start.23 = (bf16[2,256,256]{2,1,0:T(8,128)(2,1)S(1)}, bf16[2,256,256]{2,1,0:T(8,128)(2,1)S(1)}, u32[]{:S(2)}, u32[]{:S(2)}) collective-permute-start(bf16[2,256,256]{2,1,0:T(8,128)(2,1)S(1)} %slice.80), channel_id=1, source_target_pairs={{0,96},{8,104},{16,112},{24,120},{32,0},{40,8},{48,16},{56,24},{64... | collective-permute-start | bytes 786440 | tf_op jit(solution)/shard_map/ppermute | solution.py:681
  88.1 14.4 %collective-permute-start.22 = (bf16[2,256,256]{2,1,0:T(8,128)(2,1)S(1)}, bf16[2,256,256]{2,1,0:T(8,128)(2,1)S(1)}, u32[]{:S(2)}, u32[]{:S(2)}) collective-permute-start(bf16[2,256,256]{2,1,0:T(8,128)(2,1)S(1)} %slice.79), channel_id=1, source_target_pairs={{0,32},{8,40},{16,48},{24,56},{32,64},{40,72},{48,80},{56,88},{64,... | collective-permute-start | bytes 786440 | tf_op jit(solution)/shard_map/ppermute | solution.py:680
  109.6 9.6 %collective-permute-start.24 = (f32[4,72,16,128]{3,2,1,0:T(8,128)S(1)}, f32[4,72,16,128]{3,2,1,0:T(8,128)S(1)}, u32[]{:S(2)}, u32[]{:S(2)}) collective-permute-start(f32[4,72,16,128]{3,2,1,0:T(8,128)S(1)} %get-tuple-element.32), channel_id=1, source_target_pairs={{0,1},{1,0},{2,3},{3,2},{4,5},{5,4},{6,7},{7,6},{8,9},{9,8},{10,11... | collective-permute-start | bytes 7077896 | tf_op jit(solution)/shard_map/ppermute | solution.py:719
  119.2 19.0 %copy-start.6 = (f32[72,16,128]{2,1,0:T(8,128)S(1)}, f32[72,16,128]{2,1,0:T(8,128)}, u32[]{:S(2)}) copy-start(f32[72,16,128]{2,1,0:T(8,128)} %copy-done.5) | copy-start | bytes 1769476
  120.3 10.0 %collective-permute-start.25 = (s16[77,16,128]{2,1,0:T(8,128)(2,1)S(1)}, s16[77,16,128]{2,1,0:T(8,128)(2,1)S(1)}, u32[]{:S(2)}, u32[]{:S(2)}) collective-permute-start(s16[77,16,128]{2,1,0:T(8,128)(2,1)S(1)} %get-tuple-element.34), channel_id=1, source_target_pairs={{0,2},{1,3},{2,4},{3,5},{4,6},{5,7},{6,0},{7,1},{8,10},{9,11},{10,... | collective-permute-start | bytes 946184 | tf_op jit(solution)/shard_map/ppermute | solution.py:723
  121.6 16.5 %collective-permute-start.26 = (s16[77,16,128]{2,1,0:T(8,128)(2,1)S(1)}, s16[77,16,128]{2,1,0:T(8,128)(2,1)S(1)}, u32[]{:S(2)}, u32[]{:S(2)}) collective-permute-start(s16[77,16,128]{2,1,0:T(8,128)(2,1)S(1)} %get-tuple-element.35), channel_id=1, source_target_pairs={{0,4},{1,5},{2,6},{3,7},{4,0},{5,1},{6,2},{7,3},{8,12},{9,13},{10,... | collective-permute-start | bytes 946184 | tf_op jit(solution)/shard_map/ppermute | solution.py:724
  124.2 13.9 %collective-permute-start.27 = (s16[77,16,128]{2,1,0:T(8,128)(2,1)S(1)}, s16[77,16,128]{2,1,0:T(8,128)(2,1)S(1)}, u32[]{:S(2)}, u32[]{:S(2)}) collective-permute-start(s16[77,16,128]{2,1,0:T(8,128)(2,1)S(1)} %get-tuple-element.36), channel_id=1, source_target_pairs={{0,6},{1,7},{2,0},{3,1},{4,2},{5,3},{6,4},{7,5},{8,14},{9,15},{10,... | collective-permute-start | bytes 946184 | tf_op jit(solution)/shard_map/ppermute | solution.py:725
  139.7 9.1 %collective-permute-start.30 = (s16[77,16,128]{2,1,0:T(8,128)(2,1)S(1)}, s16[77,16,128]{2,1,0:T(8,128)(2,1)S(1)}, u32[]{:S(2)}, u32[]{:S(2)}) collective-permute-start(s16[77,16,128]{2,1,0:T(8,128)(2,1)S(1)} %get-tuple-element.38), channel_id=1, source_target_pairs={{0,2},{1,3},{2,4},{3,5},{4,6},{5,7},{6,0},{7,1},{8,10},{9,11},{10,... | collective-permute-start | bytes 946184 | tf_op jit(solution)/shard_map/ppermute | solution.py:706
  140.7 16.6 %collective-permute-start.29 = (s16[77,16,128]{2,1,0:T(8,128)(2,1)S(1)}, s16[77,16,128]{2,1,0:T(8,128)(2,1)S(1)}, u32[]{:S(2)}, u32[]{:S(2)}) collective-permute-start(s16[77,16,128]{2,1,0:T(8,128)(2,1)S(1)} %get-tuple-element.38), channel_id=1, source_target_pairs={{0,4},{1,5},{2,6},{3,7},{4,0},{5,1},{6,2},{7,3},{8,12},{9,13},{10,... | collective-permute-start | bytes 946184 | tf_op jit(solution)/shard_map/ppermute | solution.py:705
  143.5 13.8 %collective-permute-start.28 = (s16[77,16,128]{2,1,0:T(8,128)(2,1)S(1)}, s16[77,16,128]{2,1,0:T(8,128)(2,1)S(1)}, u32[]{:S(2)}, u32[]{:S(2)}) collective-permute-start(s16[77,16,128]{2,1,0:T(8,128)(2,1)S(1)} %get-tuple-element.38), channel_id=1, source_target_pairs={{0,6},{1,7},{2,0},{3,1},{4,2},{5,3},{6,4},{7,5},{8,14},{9,15},{10,... | collective-permute-start | bytes 946184 | tf_op jit(solution)/shard_map/ppermute | solution.py:704
  157.6 4.0 %collective-permute-start.31 = (s16[4,77,16,128]{3,2,1,0:T(8,128)(2,1)S(1)}, s16[4,77,16,128]{3,2,1,0:T(8,128)(2,1)S(1)}, u32[]{:S(2)}, u32[]{:S(2)}) collective-permute-start(s16[4,77,16,128]{3,2,1,0:T(8,128)(2,1)S(1)} %pad_add_fusion.refs_2_), channel_id=1, source_target_pairs={{0,1},{1,0},{2,3},{3,2},{4,5},{5,4},{6,7},{7,6},{8,9},{9,8},{10,11... | collective-permute-start | bytes 3784712 | tf_op jit(solution)/shard_map/ppermute | solution.py:709
  163.1 6.5 %collective-permute-start.39 = (bf16[256,256]{1,0:T(8,128)(2,1)S(1)}, bf16[256,256]{1,0:T(8,128)(2,1)S(1)}, u32[]{:S(2)}, u32[]{:S(2)}) collective-permute-start(bf16[256,256]{1,0:T(8,128)(2,1)S(1)} %hub_later.1.refs_5_.refs_3_), channel_id=1, source_target_pairs={{0,16},{8,24},{16,0},{24,8},{32,48},{40,56},{48,32},{56,40},{64,80... | collective-permute-start | bytes 393224 | tf_op jit(solution)/shard_map/ppermute | solution.py:674
  163.2 6.8 %collective-permute-start.38 = (bf16[256,256]{1,0:T(8,128)(2,1)S(1)}, bf16[256,256]{1,0:T(8,128)(2,1)S(1)}, u32[]{:S(2)}, u32[]{:S(2)}) collective-permute-start(bf16[256,256]{1,0:T(8,128)(2,1)S(1)} %hub_later.1.refs_5_.refs_3_), channel_id=1, source_target_pairs={{0,24},{8,0},{16,8},{24,16},{32,56},{40,32},{48,40},{56,48},{64,88... | collective-permute-start | bytes 393224 | tf_op jit(solution)/shard_map/ppermute | solution.py:674
  163.5 9.5 %collective-permute-start.37 = (bf16[256,256]{1,0:T(8,128)(2,1)S(1)}, bf16[256,256]{1,0:T(8,128)(2,1)S(1)}, u32[]{:S(2)}, u32[]{:S(2)}) collective-permute-start(bf16[256,256]{1,0:T(8,128)(2,1)S(1)} %hub_later.1.refs_5_.refs_3_), channel_id=1, source_target_pairs={{0,8},{8,16},{16,24},{24,0},{32,40},{40,48},{48,56},{56,32},{64,72... | collective-permute-start | bytes 393224 | tf_op jit(solution)/shard_map/ppermute | solution.py:674
  168.3 14.2 %collective-permute-start.35 = (bf16[7,128,256]{2,1,0:T(8,128)(2,1)S(1)}, bf16[7,128,256]{2,1,0:T(8,128)(2,1)S(1)}, u32[]{:S(2)}, u32[]{:S(2)}) collective-permute-start(bf16[7,128,256]{2,1,0:T(8,128)(2,1)S(1)} %get-tuple-element.45), channel_id=1, source_target_pairs={{24,0},{32,56},{56,32},{64,88},{88,64},{96,120},{25,1},{33,57},{57... | collective-permute-start | bytes 1376264 | tf_op jit(solution)/shard_map/ppermute | solution.py:665
  173.0 13.1 %collective-permute-start.41 = (bf16[4,256,256]{2,1,0:T(8,128)(2,1)S(1)}, bf16[4,256,256]{2,1,0:T(8,128)(2,1)S(1)}, u32[]{:S(2)}, u32[]{:S(2)}) collective-permute-start(bf16[4,256,256]{2,1,0:T(8,128)(2,1)S(1)} %pad_maximum_fusion.2.refs_8_), channel_id=1, source_target_pairs={{0,96},{8,104},{16,112},{24,120},{32,0},{40,8},{48,16},{56,24},{64... | collective-permute-start | bytes 1572872 | tf_op jit(solution)/shard_map/ppermute | solution.py:678
  174.8 31.2 %collective-permute-start.33 = (bf16[14,128,256]{2,1,0:T(8,128)(2,1)S(1)}, bf16[14,128,256]{2,1,0:T(8,128)(2,1)S(1)}, u32[]{:S(2)}, u32[]{:S(2)}) collective-permute-start(bf16[14,128,256]{2,1,0:T(8,128)(2,1)S(1)} %plain_later.1.refs_2_.refs_4_), channel_id=1, source_target_pairs={{8,0},{16,8},{24,16},{40,32},{48,40},{56,48},{72,64},{80,72},{88,8... | collective-permute-start | bytes 2752520 | tf_op jit(solution)/shard_map/ppermute | solution.py:669
  176.1 29.9 %collective-permute-start.32 = (bf16[14,128,256]{2,1,0:T(8,128)(2,1)S(1)}, bf16[14,128,256]{2,1,0:T(8,128)(2,1)S(1)}, u32[]{:S(2)}, u32[]{:S(2)}) collective-permute-start(bf16[14,128,256]{2,1,0:T(8,128)(2,1)S(1)} %plain_later.1.refs_2_.refs_4_), channel_id=1, source_target_pairs={{0,8},{8,16},{16,24},{32,40},{40,48},{48,56},{64,72},{72,80},{80,8... | collective-permute-start | bytes 2752520 | tf_op jit(solution)/shard_map/ppermute | solution.py:668
  180.1 13.4 %collective-permute-start.40 = (bf16[4,256,256]{2,1,0:T(8,128)(2,1)S(1)}, bf16[4,256,256]{2,1,0:T(8,128)(2,1)S(1)}, u32[]{:S(2)}, u32[]{:S(2)}) collective-permute-start(bf16[4,256,256]{2,1,0:T(8,128)(2,1)S(1)} %pad_maximum_fusion.2.refs_8_), channel_id=1, source_target_pairs={{0,32},{8,40},{16,48},{24,56},{32,64},{40,72},{48,80},{56,88},{64,... | collective-permute-start | bytes 1572872 | tf_op jit(solution)/shard_map/ppermute | solution.py:677
  182.5 11.3 %collective-permute-start.34 = (bf16[7,128,256]{2,1,0:T(8,128)(2,1)S(1)}, bf16[7,128,256]{2,1,0:T(8,128)(2,1)S(1)}, u32[]{:S(2)}, u32[]{:S(2)}) collective-permute-start(bf16[7,128,256]{2,1,0:T(8,128)(2,1)S(1)} %get-tuple-element.46), channel_id=1, source_target_pairs={{24,32},{32,24},{56,64},{64,56},{88,96},{96,88},{25,33},{33,25},{5... | collective-permute-start | bytes 1376264 | tf_op jit(solution)/shard_map/ppermute | solution.py:664
  186.1 19.9 %collective-permute-start.36 = (bf16[7,128,256]{2,1,0:T(8,128)(2,1)S(1)}, bf16[7,128,256]{2,1,0:T(8,128)(2,1)S(1)}, u32[]{:S(2)}, u32[]{:S(2)}) collective-permute-start(bf16[7,128,256]{2,1,0:T(8,128)(2,1)S(1)} %collective-permute-done.35), channel_id=1, source_target_pairs={{0,32},{56,24},{32,64},{88,56},{64,96},{120,88},{1,33},{57,25},{33... | collective-permute-start | bytes 1376264 | tf_op jit(solution)/shard_map/ppermute | solution.py:666
  193.6 10.2 %collective-permute-start.43 = (bf16[2,256,256]{2,1,0:T(8,128)(2,1)S(1)}, bf16[2,256,256]{2,1,0:T(8,128)(2,1)S(1)}, u32[]{:S(2)}, u32[]{:S(2)}) collective-permute-start(bf16[2,256,256]{2,1,0:T(8,128)(2,1)S(1)} %slice.84), channel_id=1, source_target_pairs={{0,96},{8,104},{16,112},{24,120},{32,0},{40,8},{48,16},{56,24},{64... | collective-permute-start | bytes 786440 | tf_op jit(solution)/shard_map/ppermute | solution.py:681
  193.9 12.1 %collective-permute-start.42 = (bf16[2,256,256]{2,1,0:T(8,128)(2,1)S(1)}, bf16[2,256,256]{2,1,0:T(8,128)(2,1)S(1)}, u32[]{:S(2)}, u32[]{:S(2)}) collective-permute-start(bf16[2,256,256]{2,1,0:T(8,128)(2,1)S(1)} %slice.83), channel_id=1, source_target_pairs={{0,32},{8,40},{16,48},{24,56},{32,64},{40,72},{48,80},{56,88},{64,... | collective-permute-start | bytes 786440 | tf_op jit(solution)/shard_map/ppermute | solution.py:680
  213.1 7.3 %collective-permute-start.44 = (f32[4,72,16,128]{3,2,1,0:T(8,128)S(1)}, f32[4,72,16,128]{3,2,1,0:T(8,128)S(1)}, u32[]{:S(2)}, u32[]{:S(2)}) collective-permute-start(f32[4,72,16,128]{3,2,1,0:T(8,128)S(1)} %get-tuple-element.40), channel_id=1, source_target_pairs={{0,1},{1,0},{2,3},{3,2},{4,5},{5,4},{6,7},{7,6},{8,9},{9,8},{10,11... | collective-permute-start | bytes 7077896 | tf_op jit(solution)/shard_map/ppermute | solution.py:719
  221.4 9.9 %collective-permute-start.45 = (s16[77,16,128]{2,1,0:T(8,128)(2,1)S(1)}, s16[77,16,128]{2,1,0:T(8,128)(2,1)S(1)}, u32[]{:S(2)}, u32[]{:S(2)}) collective-permute-start(s16[77,16,128]{2,1,0:T(8,128)(2,1)S(1)} %get-tuple-element.42), channel_id=1, source_target_pairs={{0,2},{1,3},{2,4},{3,5},{4,6},{5,7},{6,0},{7,1},{8,10},{9,11},{10,... | collective-permute-start | bytes 946184 | tf_op jit(solution)/shard_map/ppermute | solution.py:723
  222.4 16.1 %collective-permute-start.46 = (s16[77,16,128]{2,1,0:T(8,128)(2,1)S(1)}, s16[77,16,128]{2,1,0:T(8,128)(2,1)S(1)}, u32[]{:S(2)}, u32[]{:S(2)}) collective-permute-start(s16[77,16,128]{2,1,0:T(8,128)(2,1)S(1)} %get-tuple-element.43), channel_id=1, source_target_pairs={{0,4},{1,5},{2,6},{3,7},{4,0},{5,1},{6,2},{7,3},{8,12},{9,13},{10,... | collective-permute-start | bytes 946184 | tf_op jit(solution)/shard_map/ppermute | solution.py:724
  224.5 13.9 %collective-permute-start.47 = (s16[77,16,128]{2,1,0:T(8,128)(2,1)S(1)}, s16[77,16,128]{2,1,0:T(8,128)(2,1)S(1)}, u32[]{:S(2)}, u32[]{:S(2)}) collective-permute-start(s16[77,16,128]{2,1,0:T(8,128)(2,1)S(1)} %get-tuple-element.44), channel_id=1, source_target_pairs={{0,6},{1,7},{2,0},{3,1},{4,2},{5,3},{6,4},{7,5},{8,14},{9,15},{10,... | collective-permute-start | bytes 946184 | tf_op jit(solution)/shard_map/ppermute | solution.py:725

commit v3 on v2

--- a/solution.py
+++ b/solution.py
@@ -660,7 +660,7 @@
         direct += [(low + far, high), (high, low + far)]
         there += [(low + far, low), (high, high + far)]
         over += [(low, high), (high + far, low + far)]
-    half = value.shape[0] // 2
+    half = value.shape[0] * 5 // 14
     crossing = lax.ppermute(value[:half], "var", direct)
     turn = lax.ppermute(value[half:], "var", there)
     turn = lax.ppermute(turn, "var", over)
@@ -681,6 +681,13 @@
         lax.ppermute(behind[half:], "var", var_shift(-1, 0)),
     ]
     return [column, ahead, behind] + across
+
+
+def along_y(near, across, other, step):
+    across = lax.ppermute(across, "samp", samp_shift(2, 0))
+    near = lax.ppermute(near, "samp", samp_shift(step, 0))
+    other = lax.ppermute(other, "samp", samp_shift(-step, 0))
+    return [near, across, other]
 
 
 def per_device(data, omega, pattern, counts):
@@ -698,14 +705,7 @@
         if iteration == 0:
             m_hub, lookup, table = first_hub(counts, pattern, ids, left_hub, x_near, x_hubs)
         else:
-            mine = jnp.stack(
-                [
-                    sent,
-                    lax.ppermute(sent, "samp", samp_shift(-1, 0)),
-                    lax.ppermute(sent, "samp", samp_shift(2, 0)),
-                    lax.ppermute(sent, "samp", samp_shift(1, 0)),
-                ]
-            )
+            mine = jnp.stack([sent] + along_y(sent, sent, sent, -1))
             partner = lax.ppermute(mine, "samp", samp_shift(0, 1))
             m_hub = later_image(counts, lookup, mine, partner, table, slots, None)
         m_hubs = share_hubs(m_hub)
@@ -718,12 +718,7 @@
         keep, leave = gradient(lookup, table, firsts, m_near, m_hubs, scale, slots, parts)
         other = lax.ppermute(leave, "samp", samp_shift(0, 1))
         own, up, across, down = add_cores(keep, other)
-        terms = (
-            own,
-            lax.ppermute(up, "samp", samp_shift(1, 0)),
-            lax.ppermute(across, "samp", samp_shift(2, 0)),
-            lax.ppermute(down, "samp", samp_shift(-1, 0)),
-        )
+        terms = [own] + along_y(up, across, down, 1)
         if iteration < ITERS - 1:
             tiles, sent = prox(counts, tiles, terms, slots, False)
         else:

time: 241 us -> 249 us (1.033)
  waiting for transfers between devices: 85.4 us -> 96.1 us
  starting transfers between devices: 98.8 us -> 94.5 us
    ppermute x3, waiting for transfers between devices: 8.75 us -> 18.7 us  [share_hubs(): lax.ppermute(ahead[:half], 'var', var_shift(1, 0))]
    ppermute x3, waiting for transfers between devices: 2.75 us -> 12.1 us  [share_near(): turn = lax.ppermute(value[half:], 'var', there)]
    ppermute x9, starting transfers between devices: 9.19 us -> 16.7 us  [share_hubs(): lax.ppermute(value, 'var', var_shift(0, d))]
    ppermute x3, waiting for transfers between devices: 7.04 us -> 0.1 us  [share_hubs(): behind = lax.ppermute(column, 'var', var_shift(-1, 0))]
    ppermute x3, starting transfers between devices: 5.57 us -> 0.67 us  [share_hubs(): lax.ppermute(behind[half:], 'var', var_shift(-1, 0))]
    ppermute x3, starting transfers between devices: 15.9 us -> 11.8 us  [share_hubs(): lax.ppermute(ahead[:half], 'var', var_shift(1, 0))]
    ppermute x2, starting transfers between devices: 8.55 us -> 4.98 us  [per_device(): other = lax.ppermute(leave, 'samp', samp_shift(0, 1))]
    ppermute x9, waiting for transfers between devices: 8.71 us -> 5.41 us  [share_hubs(): lax.ppermute(value, 'var', var_shift(0, d))]
where the time goes in v3:
time: 249 us; the launch traced here: 246 us
  waiting for transfers between devices  96.1 us (39%)
  starting transfers between devices  94.5 us (38%)
  Pallas kernels  44 us (18%)
  local copies, waits for them, and re-layouts  10.8 us (4%)
    ppermute x3, waiting for transfers between devices, along_y(): across = lax.ppermute(across, 'samp', samp_shift(2, 0))  23.6 us
    ppermute x3, waiting for transfers between devices, share_hubs(): lax.ppermute(ahead[:half], 'var', var_shift(1, 0))  18.7 us
    ppermute x9, starting transfers between devices, share_hubs(): lax.ppermute(value, 'var', var_shift(0, d))  16.7 us
    pallas_call x2, Pallas kernels, gradient(): pl.pallas_call(lambda *refs: gradient_kernel(scale, slots, *refs), out_sh...  13.5 us
    ppermute x3, starting transfers between devices, share_near(): below = lax.ppermute(value, 'var', up)  13 us
    ppermute x3, starting transfers between devices, share_near(): turn = lax.ppermute(turn, 'var', over)  12.6 us
    ppermute x3, waiting for transfers between devices, share_near(): turn = lax.ppermute(value[half:], 'var', there)  12.1 us
    ppermute x3, starting transfers between devices, share_hubs(): lax.ppermute(ahead[:half], 'var', var_shift(1, 0))  11.8 us
  transfers between devices with their start and end apart: 48, of which 24 were waited for; matrix products, arithmetic and copies ran while one was open for 2% of the time, Pallas kernels for 7%

profile of v3, /device:TPU:1, one launch (start us, length us, event | category | flops | bytes accessed | tf_op | source)
XLA Modules:
  0.0 246.3 jit_solution(14318758431067910036)
XLA Ops:
  0.0 1.2 copy-done
  2.8 4.5 %collective-permute-start.2 = (bf16[272,256]{1,0:T(8,128)(2,1)S(1)}, bf16[272,256]{1,0:T(8,128)(2,1)S(1)}, u32[]{:S(2)}, u32[]{:S(2)}) collective-permute-start(bf16[272,256]{1,0:T(8,128)(2,1)S(1)} %pack_hub.1.refs_2_), channel_id=1, source_target_pairs={{0,16},{8,24},{16,0},{24,8},{32,48},{40,56},{48,32},{56,40},{64,80... | collective-permute-start | bytes 417800 | tf_op jit(solution)/shard_map/ppermute | solution.py:674
  8.8 1.2 pack_plain.1.refs_5_
  10.0 1.3 collective-permute-start.10
  11.3 2.9 %collective-permute-done.1 = bf16[272,256]{1,0:T(8,128)(2,1)S(1)} collective-permute-done((bf16[272,256]{1,0:T(8,128)(2,1)S(1)}, bf16[272,256]{1,0:T(8,128)(2,1)S(1)}, u32[]{:S(2)}, u32[]{:S(2)}) %collective-permute-start.1) | collective-permute-done | bytes 139296 | tf_op jit(solution)/shard_map/ppermute | solution.py:674
  14.3 2.7 %collective-permute-start.4 = (bf16[4,272,256]{2,1,0:T(8,128)(2,1)S(1)}, bf16[4,272,256]{2,1,0:T(8,128)(2,1)S(1)}, u32[]{:S(2)}, u32[]{:S(2)}) collective-permute-start(bf16[4,272,256]{2,1,0:T(8,128)(2,1)S(1)} %pad_maximum_fusion.refs_9_), channel_id=1, source_target_pairs={{0,96},{8,104},{16,112},{24,120},{32,0},{40,8},{48,16},{56,24},{64... | collective-permute-start | bytes 1671176 | tf_op jit(solution)/shard_map/ppermute | solution.py:678
  17.0 1.3 collective-permute-start.8
  18.3 5.0 %collective-permute-start.7 = (bf16[14,128,256]{2,1,0:T(8,128)(2,1)S(1)}, bf16[14,128,256]{2,1,0:T(8,128)(2,1)}, u32[]{:S(2)}, u32[]{:S(2)}) collective-permute-start(bf16[14,128,256]{2,1,0:T(8,128)(2,1)S(1)} %pack_plain.1.refs_5_), channel_id=1, source_target_pairs={{0,8},{8,16},{16,24},{32,40},{40,48},{48,56},{64,72},{72,80},{80,8... | collective-permute-start | bytes 2752520 | tf_op jit(solution)/shard_map/ppermute | solution.py:668
  23.3 3.3 %collective-permute-done.10 = bf16[9,128,256]{2,1,0:T(8,128)(2,1)} collective-permute-done((bf16[9,128,256]{2,1,0:T(8,128)(2,1)S(1)}, bf16[9,128,256]{2,1,0:T(8,128)(2,1)}, u32[]{:S(2)}, u32[]{:S(2)}) %collective-permute-start.10) | collective-permute-done | bytes 589856 | tf_op jit(solution)/shard_map/ppermute | solution.py:665
  26.6 3.9 %collective-permute-start.11 = (bf16[9,128,256]{2,1,0:T(8,128)(2,1)}, bf16[9,128,256]{2,1,0:T(8,128)(2,1)}, u32[]{:S(2)}, u32[]{:S(2)}) collective-permute-start(bf16[9,128,256]{2,1,0:T(8,128)(2,1)} %collective-permute-done.10), channel_id=1, source_target_pairs={{0,32},{56,24},{32,64},{88,56},{64,96},{120,88},{1,33},{57,25},{33... | collective-permute-start | bytes 1769480 | tf_op jit(solution)/shard_map/ppermute | solution.py:666
  31.5 4.6 %collective-permute-done.3.refs_10_ = bf16[4,272,256]{2,1,0:T(8,128)(2,1)S(1)} collective-permute-done((bf16[4,272,256]{2,1,0:T(8,128)(2,1)S(1)}, bf16[4,272,256]{2,1,0:T(8,128)(2,1)S(1)}, u32[]{:S(2)}, u32[]{:S(2)}) %collective-permute-start.3) | collective-permute-done | bytes 557088 | tf_op jit(solution)/shard_map/ppermute | solution.py:677
  36.0 1.4 collective-permute-start.9
  38.2 3.0 %collective-permute-start.5 = (bf16[2,272,256]{2,1,0:T(8,128)(2,1)}, bf16[2,272,256]{2,1,0:T(8,128)(2,1)}, u32[]{:S(2)}, u32[]{:S(2)}) collective-permute-start(bf16[2,272,256]{2,1,0:T(8,128)(2,1)} %slice.71), channel_id=1, source_target_pairs={{0,32},{8,40},{16,48},{24,56},{32,64},{40,72},{48,80},{56,88},{64,... | collective-permute-start | bytes 835592 | tf_op jit(solution)/shard_map/ppermute | solution.py:680
  41.2 3.4 %prep.1 = (bf16[4,256,512]{2,1,0:T(8,128)(2,1)S(1)}, bf16[14,256,512]{2,1,0:T(8,128)(2,1)S(1)}, f32[72,16,128]{2,1,0:T(8,128)S(1)}) custom-call(s32[16]{0:T(128)S(1)} %copy-done.8, f32[16,8,128,128]{3,2,1,0:T(8,128)} %omega.1), custom_call_target="tpu_custom_call" | custom-call | flops 16777216 | bytes 12582912 | tf_op jit(solution)/shard_map/prep/pallas_call | solution.py:269
  44.6 1.8 copy-done.1
  49.4 2.3 collective-permute-done.5.refs_12_
  52.8 1.2 copy-done.4
  54.0 5.3 %hub_first.1 = (bf16[256,256]{1,0:T(8,128)(2,1)S(1)}, s32[72]{0:T(128)S(1)}, bf16[9472,256]{1,0:T(8,128)(2,1)S(1)}) custom-call(s32[16]{0:T(128)S(1)} %copy-done.8, s32[16,8]{1,0:T(8,128)S(1)} %copy.18.refs_1_, s32[32]{0:T(128)S(1)} %reshape.3.refs_2_, bf16[4,256,512]{2,1,0:T(8,128)(2,1)S(1)} %copy-done.4, ...), custom_call_target="tpu_custom_call" | custom-call | flops 268435456 | bytes 12582912 | tf_op jit(solution)/shard_map/hub_first/pallas_call | solution.py:311
  59.4 7.6 %collective-permute-start.18 = (bf16[256,256]{1,0:T(8,128)(2,1)S(1)}, bf16[256,256]{1,0:T(8,128)(2,1)S(1)}, u32[]{:S(2)}, u32[]{:S(2)}) collective-permute-start(bf16[256,256]{1,0:T(8,128)(2,1)S(1)} %get-tuple-element.30.refs_3_), channel_id=1, source_target_pairs={{0,24},{8,0},{16,8},{24,16},{32,56},{40,32},{48,40},{56,48},{64,88... | collective-permute-start | bytes 393224 | tf_op jit(solution)/shard_map/ppermute | solution.py:674
  67.5 2.7 %plain_first.1.refs_2_.refs_4_ = bf16[14,128,256]{2,1,0:T(8,128)(2,1)S(1)} custom-call(s32[72]{0:T(128)S(1)} %get-tuple-element.27.refs_0_.refs_1_, bf16[14,256,512]{2,1,0:T(8,128)(2,1)S(1)} %copy-done.2, bf16[9472,256]{1,0:T(8,128)(2,1)S(1)} %get-tuple-element.28.refs_2_.refs_1_.refs_4_, bf16[256,256]{1,0:T(8,128)(2,1)S(1)} %get-tuple-element.30.refs_3_), custom_call_target="tpu_custom_call" | custom-call | flops 536870912 | bytes 10485760 | tf_op jit(solution)/shard_map/plain_first/pallas_call | solution.py:339
  70.2 1.3 collective-permute-start.15
  72.1 3.9 %collective-permute-start.21 = (bf16[4,256,256]{2,1,0:T(8,128)(2,1)S(1)}, bf16[4,256,256]{2,1,0:T(8,128)(2,1)S(1)}, u32[]{:S(2)}, u32[]{:S(2)}) collective-permute-start(bf16[4,256,256]{2,1,0:T(8,128)(2,1)S(1)} %pad_maximum_fusion.1.refs_8_), channel_id=1, source_target_pairs={{0,96},{8,104},{16,112},{24,120},{32,0},{40,8},{48,16},{56,24},{64... | collective-permute-start | bytes 1572872 | tf_op jit(solution)/shard_map/ppermute | solution.py:678
  76.0 1.3 collective-permute-start.13
  77.3 4.0 %collective-permute-start.12 = (bf16[14,128,256]{2,1,0:T(8,128)(2,1)S(1)}, bf16[14,128,256]{2,1,0:T(8,128)(2,1)S(1)}, u32[]{:S(2)}, u32[]{:S(2)}) collective-permute-start(bf16[14,128,256]{2,1,0:T(8,128)(2,1)S(1)} %plain_first.1.refs_2_.refs_4_), channel_id=1, source_target_pairs={{0,8},{8,16},{16,24},{32,40},{40,48},{48,56},{64,72},{72,80},{80,8... | collective-permute-start | bytes 2752520 | tf_op jit(solution)/shard_map/ppermute | solution.py:668
  81.5 3.5 %collective-permute-done.15 = bf16[9,128,256]{2,1,0:T(8,128)(2,1)S(1)} collective-permute-done((bf16[9,128,256]{2,1,0:T(8,128)(2,1)S(1)}, bf16[9,128,256]{2,1,0:T(8,128)(2,1)S(1)}, u32[]{:S(2)}, u32[]{:S(2)}) %collective-permute-start.15) | collective-permute-done | bytes 589856 | tf_op jit(solution)/shard_map/ppermute | solution.py:665
  85.7 4.4 %collective-permute-start.16 = (bf16[9,128,256]{2,1,0:T(8,128)(2,1)S(1)}, bf16[9,128,256]{2,1,0:T(8,128)(2,1)S(1)}, u32[]{:S(2)}, u32[]{:S(2)}) collective-permute-start(bf16[9,128,256]{2,1,0:T(8,128)(2,1)S(1)} %collective-permute-done.15), channel_id=1, source_target_pairs={{0,32},{56,24},{32,64},{88,56},{64,96},{120,88},{1,33},{57,25},{33... | collective-permute-start | bytes 1769480 | tf_op jit(solution)/shard_map/ppermute | solution.py:666
  90.1 1.3 collective-permute-done.20.refs_9_
  91.7 4.5 %collective-permute-start.22 = (bf16[2,256,256]{2,1,0:T(8,128)(2,1)S(1)}, bf16[2,256,256]{2,1,0:T(8,128)(2,1)S(1)}, u32[]{:S(2)}, u32[]{:S(2)}) collective-permute-start(bf16[2,256,256]{2,1,0:T(8,128)(2,1)S(1)} %slice.79), channel_id=1, source_target_pairs={{0,32},{8,40},{16,48},{24,56},{32,64},{40,72},{48,80},{56,88},{64,... | collective-permute-start | bytes 786440 | tf_op jit(solution)/shard_map/ppermute | solution.py:680
  96.1 3.2 %firsts.2.refs_2_ = f32[18,128,512]{2,1,0:T(8,128)S(1)} custom-call(s32[72]{0:T(128)S(1)} %get-tuple-element.27.refs_0_.refs_1_, bf16[9472,256]{1,0:T(8,128)(2,1)S(1)} %get-tuple-element.28.refs_2_.refs_1_.refs_4_, bf16[14,128,256]{2,1,0:T(8,128)(2,1)S(1)} %plain_first.1.refs_2_.refs_4_, bf16[256,256]{1,0:T(8,128)(2,1)S(1)} %get-tuple-element.30.refs_3_), custom_call_target="tpu_custom_call" | custom-call | flops 536870912 | bytes 10485760 | tf_op jit(solution)/shard_map/firsts/pallas_call | solution.py:497
  99.7 9.1 %collective-permute-done.22.refs_11_ = bf16[2,256,256]{2,1,0:T(8,128)(2,1)S(1)} collective-permute-done((bf16[2,256,256]{2,1,0:T(8,128)(2,1)S(1)}, bf16[2,256,256]{2,1,0:T(8,128)(2,1)S(1)}, u32[]{:S(2)}, u32[]{:S(2)}) %collective-permute-start.22) | collective-permute-done | bytes 262176 | tf_op jit(solution)/shard_map/ppermute | solution.py:680
  108.8 6.7 %gradient.2 = (f32[4,72,16,128]{3,2,1,0:T(8,128)S(1)}, f32[4,72,16,128]{3,2,1,0:T(8,128)S(1)}) custom-call(s32[72]{0:T(128)S(1)} %get-tuple-element.27.refs_0_.refs_1_, bf16[9472,256]{1,0:T(8,128)(2,1)S(1)} %get-tuple-element.28.refs_2_.refs_1_.refs_4_, f32[18,128,512]{2,1,0:T(8,128)S(1)} %firsts.2.refs_2_, ...), custom_call_target="tpu_custom_call" | custom-call | flops 1073741824 | bytes 16777216 | tf_op jit(solution)/shard_map/gradient/pallas_call | solution.py:540
  115.6 3.1 %collective-permute-start.24 = (f32[4,72,16,128]{3,2,1,0:T(8,128)S(1)}, f32[4,72,16,128]{3,2,1,0:T(8,128)S(1)}, u32[]{:S(2)}, u32[]{:S(2)}) collective-permute-start(f32[4,72,16,128]{3,2,1,0:T(8,128)S(1)} %get-tuple-element.32), channel_id=1, source_target_pairs={{0,1},{1,0},{2,3},{3,2},{4,5},{5,4},{6,7},{7,6},{8,9},{9,8},{10,11... | collective-permute-start | bytes 7077896 | tf_op jit(solution)/shard_map/ppermute | solution.py:719
  118.7 4.2 %collective-permute-done.24.other = f32[4,72,16,128]{3,2,1,0:T(8,128)S(1)} collective-permute-done((f32[4,72,16,128]{3,2,1,0:T(8,128)S(1)}, f32[4,72,16,128]{3,2,1,0:T(8,128)S(1)}, u32[]{:S(2)}, u32[]{:S(2)}) %collective-permute-start.24) | collective-permute-done | bytes 2359328 | tf_op jit(solution)/shard_map/ppermute | solution.py:719
  123.9 1.4 collective-permute-start.25
  125.3 2.6 %collective-permute-start.26 = (s16[77,16,128]{2,1,0:T(8,128)(2,1)S(1)}, s16[77,16,128]{2,1,0:T(8,128)(2,1)S(1)}, u32[]{:S(2)}, u32[]{:S(2)}) collective-permute-start(s16[77,16,128]{2,1,0:T(8,128)(2,1)S(1)} %get-tuple-element.35), channel_id=1, source_target_pairs={{0,4},{1,5},{2,6},{3,7},{4,0},{5,1},{6,2},{7,3},{8,12},{9,13},{10,... | collective-permute-start | bytes 946184 | tf_op jit(solution)/shard_map/ppermute | solution.py:687
  128.9 5.0 %collective-permute-done.25.refs_3_ = s16[77,16,128]{2,1,0:T(8,128)(2,1)S(1)} collective-permute-done((s16[77,16,128]{2,1,0:T(8,128)(2,1)S(1)}, s16[77,16,128]{2,1,0:T(8,128)(2,1)S(1)}, u32[]{:S(2)}, u32[]{:S(2)}) %collective-permute-start.25) | collective-permute-done | bytes 315424 | tf_op jit(solution)/shard_map/ppermute | solution.py:688
  133.9 7.9 %collective-permute-done.26.refs_4_ = s16[77,16,128]{2,1,0:T(8,128)(2,1)S(1)} collective-permute-done((s16[77,16,128]{2,1,0:T(8,128)(2,1)S(1)}, s16[77,16,128]{2,1,0:T(8,128)(2,1)S(1)}, u32[]{:S(2)}, u32[]{:S(2)}) %collective-permute-start.26) | collective-permute-done | bytes 315424 | tf_op jit(solution)/shard_map/ppermute | solution.py:687
  141.8 1.5 prox.1
  144.4 2.8 %collective-permute-start.29 = (s16[77,16,128]{2,1,0:T(8,128)(2,1)S(1)}, s16[77,16,128]{2,1,0:T(8,128)(2,1)S(1)}, u32[]{:S(2)}, u32[]{:S(2)}) collective-permute-start(s16[77,16,128]{2,1,0:T(8,128)(2,1)S(1)} %get-tuple-element.38), channel_id=1, source_target_pairs={{0,4},{1,5},{2,6},{3,7},{4,0},{5,1},{6,2},{7,3},{8,12},{9,13},{10,... | collective-permute-start | bytes 946184 | tf_op jit(solution)/shard_map/ppermute | solution.py:687
  147.5 4.9 %collective-permute-done.30 = s16[77,16,128]{2,1,0:T(8,128)(2,1)S(1)} collective-permute-done((s16[77,16,128]{2,1,0:T(8,128)(2,1)S(1)}, s16[77,16,128]{2,1,0:T(8,128)(2,1)S(1)}, u32[]{:S(2)}, u32[]{:S(2)}) %collective-permute-start.30) | collective-permute-done | bytes 315424 | tf_op jit(solution)/shard_map/ppermute | solution.py:689
  152.4 8.6 %collective-permute-done.29 = s16[77,16,128]{2,1,0:T(8,128)(2,1)S(1)} collective-permute-done((s16[77,16,128]{2,1,0:T(8,128)(2,1)S(1)}, s16[77,16,128]{2,1,0:T(8,128)(2,1)S(1)}, u32[]{:S(2)}, u32[]{:S(2)}) %collective-permute-start.29) | collective-permute-done | bytes 315424 | tf_op jit(solution)/shard_map/ppermute | solution.py:687
  161.2 1.4 collective-permute-start.31
  162.7 2.6 %collective-permute-done.31.refs_3_ = s16[4,77,16,128]{3,2,1,0:T(8,128)(2,1)S(1)} collective-permute-done((s16[4,77,16,128]{3,2,1,0:T(8,128)(2,1)S(1)}, s16[4,77,16,128]{3,2,1,0:T(8,128)(2,1)S(1)}, u32[]{:S(2)}, u32[]{:S(2)}) %collective-permute-start.31) | collective-permute-done | bytes 1261600 | tf_op jit(solution)/shard_map/ppermute | solution.py:709
  165.3 1.5 hub_later.1.refs_5_.refs_3_
  166.9 2.0 collective-permute-start.38
  169.4 3.5 %plain_later.1.refs_2_.refs_4_ = bf16[14,128,256]{2,1,0:T(8,128)(2,1)S(1)} custom-call(s32[16]{0:T(128)S(1)} %copy-done.8, s32[72]{0:T(128)S(1)} %get-tuple-element.27.refs_0_.refs_1_, s16[4,77,16,128]{3,2,1,0:T(8,128)(2,1)S(1)} %pad_add_fusion.refs_2_, s16[4,77,16,128]{3,2,1,0:T(8,128)(2,1)S(1)} %collective-permute-done.31.refs_3_, ...), custom_call_target="tpu_custom_call" | custom-call | flops 536870912 | bytes 8388608 | tf_op jit(solution)/shard_map/plain_later/pallas_call | solution.py:441
  172.9 1.3 collective-permute-start.35
  174.2 1.2 collective-permute-done.38
  176.3 2.9 %collective-permute-start.41 = (bf16[4,256,256]{2,1,0:T(8,128)(2,1)S(1)}, bf16[4,256,256]{2,1,0:T(8,128)(2,1)S(1)}, u32[]{:S(2)}, u32[]{:S(2)}) collective-permute-start(bf16[4,256,256]{2,1,0:T(8,128)(2,1)S(1)} %pad_maximum_fusion.2.refs_8_), channel_id=1, source_target_pairs={{0,96},{8,104},{16,112},{24,120},{32,0},{40,8},{48,16},{56,24},{64... | collective-permute-start | bytes 1572872 | tf_op jit(solution)/shard_map/ppermute | solution.py:678
  179.2 1.3 collective-permute-start.33
  180.5 4.0 %collective-permute-start.32 = (bf16[14,128,256]{2,1,0:T(8,128)(2,1)S(1)}, bf16[14,128,256]{2,1,0:T(8,128)(2,1)S(1)}, u32[]{:S(2)}, u32[]{:S(2)}) collective-permute-start(bf16[14,128,256]{2,1,0:T(8,128)(2,1)S(1)} %plain_later.1.refs_2_.refs_4_), channel_id=1, source_target_pairs={{0,8},{8,16},{16,24},{32,40},{40,48},{48,56},{64,72},{72,80},{80,8... | collective-permute-start | bytes 2752520 | tf_op jit(solution)/shard_map/ppermute | solution.py:668
  184.7 5.3 %collective-permute-done.35 = bf16[9,128,256]{2,1,0:T(8,128)(2,1)S(1)} collective-permute-done((bf16[9,128,256]{2,1,0:T(8,128)(2,1)S(1)}, bf16[9,128,256]{2,1,0:T(8,128)(2,1)S(1)}, u32[]{:S(2)}, u32[]{:S(2)}) %collective-permute-start.35) | collective-permute-done | bytes 589856 | tf_op jit(solution)/shard_map/ppermute | solution.py:665
  190.8 4.3 %collective-permute-start.36 = (bf16[9,128,256]{2,1,0:T(8,128)(2,1)S(1)}, bf16[9,128,256]{2,1,0:T(8,128)(2,1)S(1)}, u32[]{:S(2)}, u32[]{:S(2)}) collective-permute-start(bf16[9,128,256]{2,1,0:T(8,128)(2,1)S(1)} %collective-permute-done.35), channel_id=1, source_target_pairs={{0,32},{56,24},{32,64},{88,56},{64,96},{120,88},{1,33},{57,25},{33... | collective-permute-start | bytes 1769480 | tf_op jit(solution)/shard_map/ppermute | solution.py:666
  195.1 2.9 %collective-permute-done.40.refs_9_ = bf16[4,256,256]{2,1,0:T(8,128)(2,1)S(1)} collective-permute-done((bf16[4,256,256]{2,1,0:T(8,128)(2,1)S(1)}, bf16[4,256,256]{2,1,0:T(8,128)(2,1)S(1)}, u32[]{:S(2)}, u32[]{:S(2)}) %collective-permute-start.40) | collective-permute-done | bytes 524320 | tf_op jit(solution)/shard_map/ppermute | solution.py:677
  198.3 4.4 %collective-permute-start.42 = (bf16[2,256,256]{2,1,0:T(8,128)(2,1)S(1)}, bf16[2,256,256]{2,1,0:T(8,128)(2,1)S(1)}, u32[]{:S(2)}, u32[]{:S(2)}) collective-permute-start(bf16[2,256,256]{2,1,0:T(8,128)(2,1)S(1)} %slice.83), channel_id=1, source_target_pairs={{0,32},{8,40},{16,48},{24,56},{32,64},{40,72},{48,80},{56,88},{64,... | collective-permute-start | bytes 786440 | tf_op jit(solution)/shard_map/ppermute | solution.py:680
  202.7 3.2 %firsts.3.refs_2_ = f32[18,128,512]{2,1,0:T(8,128)S(1)} custom-call(s32[72]{0:T(128)S(1)} %get-tuple-element.27.refs_0_.refs_1_, bf16[9472,256]{1,0:T(8,128)(2,1)S(1)} %get-tuple-element.28.refs_2_.refs_1_.refs_4_, bf16[14,128,256]{2,1,0:T(8,128)(2,1)S(1)} %plain_later.1.refs_2_.refs_4_, bf16[256,256]{1,0:T(8,128)(2,1)S(1)} %hub_later.1.refs_5_.refs_3_), custom_call_target="tpu_custom_call" | custom-call | flops 536870912 | bytes 10485760 | tf_op jit(solution)/shard_map/firsts/pallas_call | solution.py:497
  205.9 7.3 %collective-permute-done.42.refs_11_ = bf16[2,256,256]{2,1,0:T(8,128)(2,1)S(1)} collective-permute-done((bf16[2,256,256]{2,1,0:T(8,128)(2,1)S(1)}, bf16[2,256,256]{2,1,0:T(8,128)(2,1)S(1)}, u32[]{:S(2)}, u32[]{:S(2)}) %collective-permute-start.42) | collective-permute-done | bytes 262176 | tf_op jit(solution)/shard_map/ppermute | solution.py:680
  213.2 6.7 %gradient.3 = (f32[4,72,16,128]{3,2,1,0:T(8,128)S(1)}, f32[4,72,16,128]{3,2,1,0:T(8,128)S(1)}) custom-call(s32[72]{0:T(128)S(1)} %get-tuple-element.27.refs_0_.refs_1_, bf16[9472,256]{1,0:T(8,128)(2,1)S(1)} %get-tuple-element.28.refs_2_.refs_1_.refs_4_, f32[18,128,512]{2,1,0:T(8,128)S(1)} %firsts.3.refs_2_, ...), custom_call_target="tpu_custom_call" | custom-call | flops 1073741824 | bytes 16777216 | tf_op jit(solution)/shard_map/gradient/pallas_call | solution.py:540
  220.0 1.9 collective-permute-start.44
  221.9 4.2 %collective-permute-done.44.other = f32[4,72,16,128]{3,2,1,0:T(8,128)S(1)} collective-permute-done((f32[4,72,16,128]{3,2,1,0:T(8,128)S(1)}, f32[4,72,16,128]{3,2,1,0:T(8,128)S(1)}, u32[]{:S(2)}, u32[]{:S(2)}) %collective-permute-start.44) | collective-permute-done | bytes 2359328 | tf_op jit(solution)/shard_map/ppermute | solution.py:719
  228.0 2.1 collective-permute-start.46
  230.8 6.2 %collective-permute-done.45.refs_3_ = s16[77,16,128]{2,1,0:T(8,128)(2,1)S(1)} collective-permute-done((s16[77,16,128]{2,1,0:T(8,128)(2,1)S(1)}, s16[77,16,128]{2,1,0:T(8,128)(2,1)S(1)}, u32[]{:S(2)}, u32[]{:S(2)}) %collective-permute-start.45) | collective-permute-done | bytes 315424 | tf_op jit(solution)/shard_map/ppermute | solution.py:688
  237.0 7.1 %collective-permute-done.46.refs_4_ = s16[77,16,128]{2,1,0:T(8,128)(2,1)S(1)} collective-permute-done((s16[77,16,128]{2,1,0:T(8,128)(2,1)S(1)}, s16[77,16,128]{2,1,0:T(8,128)(2,1)S(1)}, u32[]{:S(2)}, u32[]{:S(2)}) %collective-permute-start.46) | collective-permute-done | bytes 315424 | tf_op jit(solution)/shard_map/ppermute | solution.py:687
  244.1 2.2 prox_last.1
  (98 shorter events, 20.6 us)
Async XLA Ops:
  0.0 1.2 copy-start
  1.2 0.7 copy-start.7
  2.8 8.5 %collective-permute-start.2 = (bf16[272,256]{1,0:T(8,128)(2,1)S(1)}, bf16[272,256]{1,0:T(8,128)(2,1)S(1)}, u32[]{:S(2)}, u32[]{:S(2)}) collective-permute-start(bf16[272,256]{1,0:T(8,128)(2,1)S(1)} %pack_hub.1.refs_2_), channel_id=1, source_target_pairs={{0,16},{8,24},{16,0},{24,8},{32,48},{40,56},{48,32},{56,40},{64,80... | collective-permute-start | bytes 417800 | tf_op jit(solution)/shard_map/ppermute | solution.py:674
  7.3 6.9 %collective-permute-start.1 = (bf16[272,256]{1,0:T(8,128)(2,1)S(1)}, bf16[272,256]{1,0:T(8,128)(2,1)S(1)}, u32[]{:S(2)}, u32[]{:S(2)}) collective-permute-start(bf16[272,256]{1,0:T(8,128)(2,1)S(1)} %pack_hub.1.refs_2_), channel_id=1, source_target_pairs={{0,24},{8,0},{16,8},{24,16},{32,56},{40,32},{48,40},{56,48},{64,88... | collective-permute-start | bytes 417800 | tf_op jit(solution)/shard_map/ppermute | solution.py:674
  7.7 6.5 %collective-permute-start = (bf16[272,256]{1,0:T(8,128)(2,1)S(1)}, bf16[272,256]{1,0:T(8,128)(2,1)S(1)}, u32[]{:S(2)}, u32[]{:S(2)}) collective-permute-start(bf16[272,256]{1,0:T(8,128)(2,1)S(1)} %pack_hub.1.refs_2_), channel_id=1, source_target_pairs={{0,8},{8,16},{16,24},{24,0},{32,40},{40,48},{48,56},{56,32},{64,72... | collective-permute-start | bytes 417800 | tf_op jit(solution)/shard_map/ppermute | solution.py:674
  9.9 31.2 %copy-start.9 = (s32[16,8]{0,1:T(8,128)S(1)}, s32[16,8]{0,1:T(8,128)}, u32[]{:S(2)}) copy-start(s32[16,8]{0,1:T(8,128)} %param.6) | copy-start | bytes 1540
  9.9 31.3 %copy-start.8 = (s32[16]{0:T(128)S(1)}, s32[16]{0:T(128)}, u32[]{:S(2)}) copy-start(s32[16]{0:T(128)} %refs_0_.13) | copy-start | bytes 196
  10.0 16.6 %collective-permute-start.10 = (bf16[9,128,256]{2,1,0:T(8,128)(2,1)S(1)}, bf16[9,128,256]{2,1,0:T(8,128)(2,1)}, u32[]{:S(2)}, u32[]{:S(2)}) collective-permute-start(bf16[9,128,256]{2,1,0:T(8,128)(2,1)S(1)} %slice.76), channel_id=1, source_target_pairs={{24,0},{32,56},{56,32},{64,88},{88,64},{96,120},{25,1},{33,57},{57... | collective-permute-start | bytes 1769480 | tf_op jit(solution)/shard_map/ppermute | solution.py:665
  14.3 16.2 %collective-permute-start.4 = (bf16[4,272,256]{2,1,0:T(8,128)(2,1)S(1)}, bf16[4,272,256]{2,1,0:T(8,128)(2,1)S(1)}, u32[]{:S(2)}, u32[]{:S(2)}) collective-permute-start(bf16[4,272,256]{2,1,0:T(8,128)(2,1)S(1)} %pad_maximum_fusion.refs_9_), channel_id=1, source_target_pairs={{0,96},{8,104},{16,112},{24,120},{32,0},{40,8},{48,16},{56,24},{64... | collective-permute-start | bytes 1671176 | tf_op jit(solution)/shard_map/ppermute | solution.py:678
  17.0 35.7 %collective-permute-start.8 = (bf16[14,128,256]{2,1,0:T(8,128)(2,1)S(1)}, bf16[14,128,256]{2,1,0:T(8,128)(2,1)S(1)}, u32[]{:S(2)}, u32[]{:S(2)}) collective-permute-start(bf16[14,128,256]{2,1,0:T(8,128)(2,1)S(1)} %pack_plain.1.refs_5_), channel_id=1, source_target_pairs={{8,0},{16,8},{24,16},{40,32},{48,40},{56,48},{72,64},{80,72},{88,8... | collective-permute-start | bytes 2752520 | tf_op jit(solution)/shard_map/ppermute | solution.py:669
  18.3 34.4 %collective-permute-start.7 = (bf16[14,128,256]{2,1,0:T(8,128)(2,1)S(1)}, bf16[14,128,256]{2,1,0:T(8,128)(2,1)}, u32[]{:S(2)}, u32[]{:S(2)}) collective-permute-start(bf16[14,128,256]{2,1,0:T(8,128)(2,1)S(1)} %pack_plain.1.refs_5_), channel_id=1, source_target_pairs={{0,8},{8,16},{16,24},{32,40},{40,48},{48,56},{64,72},{72,80},{80,8... | collective-permute-start | bytes 2752520 | tf_op jit(solution)/shard_map/ppermute | solution.py:668
  23.3 12.8 %collective-permute-start.3 = (bf16[4,272,256]{2,1,0:T(8,128)(2,1)S(1)}, bf16[4,272,256]{2,1,0:T(8,128)(2,1)S(1)}, u32[]{:S(2)}, u32[]{:S(2)}) collective-permute-start(bf16[4,272,256]{2,1,0:T(8,128)(2,1)S(1)} %pad_maximum_fusion.refs_9_), channel_id=1, source_target_pairs={{0,32},{8,40},{16,48},{24,56},{32,64},{40,72},{48,80},{56,88},{64,... | collective-permute-start | bytes 1671176 | tf_op jit(solution)/shard_map/ppermute | solution.py:677
  26.6 26.2 %collective-permute-start.11 = (bf16[9,128,256]{2,1,0:T(8,128)(2,1)}, bf16[9,128,256]{2,1,0:T(8,128)(2,1)}, u32[]{:S(2)}, u32[]{:S(2)}) collective-permute-start(bf16[9,128,256]{2,1,0:T(8,128)(2,1)} %collective-permute-done.10), channel_id=1, source_target_pairs={{0,32},{56,24},{32,64},{88,56},{64,96},{120,88},{1,33},{57,25},{33... | collective-permute-start | bytes 1769480 | tf_op jit(solution)/shard_map/ppermute | solution.py:666
  30.6 7.6 %collective-permute-start.6 = (bf16[2,272,256]{2,1,0:T(8,128)(2,1)S(1)}, bf16[2,272,256]{2,1,0:T(8,128)(2,1)}, u32[]{:S(2)}, u32[]{:S(2)}) collective-permute-start(bf16[2,272,256]{2,1,0:T(8,128)(2,1)S(1)} %slice.73), channel_id=1, source_target_pairs={{0,96},{8,104},{16,112},{24,120},{32,0},{40,8},{48,16},{56,24},{64... | collective-permute-start | bytes 835592 | tf_op jit(solution)/shard_map/ppermute | solution.py:681
  36.0 16.7 %collective-permute-start.9 = (bf16[5,128,256]{2,1,0:T(8,128)(2,1)}, bf16[5,128,256]{2,1,0:T(8,128)(2,1)}, u32[]{:S(2)}, u32[]{:S(2)}) collective-permute-start(bf16[5,128,256]{2,1,0:T(8,128)(2,1)} %slice.75), channel_id=1, source_target_pairs={{24,32},{32,24},{56,64},{64,56},{88,96},{96,88},{25,33},{33,25},{5... | collective-permute-start | bytes 983048 | tf_op jit(solution)/shard_map/ppermute | solution.py:664
  38.2 13.5 %collective-permute-start.5 = (bf16[2,272,256]{2,1,0:T(8,128)(2,1)}, bf16[2,272,256]{2,1,0:T(8,128)(2,1)}, u32[]{:S(2)}, u32[]{:S(2)}) collective-permute-start(bf16[2,272,256]{2,1,0:T(8,128)(2,1)} %slice.71), channel_id=1, source_target_pairs={{0,32},{8,40},{16,48},{24,56},{32,64},{40,72},{48,80},{56,88},{64,... | collective-permute-start | bytes 835592 | tf_op jit(solution)/shard_map/ppermute | solution.py:680
  44.6 1.8 copy-start.1
  46.4 1.0 copy-start.3
  47.4 0.8 copy-start.5
  52.8 1.2 copy-start.4
  54.0 13.5 %copy-start.2 = (bf16[14,256,512]{2,1,0:T(8,128)(2,1)S(1)}, bf16[14,256,512]{2,1,0:T(8,128)(2,1)}, u32[]{:S(2)}) copy-start(bf16[14,256,512]{2,1,0:T(8,128)(2,1)} %copy-done.1) | copy-start | bytes 11010052
  59.3 12.2 %collective-permute-start.19 = (bf16[256,256]{1,0:T(8,128)(2,1)S(1)}, bf16[256,256]{1,0:T(8,128)(2,1)S(1)}, u32[]{:S(2)}, u32[]{:S(2)}) collective-permute-start(bf16[256,256]{1,0:T(8,128)(2,1)S(1)} %get-tuple-element.30.refs_3_), channel_id=1, source_target_pairs={{0,16},{8,24},{16,0},{24,8},{32,48},{40,56},{48,32},{56,40},{64,80... | collective-permute-start | bytes 393224 | tf_op jit(solution)/shard_map/ppermute | solution.py:674
  59.4 12.1 %collective-permute-start.18 = (bf16[256,256]{1,0:T(8,128)(2,1)S(1)}, bf16[256,256]{1,0:T(8,128)(2,1)S(1)}, u32[]{:S(2)}, u32[]{:S(2)}) collective-permute-start(bf16[256,256]{1,0:T(8,128)(2,1)S(1)} %get-tuple-element.30.refs_3_), channel_id=1, source_target_pairs={{0,24},{8,0},{16,8},{24,16},{32,56},{40,32},{48,40},{56,48},{64,88... | collective-permute-start | bytes 393224 | tf_op jit(solution)/shard_map/ppermute | solution.py:674
  67.0 5.0 %collective-permute-start.17 = (bf16[256,256]{1,0:T(8,128)(2,1)S(1)}, bf16[256,256]{1,0:T(8,128)(2,1)S(1)}, u32[]{:S(2)}, u32[]{:S(2)}) collective-permute-start(bf16[256,256]{1,0:T(8,128)(2,1)S(1)} %get-tuple-element.30.refs_3_), channel_id=1, source_target_pairs={{0,8},{8,16},{16,24},{24,0},{32,40},{40,48},{48,56},{56,32},{64,72... | collective-permute-start | bytes 393224 | tf_op jit(solution)/shard_map/ppermute | solution.py:674
  70.2 14.8 %collective-permute-start.15 = (bf16[9,128,256]{2,1,0:T(8,128)(2,1)S(1)}, bf16[9,128,256]{2,1,0:T(8,128)(2,1)S(1)}, u32[]{:S(2)}, u32[]{:S(2)}) collective-permute-start(bf16[9,128,256]{2,1,0:T(8,128)(2,1)S(1)} %slice.78), channel_id=1, source_target_pairs={{24,0},{32,56},{56,32},{64,88},{88,64},{96,120},{25,1},{33,57},{57... | collective-permute-start | bytes 1769480 | tf_op jit(solution)/shard_map/ppermute | solution.py:665
  72.1 13.6 %collective-permute-start.21 = (bf16[4,256,256]{2,1,0:T(8,128)(2,1)S(1)}, bf16[4,256,256]{2,1,0:T(8,128)(2,1)S(1)}, u32[]{:S(2)}, u32[]{:S(2)}) collective-permute-start(bf16[4,256,256]{2,1,0:T(8,128)(2,1)S(1)} %pad_maximum_fusion.1.refs_8_), channel_id=1, source_target_pairs={{0,96},{8,104},{16,112},{24,120},{32,0},{40,8},{48,16},{56,24},{64... | collective-permute-start | bytes 1572872 | tf_op jit(solution)/shard_map/ppermute | solution.py:678
  76.0 32.8 %collective-permute-start.13 = (bf16[14,128,256]{2,1,0:T(8,128)(2,1)S(1)}, bf16[14,128,256]{2,1,0:T(8,128)(2,1)S(1)}, u32[]{:S(2)}, u32[]{:S(2)}) collective-permute-start(bf16[14,128,256]{2,1,0:T(8,128)(2,1)S(1)} %plain_first.1.refs_2_.refs_4_), channel_id=1, source_target_pairs={{8,0},{16,8},{24,16},{40,32},{48,40},{56,48},{72,64},{80,72},{88,8... | collective-permute-start | bytes 2752520 | tf_op jit(solution)/shard_map/ppermute | solution.py:669
  77.3 31.5 %collective-permute-start.12 = (bf16[14,128,256]{2,1,0:T(8,128)(2,1)S(1)}, bf16[14,128,256]{2,1,0:T(8,128)(2,1)S(1)}, u32[]{:S(2)}, u32[]{:S(2)}) collective-permute-start(bf16[14,128,256]{2,1,0:T(8,128)(2,1)S(1)} %plain_first.1.refs_2_.refs_4_), channel_id=1, source_target_pairs={{0,8},{8,16},{16,24},{32,40},{40,48},{48,56},{64,72},{72,80},{80,8... | collective-permute-start | bytes 2752520 | tf_op jit(solution)/shard_map/ppermute | solution.py:668
  81.4 10.0 %collective-permute-start.20 = (bf16[4,256,256]{2,1,0:T(8,128)(2,1)S(1)}, bf16[4,256,256]{2,1,0:T(8,128)(2,1)S(1)}, u32[]{:S(2)}, u32[]{:S(2)}) collective-permute-start(bf16[4,256,256]{2,1,0:T(8,128)(2,1)S(1)} %pad_maximum_fusion.1.refs_8_), channel_id=1, source_target_pairs={{0,32},{8,40},{16,48},{24,56},{32,64},{40,72},{48,80},{56,88},{64,... | collective-permute-start | bytes 1572872 | tf_op jit(solution)/shard_map/ppermute | solution.py:677
  85.0 6.6 %collective-permute-start.14 = (bf16[5,128,256]{2,1,0:T(8,128)(2,1)S(1)}, bf16[5,128,256]{2,1,0:T(8,128)(2,1)S(1)}, u32[]{:S(2)}, u32[]{:S(2)}) collective-permute-start(bf16[5,128,256]{2,1,0:T(8,128)(2,1)S(1)} %slice.77), channel_id=1, source_target_pairs={{24,32},{32,24},{56,64},{64,56},{88,96},{96,88},{25,33},{33,25},{5... | collective-permute-start | bytes 983048 | tf_op jit(solution)/shard_map/ppermute | solution.py:664
  85.7 23.1 %collective-permute-start.16 = (bf16[9,128,256]{2,1,0:T(8,128)(2,1)S(1)}, bf16[9,128,256]{2,1,0:T(8,128)(2,1)S(1)}, u32[]{:S(2)}, u32[]{:S(2)}) collective-permute-start(bf16[9,128,256]{2,1,0:T(8,128)(2,1)S(1)} %collective-permute-done.15), channel_id=1, source_target_pairs={{0,32},{56,24},{32,64},{88,56},{64,96},{120,88},{1,33},{57,25},{33... | collective-permute-start | bytes 1769480 | tf_op jit(solution)/shard_map/ppermute | solution.py:666
  91.4 8.3 %collective-permute-start.23 = (bf16[2,256,256]{2,1,0:T(8,128)(2,1)S(1)}, bf16[2,256,256]{2,1,0:T(8,128)(2,1)S(1)}, u32[]{:S(2)}, u32[]{:S(2)}) collective-permute-start(bf16[2,256,256]{2,1,0:T(8,128)(2,1)S(1)} %slice.80), channel_id=1, source_target_pairs={{0,96},{8,104},{16,112},{24,120},{32,0},{40,8},{48,16},{56,24},{64... | collective-permute-start | bytes 786440 | tf_op jit(solution)/shard_map/ppermute | solution.py:681
  91.7 17.2 %collective-permute-start.22 = (bf16[2,256,256]{2,1,0:T(8,128)(2,1)S(1)}, bf16[2,256,256]{2,1,0:T(8,128)(2,1)S(1)}, u32[]{:S(2)}, u32[]{:S(2)}) collective-permute-start(bf16[2,256,256]{2,1,0:T(8,128)(2,1)S(1)} %slice.79), channel_id=1, source_target_pairs={{0,32},{8,40},{16,48},{24,56},{32,64},{40,72},{48,80},{56,88},{64,... | collective-permute-start | bytes 786440 | tf_op jit(solution)/shard_map/ppermute | solution.py:680
  115.6 7.3 %collective-permute-start.24 = (f32[4,72,16,128]{3,2,1,0:T(8,128)S(1)}, f32[4,72,16,128]{3,2,1,0:T(8,128)S(1)}, u32[]{:S(2)}, u32[]{:S(2)}) collective-permute-start(f32[4,72,16,128]{3,2,1,0:T(8,128)S(1)} %get-tuple-element.32), channel_id=1, source_target_pairs={{0,1},{1,0},{2,3},{3,2},{4,5},{5,4},{6,7},{7,6},{8,9},{9,8},{10,11... | collective-permute-start | bytes 7077896 | tf_op jit(solution)/shard_map/ppermute | solution.py:719
  122.8 19.0 %copy-start.6 = (f32[72,16,128]{2,1,0:T(8,128)S(1)}, f32[72,16,128]{2,1,0:T(8,128)}, u32[]{:S(2)}) copy-start(f32[72,16,128]{2,1,0:T(8,128)} %copy-done.5) | copy-start | bytes 1769476
  123.9 10.0 %collective-permute-start.25 = (s16[77,16,128]{2,1,0:T(8,128)(2,1)S(1)}, s16[77,16,128]{2,1,0:T(8,128)(2,1)S(1)}, u32[]{:S(2)}, u32[]{:S(2)}) collective-permute-start(s16[77,16,128]{2,1,0:T(8,128)(2,1)S(1)} %get-tuple-element.34), channel_id=1, source_target_pairs={{0,2},{1,3},{2,4},{3,5},{4,6},{5,7},{6,0},{7,1},{8,10},{9,11},{10,... | collective-permute-start | bytes 946184 | tf_op jit(solution)/shard_map/ppermute | solution.py:688
  125.3 16.5 %collective-permute-start.26 = (s16[77,16,128]{2,1,0:T(8,128)(2,1)S(1)}, s16[77,16,128]{2,1,0:T(8,128)(2,1)S(1)}, u32[]{:S(2)}, u32[]{:S(2)}) collective-permute-start(s16[77,16,128]{2,1,0:T(8,128)(2,1)S(1)} %get-tuple-element.35), channel_id=1, source_target_pairs={{0,4},{1,5},{2,6},{3,7},{4,0},{5,1},{6,2},{7,3},{8,12},{9,13},{10,... | collective-permute-start | bytes 946184 | tf_op jit(solution)/shard_map/ppermute | solution.py:687
  127.9 13.9 %collective-permute-start.27 = (s16[77,16,128]{2,1,0:T(8,128)(2,1)S(1)}, s16[77,16,128]{2,1,0:T(8,128)(2,1)S(1)}, u32[]{:S(2)}, u32[]{:S(2)}) collective-permute-start(s16[77,16,128]{2,1,0:T(8,128)(2,1)S(1)} %get-tuple-element.36), channel_id=1, source_target_pairs={{0,6},{1,7},{2,0},{3,1},{4,2},{5,3},{6,4},{7,5},{8,14},{9,15},{10,... | collective-permute-start | bytes 946184 | tf_op jit(solution)/shard_map/ppermute | solution.py:689
  143.3 9.1 %collective-permute-start.30 = (s16[77,16,128]{2,1,0:T(8,128)(2,1)S(1)}, s16[77,16,128]{2,1,0:T(8,128)(2,1)S(1)}, u32[]{:S(2)}, u32[]{:S(2)}) collective-permute-start(s16[77,16,128]{2,1,0:T(8,128)(2,1)S(1)} %get-tuple-element.38), channel_id=1, source_target_pairs={{0,2},{1,3},{2,4},{3,5},{4,6},{5,7},{6,0},{7,1},{8,10},{9,11},{10,... | collective-permute-start | bytes 946184 | tf_op jit(solution)/shard_map/ppermute | solution.py:689
  144.4 16.6 %collective-permute-start.29 = (s16[77,16,128]{2,1,0:T(8,128)(2,1)S(1)}, s16[77,16,128]{2,1,0:T(8,128)(2,1)S(1)}, u32[]{:S(2)}, u32[]{:S(2)}) collective-permute-start(s16[77,16,128]{2,1,0:T(8,128)(2,1)S(1)} %get-tuple-element.38), channel_id=1, source_target_pairs={{0,4},{1,5},{2,6},{3,7},{4,0},{5,1},{6,2},{7,3},{8,12},{9,13},{10,... | collective-permute-start | bytes 946184 | tf_op jit(solution)/shard_map/ppermute | solution.py:687
  147.2 13.8 %collective-permute-start.28 = (s16[77,16,128]{2,1,0:T(8,128)(2,1)S(1)}, s16[77,16,128]{2,1,0:T(8,128)(2,1)S(1)}, u32[]{:S(2)}, u32[]{:S(2)}) collective-permute-start(s16[77,16,128]{2,1,0:T(8,128)(2,1)S(1)} %get-tuple-element.38), channel_id=1, source_target_pairs={{0,6},{1,7},{2,0},{3,1},{4,2},{5,3},{6,4},{7,5},{8,14},{9,15},{10,... | collective-permute-start | bytes 946184 | tf_op jit(solution)/shard_map/ppermute | solution.py:688
  161.2 4.0 %collective-permute-start.31 = (s16[4,77,16,128]{3,2,1,0:T(8,128)(2,1)S(1)}, s16[4,77,16,128]{3,2,1,0:T(8,128)(2,1)S(1)}, u32[]{:S(2)}, u32[]{:S(2)}) collective-permute-start(s16[4,77,16,128]{3,2,1,0:T(8,128)(2,1)S(1)} %pad_add_fusion.refs_2_), channel_id=1, source_target_pairs={{0,1},{1,0},{2,3},{3,2},{4,5},{5,4},{6,7},{7,6},{8,9},{9,8},{10,11... | collective-permute-start | bytes 3784712 | tf_op jit(solution)/shard_map/ppermute | solution.py:709
  166.8 7.4 %collective-permute-start.39 = (bf16[256,256]{1,0:T(8,128)(2,1)S(1)}, bf16[256,256]{1,0:T(8,128)(2,1)S(1)}, u32[]{:S(2)}, u32[]{:S(2)}) collective-permute-start(bf16[256,256]{1,0:T(8,128)(2,1)S(1)} %hub_later.1.refs_5_.refs_3_), channel_id=1, source_target_pairs={{0,16},{8,24},{16,0},{24,8},{32,48},{40,56},{48,32},{56,40},{64,80... | collective-permute-start | bytes 393224 | tf_op jit(solution)/shard_map/ppermute | solution.py:674
  166.9 8.6 %collective-permute-start.38 = (bf16[256,256]{1,0:T(8,128)(2,1)S(1)}, bf16[256,256]{1,0:T(8,128)(2,1)S(1)}, u32[]{:S(2)}, u32[]{:S(2)}) collective-permute-start(bf16[256,256]{1,0:T(8,128)(2,1)S(1)} %hub_later.1.refs_5_.refs_3_), channel_id=1, source_target_pairs={{0,24},{8,0},{16,8},{24,16},{32,56},{40,32},{48,40},{56,48},{64,88... | collective-permute-start | bytes 393224 | tf_op jit(solution)/shard_map/ppermute | solution.py:674
  168.9 7.4 %collective-permute-start.37 = (bf16[256,256]{1,0:T(8,128)(2,1)S(1)}, bf16[256,256]{1,0:T(8,128)(2,1)S(1)}, u32[]{:S(2)}, u32[]{:S(2)}) collective-permute-start(bf16[256,256]{1,0:T(8,128)(2,1)S(1)} %hub_later.1.refs_5_.refs_3_), channel_id=1, source_target_pairs={{0,8},{8,16},{16,24},{24,0},{32,40},{40,48},{48,56},{56,32},{64,72... | collective-permute-start | bytes 393224 | tf_op jit(solution)/shard_map/ppermute | solution.py:674
  172.9 17.1 %collective-permute-start.35 = (bf16[9,128,256]{2,1,0:T(8,128)(2,1)S(1)}, bf16[9,128,256]{2,1,0:T(8,128)(2,1)S(1)}, u32[]{:S(2)}, u32[]{:S(2)}) collective-permute-start(bf16[9,128,256]{2,1,0:T(8,128)(2,1)S(1)} %slice.82), channel_id=1, source_target_pairs={{24,0},{32,56},{56,32},{64,88},{88,64},{96,120},{25,1},{33,57},{57... | collective-permute-start | bytes 1769480 | tf_op jit(solution)/shard_map/ppermute | solution.py:665
  176.3 14.4 %collective-permute-start.41 = (bf16[4,256,256]{2,1,0:T(8,128)(2,1)S(1)}, bf16[4,256,256]{2,1,0:T(8,128)(2,1)S(1)}, u32[]{:S(2)}, u32[]{:S(2)}) collective-permute-start(bf16[4,256,256]{2,1,0:T(8,128)(2,1)S(1)} %pad_maximum_fusion.2.refs_8_), channel_id=1, source_target_pairs={{0,96},{8,104},{16,112},{24,120},{32,0},{40,8},{48,16},{56,24},{64... | collective-permute-start | bytes 1572872 | tf_op jit(solution)/shard_map/ppermute | solution.py:678
  179.2 26.6 %collective-permute-start.33 = (bf16[14,128,256]{2,1,0:T(8,128)(2,1)S(1)}, bf16[14,128,256]{2,1,0:T(8,128)(2,1)S(1)}, u32[]{:S(2)}, u32[]{:S(2)}) collective-permute-start(bf16[14,128,256]{2,1,0:T(8,128)(2,1)S(1)} %plain_later.1.refs_2_.refs_4_), channel_id=1, source_target_pairs={{8,0},{16,8},{24,16},{40,32},{48,40},{56,48},{72,64},{80,72},{88,8... | collective-permute-start | bytes 2752520 | tf_op jit(solution)/shard_map/ppermute | solution.py:669
  180.5 25.4 %collective-permute-start.32 = (bf16[14,128,256]{2,1,0:T(8,128)(2,1)S(1)}, bf16[14,128,256]{2,1,0:T(8,128)(2,1)S(1)}, u32[]{:S(2)}, u32[]{:S(2)}) collective-permute-start(bf16[14,128,256]{2,1,0:T(8,128)(2,1)S(1)} %plain_later.1.refs_2_.refs_4_), channel_id=1, source_target_pairs={{0,8},{8,16},{16,24},{32,40},{40,48},{48,56},{64,72},{72,80},{80,8... | collective-permute-start | bytes 2752520 | tf_op jit(solution)/shard_map/ppermute | solution.py:668
  184.6 13.4 %collective-permute-start.40 = (bf16[4,256,256]{2,1,0:T(8,128)(2,1)S(1)}, bf16[4,256,256]{2,1,0:T(8,128)(2,1)S(1)}, u32[]{:S(2)}, u32[]{:S(2)}) collective-permute-start(bf16[4,256,256]{2,1,0:T(8,128)(2,1)S(1)} %pad_maximum_fusion.2.refs_8_), channel_id=1, source_target_pairs={{0,32},{8,40},{16,48},{24,56},{32,64},{40,72},{48,80},{56,88},{64,... | collective-permute-start | bytes 1572872 | tf_op jit(solution)/shard_map/ppermute | solution.py:677
  190.0 8.3 %collective-permute-start.34 = (bf16[5,128,256]{2,1,0:T(8,128)(2,1)S(1)}, bf16[5,128,256]{2,1,0:T(8,128)(2,1)S(1)}, u32[]{:S(2)}, u32[]{:S(2)}) collective-permute-start(bf16[5,128,256]{2,1,0:T(8,128)(2,1)S(1)} %slice.81), channel_id=1, source_target_pairs={{24,32},{32,24},{56,64},{64,56},{88,96},{96,88},{25,33},{33,25},{5... | collective-permute-start | bytes 983048 | tf_op jit(solution)/shard_map/ppermute | solution.py:664
  190.8 22.5 %collective-permute-start.36 = (bf16[9,128,256]{2,1,0:T(8,128)(2,1)S(1)}, bf16[9,128,256]{2,1,0:T(8,128)(2,1)S(1)}, u32[]{:S(2)}, u32[]{:S(2)}) collective-permute-start(bf16[9,128,256]{2,1,0:T(8,128)(2,1)S(1)} %collective-permute-done.35), channel_id=1, source_target_pairs={{0,32},{56,24},{32,64},{88,56},{64,96},{120,88},{1,33},{57,25},{33... | collective-permute-start | bytes 1769480 | tf_op jit(solution)/shard_map/ppermute | solution.py:666
  198.0 7.9 %collective-permute-start.43 = (bf16[2,256,256]{2,1,0:T(8,128)(2,1)S(1)}, bf16[2,256,256]{2,1,0:T(8,128)(2,1)S(1)}, u32[]{:S(2)}, u32[]{:S(2)}) collective-permute-start(bf16[2,256,256]{2,1,0:T(8,128)(2,1)S(1)} %slice.84), channel_id=1, source_target_pairs={{0,96},{8,104},{16,112},{24,120},{32,0},{40,8},{48,16},{56,24},{64... | collective-permute-start | bytes 786440 | tf_op jit(solution)/shard_map/ppermute | solution.py:681
  198.3 15.0 %collective-permute-start.42 = (bf16[2,256,256]{2,1,0:T(8,128)(2,1)S(1)}, bf16[2,256,256]{2,1,0:T(8,128)(2,1)S(1)}, u32[]{:S(2)}, u32[]{:S(2)}) collective-permute-start(bf16[2,256,256]{2,1,0:T(8,128)(2,1)S(1)} %slice.83), channel_id=1, source_target_pairs={{0,32},{8,40},{16,48},{24,56},{32,64},{40,72},{48,80},{56,88},{64,... | collective-permute-start | bytes 786440 | tf_op jit(solution)/shard_map/ppermute | solution.py:680
  220.0 6.0 %collective-permute-start.44 = (f32[4,72,16,128]{3,2,1,0:T(8,128)S(1)}, f32[4,72,16,128]{3,2,1,0:T(8,128)S(1)}, u32[]{:S(2)}, u32[]{:S(2)}) collective-permute-start(f32[4,72,16,128]{3,2,1,0:T(8,128)S(1)} %get-tuple-element.40), channel_id=1, source_target_pairs={{0,1},{1,0},{2,3},{3,2},{4,5},{5,4},{6,7},{7,6},{8,9},{9,8},{10,11... | collective-permute-start | bytes 7077896 | tf_op jit(solution)/shard_map/ppermute | solution.py:719
  227.1 9.9 %collective-permute-start.45 = (s16[77,16,128]{2,1,0:T(8,128)(2,1)S(1)}, s16[77,16,128]{2,1,0:T(8,128)(2,1)S(1)}, u32[]{:S(2)}, u32[]{:S(2)}) collective-permute-start(s16[77,16,128]{2,1,0:T(8,128)(2,1)S(1)} %get-tuple-element.42), channel_id=1, source_target_pairs={{0,2},{1,3},{2,4},{3,5},{4,6},{5,7},{6,0},{7,1},{8,10},{9,11},{10,... | collective-permute-start | bytes 946184 | tf_op jit(solution)/shard_map/ppermute | solution.py:688
  228.0 16.1 %collective-permute-start.46 = (s16[77,16,128]{2,1,0:T(8,128)(2,1)S(1)}, s16[77,16,128]{2,1,0:T(8,128)(2,1)S(1)}, u32[]{:S(2)}, u32[]{:S(2)}) collective-permute-start(s16[77,16,128]{2,1,0:T(8,128)(2,1)S(1)} %get-tuple-element.43), channel_id=1, source_target_pairs={{0,4},{1,5},{2,6},{3,7},{4,0},{5,1},{6,2},{7,3},{8,12},{9,13},{10,... | collective-permute-start | bytes 946184 | tf_op jit(solution)/shard_map/ppermute | solution.py:687
  230.2 13.9 %collective-permute-start.47 = (s16[77,16,128]{2,1,0:T(8,128)(2,1)S(1)}, s16[77,16,128]{2,1,0:T(8,128)(2,1)S(1)}, u32[]{:S(2)}, u32[]{:S(2)}) collective-permute-start(s16[77,16,128]{2,1,0:T(8,128)(2,1)S(1)} %get-tuple-element.44), channel_id=1, source_target_pairs={{0,6},{1,7},{2,0},{3,1},{4,2},{5,3},{6,4},{7,5},{8,14},{9,15},{10,... | collective-permute-start | bytes 946184 | tf_op jit(solution)/shard_map/ppermute | solution.py:689
